TPU v7x, 32 devices: a whole 2x2x4 slice. The times are simulated.
32 devices in a mesh: dp: 8 (over y, x, core), head: 4 (over z).
Axes of the slice: x: 2, y: 2, z: 4, core: 2. Of those that a mesh axis runs over, the one named last changes fastest.
Arguments:
- activations: bfloat16 [4, 6144, 1024], P(None, ('dp', 'head')), may hold values from -6 to 6
- conditioning: bfloat16 [4, 1536, 1024], P(None, ('dp', 'head')), may hold values from -3 to 3
- cotangent: bfloat16 [4, 6144, 1024], P(None, ('dp', 'head')), may hold values from -6 to 6
- block_targets: int32 [4, 48], replicated, may hold values from -1 to 46, as said below
- up_gain: float32 [4, 1024], replicated, may hold values from -6 to 6
- norm1_gain: float32 [1024], replicated, may hold values from 0.1 to 1.9
- norm1_shift: float32 [1024], replicated, may hold values from -1.75 to 1.75
- w_qkv: bfloat16 [3, 1024, 1024], P(None, None, 'head'), may hold values from -0.1875 to 0.1875
- b_qv: float32 [2, 1024], P(None, 'head'), may hold values from -3 to 3
- w_out: bfloat16 [1024, 1024], P('head'), may hold values from -1.5 to 1.5
- b_out: float32 [1024], replicated, may hold values from -3 to 3
- norm2_gain: float32 [1024], replicated, may hold values from 0.1 to 1.9
- norm2_shift: float32 [1024], replicated, may hold values from -1.75 to 1.75
- w_fc1: bfloat16 [1024, 4096], P(None, 'head'), may hold values from -0.1875 to 0.1875
- b_fc1: float32 [4096], P('head'), may hold values from -3 to 3
- w_fc2: bfloat16 [4096, 1024], P('head'), may hold values from -0.09375 to 0.09375
- b_fc2: float32 [1024], replicated, may hold values from -3 to 3
Outputs:
- layer_out: bfloat16 [4, 6144, 1024], P(None, ('dp', 'head'))
- grad_input: float32 [4, 6144, 1024], P(None, ('dp', 'head'))
- grad_conditioning: float32 [4, 1536, 1024], P(None, ('dp', 'head'))
- grad_up_gain: float32 [4, 1024], replicated
- grad_norm1_gain: float32 [1024], replicated
- grad_norm1_shift: float32 [1024], replicated
- grad_w_qkv: float32 [3, 1024, 1024], P(None, 'dp', 'head')
- grad_b_qv: float32 [2, 1024], replicated
- grad_w_out: float32 [1024, 1024], P('head', 'dp')
- grad_b_out: float32 [1024], replicated
- grad_norm2_gain: float32 [1024], replicated
- grad_norm2_shift: float32 [1024], replicated
- grad_w_fc1: float32 [1024, 4096], P('dp', 'head')
- grad_b_fc1: float32 [4096], replicated
- grad_w_fc2: float32 [4096, 1024], P('head', 'dp')
- grad_b_fc2: float32 [1024], replicated
Inputs may be any that keep to these rules, and one draw needn't show every extreme that they name: `block_targets`: entry b of a micro-batch is -1 or a block below b in the same window; windows are runs of whole blocks and the first block of each has -1. In micro-batches of even index one window covers all 48 blocks and its last block names block 0; in the others no window is longer than 2048 tokens and the last block names the block before it.
All inputs are finite; a program needn't handle non-finite values.
Results may differ from a plain program's by a relative error of at most 0.015.
Values may be sent and summed in bfloat16 or wider, within the bound.
No kernel may reach another device: no remote copies, remote signals or barrier semaphores. Data moves between devices by JAX's collectives and lax.ppermute only.
A program may use at most 192 MiB of HBM per device.

v0:
```python
import math

import jax
import jax.numpy as jnp
from jax import lax
from jax.sharding import PartitionSpec as P

HEAD_DIM = 64
BLOCK = 128
UP = 4


epsilon = 1e-05
highest = lax.Precision.HIGHEST


def norm_forward(values, gain, shift):
    centered = values - jnp.mean(values, axis=-1, keepdims=True)
    inverse = lax.rsqrt(jnp.mean(centered * centered, axis=-1, keepdims=True) + epsilon)
    standard = centered * inverse
    return (standard * gain + shift, standard, inverse)


def norm_backward(upstream, standard, inverse, gain):
    scaled = upstream * gain
    inner = (
        scaled
        - jnp.mean(scaled, axis=-1, keepdims=True)
        - standard * jnp.mean(scaled * standard, axis=-1, keepdims=True)
    )
    return (inner * inverse, jnp.sum(upstream * standard, axis=0), jnp.sum(upstream, axis=0))


def gelu_tanh(values):
    return jax.nn.gelu(values, approximate=True)


def masked_scores(q_blocks, key_cat, allowed, score_scale):
    scores = (
        jnp.einsum("bqhd,bkhd->bhqk", q_blocks, key_cat, preferred_element_type=jnp.float32)
        * score_scale
    )
    return jnp.where(allowed, scores, -1e30)


def local(
    activations,
    conditioning,
    cotangent,
    block_targets,
    up_gain,
    norm1_gain,
    norm1_shift,
    w_qkv,
    b_qv,
    w_out,
    b_out,
    norm2_gain,
    norm2_shift,
    w_fc1,
    b_fc1,
    w_fc2,
    b_fc2,
):
    local_rows = activations.shape[1]
    model_width = activations.shape[2]
    head_cols = w_qkv.shape[2]
    hidden_cols = w_fc1.shape[1]
    heads_here = head_cols // HEAD_DIM
    gathered_rows = local_rows * lax.axis_size("head")
    query_blocks = gathered_rows // BLOCK
    dp_index = lax.axis_index("dp")
    head_index = lax.axis_index("head")
    score_scale = 1.0 / math.sqrt(HEAD_DIM)
    causal = jnp.arange(BLOCK)[:, None] >= jnp.arange(BLOCK)[None, :]
    shape_four = (query_blocks, BLOCK, heads_here, HEAD_DIM)

    def one_batch(totals, inputs_now):
        tokens, coarse, incoming, table_row = inputs_now
        coarse_f = coarse.astype(jnp.float32)
        joined = (
            tokens.astype(jnp.float32).reshape(-1, UP, model_width)
            + coarse_f[:, None, :] * up_gain[None]
        ).reshape(local_rows, model_width)
        normed_f, standard_one, inverse_one = norm_forward(joined, norm1_gain, norm1_shift)
        normed = normed_f.astype(jnp.bfloat16)
        normed_all = lax.all_gather(normed, "head", axis=0, tiled=True)
        project = jnp.einsum("gd,tdc->tgc", normed_all, w_qkv, preferred_element_type=jnp.float32)
        queries = (project[0] + b_qv[0]).astype(jnp.bfloat16)
        keys_here = project[1].astype(jnp.bfloat16)
        values_here = (project[2] + b_qv[1]).astype(jnp.bfloat16)
        key_value = jnp.concatenate([keys_here, values_here], axis=1)
        targets = lax.dynamic_slice_in_dim(table_row, dp_index * query_blocks, query_blocks)
        has_far = targets >= 0
        piece = lax.all_gather(key_value, "dp", axis=0, tiled=True)
        piece_blocks = piece.shape[0] // BLOCK
        shaped = piece.reshape(piece_blocks, BLOCK, piece.shape[1])
        inside = (targets >= 0) & (targets < piece_blocks)
        chosen = shaped[jnp.clip(targets, 0, piece_blocks - 1)]
        far_blocks = jnp.where(inside[:, None, None], chosen, jnp.zeros_like(chosen))
        q_blocks = queries.reshape(shape_four)
        key_cat = jnp.concatenate(
            [keys_here.reshape(shape_four), far_blocks[:, :, :head_cols].reshape(shape_four)],
            axis=1,
        )
        value_cat = jnp.concatenate(
            [values_here.reshape(shape_four), far_blocks[:, :, head_cols:].reshape(shape_four)],
            axis=1,
        )
        own_mask = jnp.broadcast_to(causal, (query_blocks, 1, BLOCK, BLOCK))
        far_mask = jnp.broadcast_to(has_far[:, None, None, None], own_mask.shape)
        allowed = jnp.concatenate([own_mask, far_mask], axis=-1)
        scores = masked_scores(q_blocks, key_cat, allowed, score_scale)
        row_top = jnp.max(scores, axis=-1, keepdims=True)
        log_total = row_top + jnp.log(jnp.sum(jnp.exp(scores - row_top), axis=-1, keepdims=True))
        probs_low = jnp.exp(scores - log_total).astype(jnp.bfloat16)
        attended = (
            jnp.einsum("bhqk,bkhd->bqhd", probs_low, value_cat, preferred_element_type=jnp.float32)
            .reshape(gathered_rows, head_cols)
            .astype(jnp.bfloat16)
        )
        residual = (
            joined
            + lax.psum_scatter(
                jnp.dot(attended, w_out, preferred_element_type=jnp.float32),
                "head",
                scatter_dimension=0,
                tiled=True,
            )
            + b_out
        )
        normed2_f, standard_two, inverse_two = norm_forward(residual, norm2_gain, norm2_shift)
        normed_two = normed2_f.astype(jnp.bfloat16)
        normed_two_all = lax.all_gather(normed_two, "head", axis=0, tiled=True)
        hidden = jnp.dot(normed_two_all, w_fc1, preferred_element_type=jnp.float32) + b_fc1
        activated = gelu_tanh(hidden).astype(jnp.bfloat16)
        layer_out = (
            residual
            + lax.psum_scatter(
                jnp.dot(activated, w_fc2, preferred_element_type=jnp.float32).astype(jnp.bfloat16),
                "head",
                scatter_dimension=0,
                tiled=True,
            ).astype(jnp.float32)
            + b_fc2
        )
        incoming_f = incoming.astype(jnp.float32)
        grad_b2 = jnp.sum(incoming_f, axis=0)
        incoming_all = lax.all_gather(incoming, "head", axis=0, tiled=True)
        grad_w2 = jnp.einsum(
            "gf,gd->fd", activated, incoming_all, preferred_element_type=jnp.float32
        )
        grad_act = jnp.einsum("gd,fd->gf", incoming_all, w_fc2, preferred_element_type=jnp.float32)
        grad_hidden = jax.vjp(gelu_tanh, hidden)[1](grad_act)[0].astype(jnp.bfloat16)
        grad_b1 = jnp.sum(grad_hidden.astype(jnp.float32), axis=0)
        grad_w1 = jnp.einsum(
            "gd,gf->df", normed_two_all, grad_hidden, preferred_element_type=jnp.float32
        )
        grad_normed_two = lax.psum_scatter(
            jnp.einsum("gf,df->gd", grad_hidden, w_fc1, preferred_element_type=jnp.float32).astype(
                jnp.bfloat16
            ),
            "head",
            scatter_dimension=0,
            tiled=True,
        ).astype(jnp.float32)
        grad_res_part, grad_g2, grad_s2 = norm_backward(
            grad_normed_two, standard_two, inverse_two, norm2_gain
        )
        grad_residual = incoming_f + grad_res_part
        grad_branch = grad_residual.astype(jnp.bfloat16)
        grad_bo = jnp.sum(grad_branch.astype(jnp.float32), axis=0)
        grad_branch_all = lax.all_gather(grad_branch, "head", axis=0, tiled=True)
        grad_wo = jnp.einsum(
            "gc,gd->cd", attended, grad_branch_all, preferred_element_type=jnp.float32
        )
        grad_att = (
            jnp.einsum("gd,cd->gc", grad_branch_all, w_out, preferred_element_type=jnp.float32)
            .astype(jnp.bfloat16)
            .reshape(shape_four)
        )
        probs = jnp.exp(masked_scores(q_blocks, key_cat, allowed, score_scale) - log_total)
        probs_again = probs.astype(jnp.bfloat16)
        grad_probs = jnp.einsum(
            "bqhd,bkhd->bhqk", grad_att, value_cat, preferred_element_type=jnp.float32
        )
        grad_scores = (
            probs * (grad_probs - jnp.sum(probs * grad_probs, axis=-1, keepdims=True))
        ).astype(jnp.bfloat16)
        grad_q = (
            jnp.einsum("bhqk,bkhd->bqhd", grad_scores, key_cat, preferred_element_type=jnp.float32)
            * score_scale
        )
        grad_kc = (
            jnp.einsum("bhqk,bqhd->bkhd", grad_scores, q_blocks, preferred_element_type=jnp.float32)
            * score_scale
        )
        grad_vc = jnp.einsum(
            "bhqk,bqhd->bkhd", probs_again, grad_att, preferred_element_type=jnp.float32
        )
        grad_far = jnp.concatenate(
            [
                grad_kc[:, BLOCK:].reshape(query_blocks, BLOCK, head_cols),
                grad_vc[:, BLOCK:].reshape(query_blocks, BLOCK, head_cols),
            ],
            axis=-1,
        )
        piece = lax.all_gather(grad_far.astype(jnp.bfloat16), "dp", axis=0, tiled=True).astype(
            jnp.float32
        )
        block_ids = dp_index * query_blocks + jnp.arange(query_blocks)
        routing = ((table_row[None, :] == block_ids[:, None]) & (table_row[None, :] >= 0)).astype(
            jnp.float32
        )
        far_sum = jnp.zeros((gathered_rows, 2 * head_cols), jnp.float32) + jnp.einsum(
            "cq,qrk->crk", routing, piece, precision=highest
        ).reshape(gathered_rows, 2 * head_cols)
        grad_keys = (
            grad_kc[:, :BLOCK].reshape(gathered_rows, head_cols) + far_sum[:, :head_cols]
        ).astype(jnp.bfloat16)
        grad_values = (
            grad_vc[:, :BLOCK].reshape(gathered_rows, head_cols) + far_sum[:, head_cols:]
        ).astype(jnp.bfloat16)
        grad_queries = grad_q.reshape(gathered_rows, head_cols).astype(jnp.bfloat16)
        grad_stack = jnp.stack([grad_queries, grad_keys, grad_values])
        grad_wqkv = jnp.einsum(
            "gd,tgc->tdc", normed_all, grad_stack, preferred_element_type=jnp.float32
        )
        grad_bqv = jnp.stack(
            [
                jnp.sum(grad_queries.astype(jnp.float32), axis=0),
                jnp.sum(grad_values.astype(jnp.float32), axis=0),
            ]
        )
        grad_normed = lax.psum_scatter(
            jnp.einsum("tgc,tdc->gd", grad_stack, w_qkv, preferred_element_type=jnp.float32).astype(
                jnp.bfloat16
            ),
            "head",
            scatter_dimension=0,
            tiled=True,
        ).astype(jnp.float32)
        grad_join_part, grad_g1, grad_s1 = norm_backward(
            grad_normed, standard_one, inverse_one, norm1_gain
        )
        grad_joined = grad_residual + grad_join_part
        grouped_grad = grad_joined.reshape(-1, UP, model_width)
        grad_coarse = jnp.sum(grouped_grad * up_gain[None], axis=1)
        grad_up = jnp.sum(grouped_grad * coarse_f[:, None, :], axis=0)
        updates = (
            grad_up,
            grad_g1,
            grad_s1,
            grad_wqkv,
            grad_bqv,
            grad_wo,
            grad_bo,
            grad_g2,
            grad_s2,
            grad_w1,
            grad_b1,
            grad_w2,
            grad_b2,
        )
        totals = tuple((acc_item + new_item for acc_item, new_item in zip(totals, updates)))
        return (totals, (layer_out.astype(jnp.bfloat16), grad_joined, grad_coarse))

    start_totals = (
        jnp.zeros((UP, model_width), jnp.float32),
        jnp.zeros((model_width,), jnp.float32),
        jnp.zeros((model_width,), jnp.float32),
        jnp.zeros((3, model_width, head_cols), jnp.float32),
        jnp.zeros((2, head_cols), jnp.float32),
        jnp.zeros((head_cols, model_width), jnp.float32),
        jnp.zeros((model_width,), jnp.float32),
        jnp.zeros((model_width,), jnp.float32),
        jnp.zeros((model_width,), jnp.float32),
        jnp.zeros((model_width, hidden_cols), jnp.float32),
        jnp.zeros((hidden_cols,), jnp.float32),
        jnp.zeros((hidden_cols, model_width), jnp.float32),
        jnp.zeros((model_width,), jnp.float32),
    )
    totals, stacked = lax.scan(
        one_batch, start_totals, (activations, conditioning, cotangent, block_targets)
    )
    large_sums = (
        lax.psum_scatter(
            totals[3].astype(jnp.bfloat16), "dp", scatter_dimension=1, tiled=True
        ).astype(jnp.float32),
        lax.psum_scatter(
            totals[5].astype(jnp.bfloat16), "dp", scatter_dimension=1, tiled=True
        ).astype(jnp.float32),
        lax.psum_scatter(
            totals[9].astype(jnp.bfloat16), "dp", scatter_dimension=0, tiled=True
        ).astype(jnp.float32),
        lax.psum_scatter(
            totals[11].astype(jnp.bfloat16), "dp", scatter_dimension=1, tiled=True
        ).astype(jnp.float32),
    )
    bqv_full = lax.dynamic_update_slice(
        jnp.zeros((2, model_width), jnp.float32), totals[4], (jnp.int32(0), head_index * head_cols)
    )
    fc_bias_full = lax.dynamic_update_slice(
        jnp.zeros((hidden_cols * lax.axis_size("head"),), jnp.float32),
        totals[10],
        (head_index * hidden_cols,),
    )
    small_sums = lax.psum(
        (
            totals[0],
            totals[1],
            totals[2],
            bqv_full,
            totals[6],
            totals[7],
            totals[8],
            fc_bias_full,
            totals[12],
        ),
        ("dp", "head"),
    )
    return (
        stacked[0],
        stacked[1],
        stacked[2],
        small_sums[0],
        small_sums[1],
        small_sums[2],
        large_sums[0],
        small_sums[3],
        large_sums[1],
        small_sums[4],
        small_sums[5],
        small_sums[6],
        large_sums[2],
        small_sums[7],
        large_sums[3],
        small_sums[8],
    )


def solution(mesh):
    return jax.shard_map(
        local,
        mesh=mesh,
        in_specs=(
            P(None, ("dp", "head"), None),
            P(None, ("dp", "head"), None),
            P(None, ("dp", "head"), None),
            P(),
            P(),
            P(),
            P(),
            P(None, None, "head"),
            P(None, "head"),
            P("head", None),
            P(),
            P(),
            P(),
            P(None, "head"),
            P("head"),
            P("head", None),
            P(),
        ),
        out_specs=(
            P(None, ("dp", "head"), None),
            P(None, ("dp", "head"), None),
            P(None, ("dp", "head"), None),
            P(),
            P(),
            P(),
            P(None, "dp", "head"),
            P(),
            P("head", "dp"),
            P(),
            P(),
            P(),
            P("dp", "head"),
            P(),
            P("head", "dp"),
            P(),
        ),
        check_vma=False,
    )
```

profile of v0, /device:TPU:0, one launch (start us, length us, event | category | flops | bytes accessed | tf_op | source)
XLA Modules:
  0.0 2144.5 jit_solution(5609583396227685708)
XLA Ops:
  8.2 1946.9 %while.44 = (s32[]{:T(128)}, f32[4,1024]{1,0:T(4,128)}, f32[1024]{0:T(1024)}, f32[1024]{0:T(1024)}, f32[3,1024,256]{1,2,0:T(8,128)}, /*index=5*/f32[2,256]{1,0:T...) while((s32[]{:T(128)}, f32[4,1024]{1,0:T(4,128)}, ...), condition=%wide.region_27.28_spmd.clone, body=%wide.region_0.27_spmd.clone.sunk | while | flops 15231246336 | bytes 442530400 | solution.py:283
  13.8 39.9 %all-gather.11.cloned.1.call-done = bf16[768,1024]{1,0:T(8,128)(2,1)} async-done(((bf16[192,1024]{1,0:T(8,128)(2,1)}), bf16[768,1024]{1,0:T(8,128)(2,1)}) %all-gather.11.cloned.1.call-update) | async-done | bytes 1572880 | tf_op jit(solution)/shard_map/while/body/eval_jaxpr/all_gather | solution.py:87
  67.1 35.4 %all-gather.13.cloned.1.call-done = bf16[6144,512]{0,1:T(8,128)(2,1)} async-done(((bf16[768,512]{0,1:T(8,128)(2,1)}), bf16[6144,512]{0,1:T(8,128)(2,1)}) %all-gather.13.cloned.1.call-update) | async-done | bytes 6291472 | tf_op jit(solution)/shard_map/while/body/eval_jaxpr/all_gather | solution.py:95
  124.6 60.4 %reduce-scatter.21.cloned.1.call-done = f32[192,1024]{1,0:T(8,128)} async-done(((f32[768,1024]{1,0:T(8,128)}), f32[192,1024]{1,0:T(8,128)}) %reduce-scatter.21.cloned.1.call-update) | async-done | bytes 786448 | tf_op jit(solution)/shard_map/while/body/eval_jaxpr/reduce_scatter | solution.py:124
  274.8 34.2 %reduce-scatter.23.cloned.1.call-done = bf16[192,1024]{1,0:T(8,128)(2,1)} async-done(((bf16[768,1024]{1,0:T(8,128)(2,1)}), bf16[192,1024]{1,0:T(8,128)(2,1)}) %reduce-scatter.23.cloned.1.call-update) | async-done | bytes 393232 | tf_op jit(solution)/shard_map/while/body/eval_jaxpr/reduce_scatter | solution.py:159
  314.7 36.2 %all-gather.19.cloned.1.call-done = bf16[768,1024]{1,0:T(8,128)(2,1)} async-done(((bf16[192,1024]{1,0:T(8,128)(2,1)}), bf16[768,1024]{1,0:T(8,128)(2,1)}) %all-gather.19.cloned.1.call-update) | async-done | bytes 1572880 | tf_op jit(solution)/shard_map/while/body/eval_jaxpr/all_gather | solution.py:173
  502.6 36.1 %all-gather.11.cloned.1.call-done = bf16[768,1024]{1,0:T(8,128)(2,1)} async-done(((bf16[192,1024]{1,0:T(8,128)(2,1)}), bf16[768,1024]{1,0:T(8,128)(2,1)}) %all-gather.11.cloned.1.call-update) | async-done | bytes 1572880 | tf_op jit(solution)/shard_map/while/body/eval_jaxpr/all_gather | solution.py:87
  552.2 35.4 %all-gather.13.cloned.1.call-done = bf16[6144,512]{0,1:T(8,128)(2,1)} async-done(((bf16[768,512]{0,1:T(8,128)(2,1)}), bf16[6144,512]{0,1:T(8,128)(2,1)}) %all-gather.13.cloned.1.call-update) | async-done | bytes 6291472 | tf_op jit(solution)/shard_map/while/body/eval_jaxpr/all_gather | solution.py:95
  609.7 60.4 %reduce-scatter.21.cloned.1.call-done = f32[192,1024]{1,0:T(8,128)} async-done(((f32[768,1024]{1,0:T(8,128)}), f32[192,1024]{1,0:T(8,128)}) %reduce-scatter.21.cloned.1.call-update) | async-done | bytes 786448 | tf_op jit(solution)/shard_map/while/body/eval_jaxpr/reduce_scatter | solution.py:124
  759.9 34.2 %reduce-scatter.23.cloned.1.call-done = bf16[192,1024]{1,0:T(8,128)(2,1)} async-done(((bf16[768,1024]{1,0:T(8,128)(2,1)}), bf16[192,1024]{1,0:T(8,128)(2,1)}) %reduce-scatter.23.cloned.1.call-update) | async-done | bytes 393232 | tf_op jit(solution)/shard_map/while/body/eval_jaxpr/reduce_scatter | solution.py:159
  799.8 36.2 %all-gather.19.cloned.1.call-done = bf16[768,1024]{1,0:T(8,128)(2,1)} async-done(((bf16[192,1024]{1,0:T(8,128)(2,1)}), bf16[768,1024]{1,0:T(8,128)(2,1)}) %all-gather.19.cloned.1.call-update) | async-done | bytes 1572880 | tf_op jit(solution)/shard_map/while/body/eval_jaxpr/all_gather | solution.py:173
  987.5 36.1 %all-gather.11.cloned.1.call-done = bf16[768,1024]{1,0:T(8,128)(2,1)} async-done(((bf16[192,1024]{1,0:T(8,128)(2,1)}), bf16[768,1024]{1,0:T(8,128)(2,1)}) %all-gather.11.cloned.1.call-update) | async-done | bytes 1572880 | tf_op jit(solution)/shard_map/while/body/eval_jaxpr/all_gather | solution.py:87
  1037.1 35.4 %all-gather.13.cloned.1.call-done = bf16[6144,512]{0,1:T(8,128)(2,1)} async-done(((bf16[768,512]{0,1:T(8,128)(2,1)}), bf16[6144,512]{0,1:T(8,128)(2,1)}) %all-gather.13.cloned.1.call-update) | async-done | bytes 6291472 | tf_op jit(solution)/shard_map/while/body/eval_jaxpr/all_gather | solution.py:95
  1094.6 60.4 %reduce-scatter.21.cloned.1.call-done = f32[192,1024]{1,0:T(8,128)} async-done(((f32[768,1024]{1,0:T(8,128)}), f32[192,1024]{1,0:T(8,128)}) %reduce-scatter.21.cloned.1.call-update) | async-done | bytes 786448 | tf_op jit(solution)/shard_map/while/body/eval_jaxpr/reduce_scatter | solution.py:124
  1161.4 34.3 %all-gather.15.cloned.1.call-done = bf16[768,1024]{1,0:T(8,128)(2,1)} async-done(((bf16[192,1024]{1,0:T(8,128)(2,1)}), bf16[768,1024]{1,0:T(8,128)(2,1)}) %all-gather.15.cloned.1.call-update) | async-done | bytes 1572880 | tf_op jit(solution)/shard_map/while/body/eval_jaxpr/all_gather | solution.py:134
  1284.9 36.2 %all-gather.19.cloned.1.call-done = bf16[768,1024]{1,0:T(8,128)(2,1)} async-done(((bf16[192,1024]{1,0:T(8,128)(2,1)}), bf16[768,1024]{1,0:T(8,128)(2,1)}) %all-gather.19.cloned.1.call-update) | async-done | bytes 1572880 | tf_op jit(solution)/shard_map/while/body/eval_jaxpr/all_gather | solution.py:173
  1472.8 36.1 %all-gather.11.cloned.1.call-done = bf16[768,1024]{1,0:T(8,128)(2,1)} async-done(((bf16[192,1024]{1,0:T(8,128)(2,1)}), bf16[768,1024]{1,0:T(8,128)(2,1)}) %all-gather.11.cloned.1.call-update) | async-done | bytes 1572880 | tf_op jit(solution)/shard_map/while/body/eval_jaxpr/all_gather | solution.py:87
  1522.3 35.4 %all-gather.13.cloned.1.call-done = bf16[6144,512]{0,1:T(8,128)(2,1)} async-done(((bf16[768,512]{0,1:T(8,128)(2,1)}), bf16[6144,512]{0,1:T(8,128)(2,1)}) %all-gather.13.cloned.1.call-update) | async-done | bytes 6291472 | tf_op jit(solution)/shard_map/while/body/eval_jaxpr/all_gather | solution.py:95
  1579.9 60.4 %reduce-scatter.21.cloned.1.call-done = f32[192,1024]{1,0:T(8,128)} async-done(((f32[768,1024]{1,0:T(8,128)}), f32[192,1024]{1,0:T(8,128)}) %reduce-scatter.21.cloned.1.call-update) | async-done | bytes 786448 | tf_op jit(solution)/shard_map/while/body/eval_jaxpr/reduce_scatter | solution.py:124
  1730.2 34.3 %reduce-scatter.23.cloned.1.call-done = bf16[192,1024]{1,0:T(8,128)(2,1)} async-done(((bf16[768,1024]{1,0:T(8,128)(2,1)}), bf16[192,1024]{1,0:T(8,128)(2,1)}) %reduce-scatter.23.cloned.1.call-update) | async-done | bytes 393232 | tf_op jit(solution)/shard_map/while/body/eval_jaxpr/reduce_scatter | solution.py:159
  1770.1 36.1 %all-gather.19.cloned.1.call-done = bf16[768,1024]{1,0:T(8,128)(2,1)} async-done(((bf16[192,1024]{1,0:T(8,128)(2,1)}), bf16[768,1024]{1,0:T(8,128)(2,1)}) %all-gather.19.cloned.1.call-update) | async-done | bytes 1572880 | tf_op jit(solution)/shard_map/while/body/eval_jaxpr/all_gather | solution.py:173
  1994.3 39.9 %reduce-scatter.13.cloned.1.call-done = bf16[3,128,256]{2,1,0:T(8,128)(2,1)} async-done(((bf16[3,1024,256]{2,1,0:T(8,128)(2,1)}), bf16[3,128,256]{2,1,0:T(8,128)(2,1)}) %reduce-scatter.13.cloned.1.call-update) | async-done | bytes 196624 | tf_op jit(solution)/shard_map/reduce_scatter | solution.py:287
  2035.9 42.7 %reduce-scatter.19.cloned.1.call-done = bf16[128,1024]{1,0:T(8,128)(2,1)} async-done(((bf16[1024,1024]{1,0:T(8,128)(2,1)}), bf16[128,1024]{1,0:T(8,128)(2,1)}) %reduce-scatter.19.cloned.1.call-update) | async-done | bytes 262160
  2080.5 42.9 %reduce-scatter.15.cloned.1.call-done = bf16[128,1024]{1,0:T(8,128)(2,1)} async-done(((bf16[1024,1024]{1,0:T(8,128)(2,1)}), bf16[128,1024]{1,0:T(8,128)(2,1)}) %reduce-scatter.15.cloned.1.call-update) | async-done | bytes 262160 | tf_op jit(solution)/shard_map/reduce_scatter | solution.py:293
  (1157 shorter events, 1181.5 us)
Async XLA Ops:
  13.7 88.8 %all-gather.13.cloned.1.call-start = ((), (), s32[]{:S(2)}) async-start(), calls=%async_computation.14 | async-start | bytes 7077888 | tf_op jit(solution)/shard_map/while/body/eval_jaxpr/all_gather | solution.py:95
  58.1 126.9 %reduce-scatter.21.cloned.1.call-start = ((), (), s32[]{:S(2)}) async-start(), calls=%async_computation.15 | async-start | bytes 3932160 | tf_op jit(solution)/shard_map/while/body/eval_jaxpr/reduce_scatter | solution.py:124
  124.6 101.2 %all-gather.15.cloned.1.call-start = ((), (), s32[]{:S(2)}) async-start(), calls=%async_computation.16 | async-start | bytes 1966080 | tf_op jit(solution)/shard_map/while/body/eval_jaxpr/all_gather | solution.py:134
  191.0 118.1 %reduce-scatter.23.cloned.1.call-start = ((), (), s32[]{:S(2)}) async-start(), calls=%async_computation.18 | async-start | bytes 1966080 | tf_op jit(solution)/shard_map/while/body/eval_jaxpr/reduce_scatter | solution.py:159
  314.7 102.2 %all-gather.21.cloned.1.call-start = ((), (), s32[]{:S(2)}) async-start(), calls=%async_computation.20 | async-start | bytes 7077888 | tf_op jit(solution)/shard_map/while/body/eval_jaxpr/all_gather | solution.py:208
  378.4 112.5 %reduce-scatter.25.cloned.1.call-start = ((), (), s32[]{:S(2)}) async-start(), calls=%async_computation.21 | async-start | bytes 1966080 | tf_op jit(solution)/shard_map/while/body/eval_jaxpr/reduce_scatter | solution.py:235
  543.2 126.9 %reduce-scatter.21.cloned.1.call-start = ((), (), s32[]{:S(2)}) async-start(), calls=%async_computation.15 | async-start | bytes 3932160 | tf_op jit(solution)/shard_map/while/body/eval_jaxpr/reduce_scatter | solution.py:124
  609.7 101.2 %all-gather.15.cloned.1.call-start = ((), (), s32[]{:S(2)}) async-start(), calls=%async_computation.16 | async-start | bytes 1966080 | tf_op jit(solution)/shard_map/while/body/eval_jaxpr/all_gather | solution.py:134
  676.1 118.1 %reduce-scatter.23.cloned.1.call-start = ((), (), s32[]{:S(2)}) async-start(), calls=%async_computation.18 | async-start | bytes 1966080 | tf_op jit(solution)/shard_map/while/body/eval_jaxpr/reduce_scatter | solution.py:159
  799.8 102.2 %all-gather.21.cloned.1.call-start = ((), (), s32[]{:S(2)}) async-start(), calls=%async_computation.20 | async-start | bytes 7077888 | tf_op jit(solution)/shard_map/while/body/eval_jaxpr/all_gather | solution.py:208
  863.5 112.5 %reduce-scatter.25.cloned.1.call-start = ((), (), s32[]{:S(2)}) async-start(), calls=%async_computation.21 | async-start | bytes 1966080 | tf_op jit(solution)/shard_map/while/body/eval_jaxpr/reduce_scatter | solution.py:235
  1028.1 126.9 %reduce-scatter.21.cloned.1.call-start = ((), (), s32[]{:S(2)}) async-start(), calls=%async_computation.15 | async-start | bytes 3932160 | tf_op jit(solution)/shard_map/while/body/eval_jaxpr/reduce_scatter | solution.py:124
  1094.6 101.2 %all-gather.15.cloned.1.call-start = ((), (), s32[]{:S(2)}) async-start(), calls=%async_computation.16 | async-start | bytes 1966080 | tf_op jit(solution)/shard_map/while/body/eval_jaxpr/all_gather | solution.py:134
  1161.0 118.2 %reduce-scatter.23.cloned.1.call-start = ((), (), s32[]{:S(2)}) async-start(), calls=%async_computation.18 | async-start | bytes 1966080 | tf_op jit(solution)/shard_map/while/body/eval_jaxpr/reduce_scatter | solution.py:159
  1284.8 102.2 %all-gather.21.cloned.1.call-start = ((), (), s32[]{:S(2)}) async-start(), calls=%async_computation.20 | async-start | bytes 7077888 | tf_op jit(solution)/shard_map/while/body/eval_jaxpr/all_gather | solution.py:208
  1348.6 112.5 %reduce-scatter.25.cloned.1.call-start = ((), (), s32[]{:S(2)}) async-start(), calls=%async_computation.21 | async-start | bytes 1966080 | tf_op jit(solution)/shard_map/while/body/eval_jaxpr/reduce_scatter | solution.py:235
  1513.3 126.9 %reduce-scatter.21.cloned.1.call-start = ((), (), s32[]{:S(2)}) async-start(), calls=%async_computation.15 | async-start | bytes 3932160 | tf_op jit(solution)/shard_map/while/body/eval_jaxpr/reduce_scatter | solution.py:124
  1579.8 101.2 %all-gather.15.cloned.1.call-start = ((), (), s32[]{:S(2)}) async-start(), calls=%async_computation.16 | async-start | bytes 1966080 | tf_op jit(solution)/shard_map/while/body/eval_jaxpr/all_gather | solution.py:134
  1646.2 118.3 %reduce-scatter.23.cloned.1.call-start = ((), (), s32[]{:S(2)}) async-start(), calls=%async_computation.18 | async-start | bytes 1966080 | tf_op jit(solution)/shard_map/while/body/eval_jaxpr/reduce_scatter | solution.py:159
  1770.1 102.2 %all-gather.21.cloned.1.call-start = ((), (), s32[]{:S(2)}) async-start(), calls=%async_computation.20 | async-start | bytes 7077888 | tf_op jit(solution)/shard_map/while/body/eval_jaxpr/all_gather | solution.py:208
  1833.8 112.5 %reduce-scatter.25.cloned.1.call-start = ((), (), s32[]{:S(2)}) async-start(), calls=%async_computation.21 | async-start | bytes 1966080 | tf_op jit(solution)/shard_map/while/body/eval_jaxpr/reduce_scatter | solution.py:235
  1960.6 117.9 %reduce-scatter.19.cloned.1.call-start = ((), (), s32[]{:S(2)}) async-start(), calls=%async_computation.11 | async-start | bytes 2359296
  1965.8 157.6 %reduce-scatter.15.cloned.1.call-start = ((), (), s32[]{:S(2)}) async-start(), calls=%async_computation.9 | async-start | bytes 2359296 | tf_op jit(solution)/shard_map/reduce_scatter | solution.py:293
  1969.8 155.4 %all-reduce.3.cloned.1.call-start = ((), (), s32[]{:S(2)}) async-start(), calls=%async_computation.12 | async-start | bytes 131072 | tf_op jit(solution)/shard_map/psum | solution.py:308
  (317 other events, 4307.8 us)
Sparse Core Ops, SparseCore 0:
  13.8 39.7 all-gather.10
  58.2 44.2 all-gather.12
  124.7 60.2 reduce-scatter.20
  188.6 37.1 all-gather.14
  314.8 36.0 all-gather.18
  372.4 44.3 all-gather.20
  502.7 36.0 all-gather.10
  543.3 44.2 all-gather.12
  609.8 60.2 reduce-scatter.20
  673.7 37.1 all-gather.14
  799.9 36.0 all-gather.18
  857.5 44.3 all-gather.20
  987.6 36.0 all-gather.10
  1028.2 44.2 all-gather.12
  1094.7 60.2 reduce-scatter.20
  1158.6 37.1 all-gather.14
  1285.0 36.0 all-gather.18
  1342.6 44.3 all-gather.20
  1472.8 36.0 all-gather.10
  1513.5 44.2 all-gather.12
  1579.9 60.2 reduce-scatter.20
  1643.9 37.1 all-gather.14
  1827.8 44.3 all-gather.20
  1978.2 122.0 all-reduce.2
  (17 shorter events, 593.7 us)
Sparse Core Ops, SparseCore 1:
  1959.5 33.1 reduce-scatter.16
  1995.8 38.3 reduce-scatter.12
  2037.3 41.2 reduce-scatter.18
  2082.2 41.1 reduce-scatter.14
where the time goes:
time: 2150 us; the launch traced here: 2140 us
  waiting for transfers between devices  1480 us (69%)
  matrix products  281 us (13%)
  local copies, waits for them, and re-layouts  199 us (9%)
  other arithmetic  134 us (6%)
  starting transfers between devices  25.1 us (1%)
    reduce_scatter x4, waiting for transfers between devices, one_batch(): lax.psum_scatter(jnp.dot(attended, w_out, preferred_element_type=jnp.floa...  241 us
    all_gather x4, waiting for transfers between devices, one_batch(): normed_all = lax.all_gather(normed, 'head', axis=0, tiled=True)  148 us
    all_gather x4, waiting for transfers between devices, one_batch(): grad_branch_all = lax.all_gather(grad_branch, 'head', axis=0, tiled=True)  145 us
    all_gather x4, waiting for transfers between devices, one_batch(): piece = lax.all_gather(key_value, 'dp', axis=0, tiled=True)  142 us
    reduce_scatter x4, waiting for transfers between devices, one_batch(): lax.psum_scatter(jnp.einsum('gf,df->gd', grad_hidden, w_fc1, preferred_el...  137 us
    all_gather x4, waiting for transfers between devices, one_batch(): incoming_all = lax.all_gather(incoming, 'head', axis=0, tiled=True)  128 us
    all_gather x4, waiting for transfers between devices, one_batch(): normed_two_all = lax.all_gather(normed_two, 'head', axis=0, tiled=True)  116 us
    all_gather x4, waiting for transfers between devices, one_batch(): lax.all_gather(grad_far.astype(jnp.bfloat16), 'dp', axis=0, tiled=True)  112 us
  transfers between devices with their start and end apart: 45, of which 44 were waited for; matrix products, arithmetic and copies ran while one was open for 13% of the time, Pallas kernels for 0%

commit v1 on v0

v1 whole, which is shorter than its diff:
```python
import functools
import math

import jax
import jax.numpy as jnp
from jax import lax
from jax.experimental import pallas as pl
from jax.experimental.pallas import tpu as pltpu
from jax.sharding import PartitionSpec as P

HEAD_DIM = 64
BLOCK = 128
UP = 4
PAIR = 2 * HEAD_DIM
NEGATIVE = -1e30
epsilon = 1e-05
f32 = jnp.float32
bf16 = jnp.bfloat16
ROOT_2_PI = math.sqrt(2.0 / math.pi)
ANY = pl.BlockSpec(memory_space=pl.ANY)


def xor_swap(value, axis, mask):
    size = lax.axis_size(axis)
    return lax.ppermute(value, axis, [(i, i ^ mask) for i in range(size)])


def norm_forward(values, gain, shift):
    centered = values - jnp.mean(values, axis=-1, keepdims=True)
    inverse = lax.rsqrt(jnp.mean(centered * centered, axis=-1, keepdims=True) + epsilon)
    standard = centered * inverse
    return (standard * gain + shift, standard, inverse)


def norm_backward(upstream, standard, inverse, gain):
    scaled = upstream * gain
    inner = (
        scaled
        - jnp.mean(scaled, axis=-1, keepdims=True)
        - standard * jnp.mean(scaled * standard, axis=-1, keepdims=True)
    )
    return (inner * inverse, jnp.sum(upstream * standard, axis=0), jnp.sum(upstream, axis=0))


def mm(left, right):
    return jnp.dot(left, right, preferred_element_type=f32)


def mm_nt(left, right):
    return lax.dot_general(left, right, (((1,), (1,)), ((), ())), preferred_element_type=f32)


def mm_tn(left, right):
    return lax.dot_general(left, right, (((0,), (0,)), ((), ())), preferred_element_type=f32)


def pair_probs(q_pair, k_cat, allowed):
    low_half = lax.broadcasted_iota(jnp.int32, (BLOCK, PAIR), 1) < HEAD_DIM
    zero = jnp.zeros_like(q_pair)
    q_stack = jnp.concatenate(
        [jnp.where(low_half, q_pair, zero), jnp.where(low_half, zero, q_pair)], axis=0
    )
    scores = mm_nt(k_cat, q_stack) * (1.0 / math.sqrt(HEAD_DIM))
    scores = jnp.where(allowed, scores, NEGATIVE)
    top = jnp.max(scores, axis=0, keepdims=True)
    raised = jnp.exp(scores - top)
    probs = raised * (1.0 / jnp.sum(raised, axis=0, keepdims=True))
    return q_stack, probs, low_half


def allowed_mask(far_flag):
    key_at = lax.broadcasted_iota(jnp.int32, (2 * BLOCK, 2 * BLOCK), 0)
    query_at = lax.broadcasted_iota(jnp.int32, (2 * BLOCK, 2 * BLOCK), 1)
    query_at = jnp.where(query_at >= BLOCK, query_at - BLOCK, query_at)
    first = jnp.where(far_flag > 0, BLOCK, 2 * BLOCK)
    return (key_at <= query_at) | (key_at >= first)


def attention_forward_kernel(pairs, has_far, q_ref, own_ref, far_ref, out_ref):
    allowed = allowed_mask(has_far[pl.program_id(0)])
    width = pairs * PAIR
    for p in range(pairs):
        cols = slice(p * PAIR, (p + 1) * PAIR)
        vcols = slice(width + p * PAIR, width + (p + 1) * PAIR)
        k_cat = jnp.concatenate([own_ref[:, cols], far_ref[:, cols]], axis=0)
        v_cat = jnp.concatenate([own_ref[:, vcols], far_ref[:, vcols]], axis=0)
        _, probs, low_half = pair_probs(q_ref[:, cols], k_cat, allowed)
        mixed = mm_tn(probs.astype(bf16), v_cat)
        out_ref[:, cols] = jnp.where(low_half, mixed[:BLOCK], mixed[BLOCK:]).astype(bf16)


def attention_backward_kernel(
    pairs, has_far, q_ref, own_ref, far_ref, grad_ref, dq_ref, down_ref, dfar_ref
):
    allowed = allowed_mask(has_far[pl.program_id(0)])
    width = pairs * PAIR
    scale = 1.0 / math.sqrt(HEAD_DIM)
    for p in range(pairs):
        cols = slice(p * PAIR, (p + 1) * PAIR)
        vcols = slice(width + p * PAIR, width + (p + 1) * PAIR)
        k_cat = jnp.concatenate([own_ref[:, cols], far_ref[:, cols]], axis=0)
        v_cat = jnp.concatenate([own_ref[:, vcols], far_ref[:, vcols]], axis=0)
        q_stack, probs, low_half = pair_probs(q_ref[:, cols], k_cat, allowed)
        grad = grad_ref[:, cols]
        zero = jnp.zeros_like(grad)
        grad_stack = jnp.concatenate(
            [jnp.where(low_half, grad, zero), jnp.where(low_half, zero, grad)], axis=0
        )
        grad_probs = mm_nt(v_cat, grad_stack)
        total = jnp.sum(probs * grad_probs, axis=0, keepdims=True)
        grad_scores = (probs * (grad_probs - total)).astype(bf16)
        dq = mm_tn(grad_scores, k_cat) * scale
        dq_ref[:, cols] = jnp.where(low_half, dq[:BLOCK], dq[BLOCK:]).astype(bf16)
        dk = (mm(grad_scores, q_stack) * scale).astype(bf16)
        dv = mm(probs.astype(bf16), grad_stack).astype(bf16)
        down_ref[:, cols] = dk[:BLOCK]
        dfar_ref[:, cols] = dk[BLOCK:]
        down_ref[:, vcols] = dv[:BLOCK]
        dfar_ref[:, vcols] = dv[BLOCK:]


def attention_call(kernel, has_far, blocked, outs):
    blocks = has_far.shape[0]
    row_block = lambda width: pl.BlockSpec((BLOCK, width), lambda b, flags: (b, 0))
    width = blocked[0].shape[1]
    return pl.pallas_call(
        functools.partial(kernel, width // PAIR),
        grid_spec=pltpu.PrefetchScalarGridSpec(
            num_scalar_prefetch=1,
            grid=(blocks,),
            in_specs=[row_block(a.shape[1]) for a in blocked],
            out_specs=[row_block(w) for w in outs],
        ),
        out_shape=[jax.ShapeDtypeStruct((blocks * BLOCK, w), bf16) for w in outs],
        compiler_params=pltpu.CompilerParams(vmem_limit_bytes=48 << 20),
        cost_estimate=pl.CostEstimate(
            flops=blocks * width * BLOCK * BLOCK * 16,
            bytes_accessed=blocks * BLOCK * width * 16,
            transcendentals=blocks * width * BLOCK * 4,
        ),
    )(has_far, *blocked)


def far_pick_kernel(where_a, where_b, a_ref, b_ref, out_ref):
    half = a_ref.shape[2]
    out_ref[0, :, :half] = a_ref[0]
    out_ref[0, :, half:] = b_ref[0]


def far_pick(table_a, table_b, where_a, where_b):
    count, half = where_a.shape[0], table_a.shape[2]
    spec = lambda which: pl.BlockSpec((1, BLOCK, half), lambda j, wa, wb: ((wa, wb)[which][j], 0, 0))
    return pl.pallas_call(
        far_pick_kernel,
        grid_spec=pltpu.PrefetchScalarGridSpec(
            num_scalar_prefetch=2,
            grid=(count,),
            in_specs=[spec(0), spec(1)],
            out_specs=pl.BlockSpec((1, BLOCK, 2 * half), lambda j, wa, wb: (j, 0, 0)),
        ),
        out_shape=jax.ShapeDtypeStruct((count, BLOCK, 2 * half), bf16),
        cost_estimate=pl.CostEstimate(
            flops=0, bytes_accessed=count * BLOCK * half * 8, transcendentals=0
        ),
    )(where_a, where_b, table_a, table_b)


def far_route_kernel(count, where_a, where_b, mine_ref, other_ref, a_ref, b_ref, acc_ref):
    step = pl.program_id(0)
    half = a_ref.shape[2]
    acc_ref[...] = jnp.zeros_like(acc_ref)
    for source, base in ((mine_ref, 0), (other_ref, count)):
        for j in range(count):

            @pl.when(where_a[base + j] == step)
            def _():
                acc_ref[:, :half] += source[j, :, :half].astype(f32)

            @pl.when(where_b[base + j] == step)
            def _():
                acc_ref[:, half:] += source[j, :, half:].astype(f32)

    a_ref[0] = acc_ref[:, :half].astype(bf16)
    b_ref[0] = acc_ref[:, half:].astype(bf16)


def far_route(mine, other, where_a, where_b, table):
    count, _, width = mine.shape
    whole = pl.BlockSpec(mine.shape, lambda k, wa, wb: (0, 0, 0))
    out = pl.BlockSpec((1, BLOCK, width // 2), lambda k, wa, wb: (k, 0, 0))
    shape = jax.ShapeDtypeStruct((table, BLOCK, width // 2), bf16)
    return pl.pallas_call(
        functools.partial(far_route_kernel, count),
        grid_spec=pltpu.PrefetchScalarGridSpec(
            num_scalar_prefetch=2,
            grid=(table,),
            in_specs=[whole, whole],
            out_specs=[out, out],
            scratch_shapes=[pltpu.VMEM((BLOCK, width), f32)],
        ),
        out_shape=[shape, shape],
        compiler_params=pltpu.CompilerParams(vmem_limit_bytes=32 << 20),
        cost_estimate=pl.CostEstimate(
            flops=0, bytes_accessed=table * BLOCK * width * 2, transcendentals=0
        ),
    )(where_a, where_b, mine, other)


def gather_strips(strip, masks):
    head_size = lax.axis_size("head")
    slots = jnp.stack(
        [
            lax.ppermute(strip, "head", [((i + s) % head_size, i) for i in range(head_size)])
            for s in range(1, head_size)
        ]
    )
    half = strip.shape[0] // 2
    out = []
    for color, order in ((0, masks), (1, masks[::-1])):
        held = slots[None, :, color * half : (color + 1) * half]
        for mask in order:
            held = jnp.concatenate([held, xor_swap(held, "dp", mask)], axis=0)
        out.append(held)
    return out + [xor_swap(held, "dp", 1) for held in out]


def relative_masks(masks):
    return [sum(m for bit, m in enumerate(masks) if k >> bit & 1) for k in range(1 << len(masks))]


def assemble_kernel(copies, n_in, dp_index, *refs):
    ins, outs, sem = refs[:n_in], refs[n_in:-1], refs[-1]
    me = dp_index[0]
    started = []
    for which, index, target, row_xor, half, c0, width, t0 in copies:
        src = ins[which]
        for at in index:
            src = src.at[at]
        if c0 is not None:
            src = src.at[:, pl.ds(c0, width)]
        dst = outs[target]
        if row_xor is not None:
            rows = src.shape[0]
            dst = dst.at[pl.ds(pl.multiple_of((me ^ row_xor) * 2 * rows + half * rows, rows), rows)]
        dst = dst.at[:, pl.ds(t0, width)]
        copy = pltpu.make_async_copy(src, dst, sem.at[len(started)])
        copy.start()
        started.append(copy)
    for copy in started:
        copy.wait()


def assemble(dp_index, ins, copies, shapes):
    return pl.pallas_call(
        functools.partial(assemble_kernel, copies, len(ins)),
        grid_spec=pltpu.PrefetchScalarGridSpec(
            num_scalar_prefetch=1,
            grid=(1,),
            in_specs=[ANY] * len(ins),
            out_specs=[ANY] * len(shapes),
            scratch_shapes=[pltpu.SemaphoreType.DMA((len(copies),))],
        ),
        out_shape=[jax.ShapeDtypeStruct(s, bf16) for s in shapes],
        cost_estimate=pl.CostEstimate(
            flops=0,
            bytes_accessed=sum(4 * math.prod(s) for s in shapes),
            transcendentals=0,
        ),
    )(dp_index, *ins)


def strip_copies(masks, slots, columns):
    out = []
    for which in range(4):
        order = masks if which % 2 == 0 else masks[::-1]
        for k, mask in enumerate(relative_masks(order)):
            for s in range(slots):
                for c0, width, target, place in columns:
                    out.append(
                        (which, (k, s), target, mask | (which // 2), which % 2, c0, width, place(s + 1))
                    )
    return out


def reduce_over_dp(left, right, masks, color):
    keep, send = left
    got = xor_swap(mm_tn(send, right).astype(bf16), "dp", 1)
    part = (mm_tn(keep, right) + got.astype(f32)).astype(bf16)
    bits = len(masks)
    width = part.shape[1]
    part = part.reshape((2,) * bits + (-1, width))
    order = masks if color == 0 else masks[::-1]
    axes = {mask: bits - 1 - i for i, mask in enumerate(masks)}
    live = list(masks)
    for step, mask in enumerate(order):
        axis = len(live) - 1 - live.index(mask)
        live.remove(mask)
        mine = lax.index_in_dim(part, 0, axis, keepdims=False)
        away = lax.index_in_dim(part, 1, axis, keepdims=False)
        got = xor_swap(away, "dp", mask)
        part = (mine.astype(f32) + got.astype(f32)).astype(bf16)
    return part


def reduce_over_head(parts):
    head_size = lax.axis_size("head")
    total = parts[0].astype(f32)
    for s in range(1, head_size):
        got = lax.ppermute(parts[s], "head", [(i, (i + s) % head_size) for i in range(head_size)])
        total = total + got.astype(f32)
    return total


def local(
    activations,
    conditioning,
    cotangent,
    block_targets,
    up_gain,
    norm1_gain,
    norm1_shift,
    w_qkv,
    b_qv,
    w_out,
    b_out,
    norm2_gain,
    norm2_shift,
    w_fc1,
    b_fc1,
    w_fc2,
    b_fc2,
):
    micro, rows, model = activations.shape
    head_cols = w_qkv.shape[2]
    hidden_cols = w_fc1.shape[1]
    dp_size, head_size = lax.axis_size("dp"), lax.axis_size("head")
    me, here = lax.axis_index("dp"), lax.axis_index("head")
    group = head_size // micro
    tokens = rows * micro
    blocks = tokens // BLOCK
    slab = model // dp_size
    masks = [1 << i for i in range(1, dp_size.bit_length() - 1)]
    remote = head_size - 1
    heads_all, hidden_all = head_cols * head_size, hidden_cols * head_size

    src_rank = here % micro
    my_micro, my_sub = here // group, here % group
    shifts = [
        [(hs * micro + hr, ((hr + s) % micro) * group + hs) for hs in range(group) for hr in range(micro)]
        for s in range(micro)
    ]

    def send(value, pairs):
        return value if all(a == b for a, b in pairs) else lax.ppermute(value, "head", pairs)

    def choose(options, index):
        out = options[-1]
        for k in range(len(options) - 1):
            out = jnp.where(index == k, options[k], out)
        return out

    def to_micro(value):
        got = [
            send(lax.dynamic_index_in_dim(value, (src_rank + s) % micro, 0, False), shifts[s])
            for s in range(micro)
        ]
        return [choose(got, (my_micro - p) % micro) for p in range(micro)]

    def from_micro(value):
        pieces = value.reshape(micro, rows, -1)
        got = [
            send(
                lax.dynamic_index_in_dim(pieces, (my_micro - s) % micro, 0, False),
                [(b, a) for a, b in shifts[s]],
            )
            for s in range(micro)
        ]
        return jnp.stack([choose(got, (m - src_rank) % micro) for m in range(micro)])

    packed = to_micro(jnp.concatenate([activations, conditioning], axis=1))
    acts = jnp.concatenate([p[:rows] for p in packed], axis=0)
    coarse = jnp.concatenate([p[rows:] for p in packed], axis=0).astype(f32)
    incoming = jnp.concatenate(to_micro(cotangent), axis=0)

    def my_slab(value, axis):
        return lax.dynamic_slice_in_dim(value, me * slab, slab, axis)

    strip_a = jnp.concatenate(
        [my_slab(w_qkv[0], 0), my_slab(w_qkv[1], 0), my_slab(w_qkv[2], 0), my_slab(w_out, 1).T],
        axis=1,
    )
    strip_f = jnp.concatenate([my_slab(w_fc1, 0), my_slab(w_fc2, 1).T], axis=1)
    dp_index = me.reshape(1).astype(jnp.int32)
    hc, fc = head_cols, hidden_cols
    got_a = gather_strips(strip_a, masks)
    own_a = [(4, (t,), 0 if t == 0 else 1, None, 0, 0, hc, (t == 2) * heads_all) for t in range(3)]
    own_a += [(5, (), 2, None, 0, 0, hc, 0)]
    w_query, w_kv, w_out_t = assemble(
        dp_index,
        got_a + [w_qkv, w_out.T],
        strip_copies(
            masks,
            remote,
            [
                (0, hc, 0, lambda s: s * hc),
                (hc, hc, 1, lambda s: s * hc),
                (2 * hc, hc, 1, lambda s: heads_all + s * hc),
                (3 * hc, hc, 2, lambda s: s * hc),
            ],
        )
        + own_a,
        [(model, heads_all), (model, 2 * heads_all), (model, heads_all)],
    )
    got_f = gather_strips(strip_f, masks)
    w_one, w_two_t = assemble(
        dp_index,
        got_f + [w_fc1, w_fc2.T],
        strip_copies(masks, remote, [(0, fc, 0, lambda s: s * fc), (fc, fc, 1, lambda s: s * fc)])
        + [(4, (), 0, None, 0, 0, fc, 0), (5, (), 1, None, 0, 0, fc, 0)],
        [(model, hidden_all), (model, hidden_all)],
    )
    small = jnp.concatenate([b_qv.reshape(-1), b_fc1])
    biases = [small] + [
        lax.ppermute(small, "head", [((i + s) % head_size, i) for i in range(head_size)])
        for s in range(1, head_size)
    ]
    bias_q = jnp.concatenate([b[:hc] for b in biases])
    bias_v = jnp.concatenate([b[hc : 2 * hc] for b in biases])
    bias_one = jnp.concatenate([b[2 * hc :] for b in biases])
    bias_kv = jnp.concatenate([jnp.zeros_like(bias_v), bias_v])

    joined = (
        acts.astype(f32).reshape(-1, UP, model) + coarse[:, None, :] * up_gain[None]
    ).reshape(tokens, model)
    normed_f, standard_one, inverse_one = norm_forward(joined, norm1_gain, norm1_shift)
    normed = normed_f.astype(bf16)

    stages_sub = [("head", 1 << i) for i in range(group.bit_length() - 1)]
    stage_lists = [
        stages_sub + [("dp", m) for m in masks],
        stages_sub + [("dp", m) for m in masks[::-1]],
    ]
    shaped = normed.reshape(blocks, BLOCK, model)
    half = model // 2
    tables = []
    for color in range(2):
        held = shaped[:, :, color * half : (color + 1) * half]
        for axis, mask in stage_lists[color]:
            held = jnp.concatenate([held, xor_swap(held, axis, mask)], axis=0)
        tables.append(held)
    table_blocks = tables[0].shape[0]
    table_row = lax.dynamic_index_in_dim(block_targets, my_micro, 0, False)

    def targets_of(device):
        return lax.dynamic_slice_in_dim(table_row, (device * group + my_sub) * blocks, blocks)

    targets = targets_of(me)
    targets_both = jnp.concatenate([targets, targets_of(me ^ 1)])
    owner = jnp.maximum(targets_both, 0) // blocks
    away = (owner // group) ^ me
    away_sub = (owner % group) ^ my_sub

    def table_index(stages):
        index = jnp.zeros_like(owner)
        for bit, (axis, mask) in enumerate(stages):
            far_bits = away if axis == "dp" else away_sub
            index = index + (((far_bits & mask) != 0).astype(jnp.int32) << bit)
        return index * blocks + jnp.maximum(targets_both, 0) % blocks

    index_a, index_b = table_index(stage_lists[0]), table_index(stage_lists[1])
    on_my_core = (away & 1) == 0
    picked = far_pick(tables[0], tables[1], index_a, index_b)
    passed = xor_swap(picked[blocks:], "dp", 1)
    far = jnp.where(on_my_core[:blocks, None, None], picked[:blocks], passed).reshape(tokens, model)
    has_far = (targets >= 0).astype(jnp.int32)

    queries = (mm(normed, w_query) + bias_q).astype(bf16)
    kv_own = (mm(normed, w_kv) + bias_kv).astype(bf16)
    kv_far = (mm(far, w_kv) + bias_kv).astype(bf16)
    (attended,) = attention_call(
        attention_forward_kernel, has_far, [queries, kv_own, kv_far], [heads_all]
    )
    residual = joined + (mm_nt(attended, w_out_t) + b_out)

    normed2_f, standard_two, inverse_two = norm_forward(residual, norm2_gain, norm2_shift)
    normed_two = normed2_f.astype(bf16)
    hidden = mm(normed_two, w_one) + bias_one
    inner = jnp.tanh(ROOT_2_PI * (hidden + 0.044715 * hidden * hidden * hidden))
    activated = (0.5 * hidden * (1.0 + inner)).astype(bf16)
    slope = (
        0.5 * (1.0 + inner)
        + 0.5 * hidden * (1.0 - inner * inner) * (ROOT_2_PI * (1.0 + 3 * 0.044715 * hidden * hidden))
    ).astype(bf16)
    layer_out = from_micro((residual + (mm_nt(activated, w_two_t) + b_fc2)).astype(bf16))

    position_masks = relative_masks(masks)
    order = jnp.array(position_masks + [m | 1 for m in position_masks], jnp.int32)
    column = jnp.arange(model, dtype=jnp.int32)
    source = (me ^ jnp.repeat(order, slab)) * slab + column % slab
    shuffle = (column[:, None] == source[None, :]).astype(bf16)

    def relative(value):
        moved = mm(value, shuffle).astype(bf16)
        return moved[:, : model // 2], moved[:, model // 2 :]

    incoming_f = incoming.astype(f32)
    grad_b2 = jnp.sum(incoming_f, axis=0)
    left_two = relative(incoming)
    hidden_half = hidden_all // 2
    part_two = [
        reduce_over_dp(left_two, activated[:, c * hidden_half : (c + 1) * hidden_half], masks, c)
        for c in range(2)
    ]
    grad_hidden = (mm(incoming, w_two_t) * slope.astype(f32)).astype(bf16)
    grad_b1 = jnp.sum(grad_hidden.astype(f32), axis=0)
    left_one = relative(normed_two)
    part_one = [
        reduce_over_dp(left_one, grad_hidden[:, c * hidden_half : (c + 1) * hidden_half], masks, c)
        for c in range(2)
    ]

    def slots_of(halves, width):
        whole = jnp.concatenate(halves, axis=1)
        return [whole[:, s * width : (s + 1) * width] for s in range(head_size)]

    grad_w2 = reduce_over_head(slots_of(part_two, fc)).T
    grad_w1 = reduce_over_head(slots_of(part_one, fc))

    grad_normed_two = mm_nt(grad_hidden, w_one)
    grad_res_part, grad_g2, grad_s2 = norm_backward(
        grad_normed_two, standard_two, inverse_two, norm2_gain
    )
    grad_residual = incoming_f + grad_res_part
    grad_branch = grad_residual.astype(bf16)
    grad_bo = jnp.sum(grad_branch.astype(f32), axis=0)
    grad_att = mm(grad_branch, w_out_t).astype(bf16)
    grad_q, grad_own, grad_far = attention_call(
        attention_backward_kernel,
        has_far,
        [queries, kv_own, kv_far, grad_att],
        [heads_all, 2 * heads_all, 2 * heads_all],
    )
    far_back = mm_nt(grad_far, w_kv).astype(bf16).reshape(blocks, BLOCK, model)
    far_other = xor_swap(far_back, "dp", 1)
    valid = on_my_core & (targets_both >= 0)
    route_a = jnp.where(valid, index_a, -1)
    route_b = jnp.where(valid, index_b, -1)
    returned = []
    for color, held in enumerate(far_route(far_back, far_other, route_a, route_b, table_blocks)):
        for axis, mask in stage_lists[color][::-1]:
            keep = held.shape[0] // 2
            got = xor_swap(held[keep:], axis, mask)
            held = held[:keep].astype(f32) + got.astype(f32)
            if keep > blocks:
                held = held.astype(bf16)
        returned.append(held)
    returned = jnp.concatenate(returned, axis=2).reshape(tokens, model).astype(f32)

    left_q, left_o = relative(normed), relative(grad_branch)
    left_kv = tuple(
        jnp.concatenate([a, b], axis=0) for a, b in zip(left_q, relative(far))
    )
    grad_kv = jnp.concatenate([grad_own, grad_far], axis=0)
    part_q = reduce_over_dp(left_q, grad_q, masks, 0)
    part_k = reduce_over_dp(left_kv, grad_kv[:, :heads_all], masks, 0)
    part_v = reduce_over_dp(left_kv, grad_kv[:, heads_all:], masks, 1)
    part_o = reduce_over_dp(left_o, attended, masks, 1)
    per_slot = [
        jnp.concatenate([p[:, s * hc : (s + 1) * hc] for p in (part_q, part_k, part_v, part_o)], axis=1)
        for s in range(head_size)
    ]
    grad_wa = reduce_over_head(per_slot)
    grad_wqkv = jnp.stack([grad_wa[:, t * hc : (t + 1) * hc] for t in range(3)])
    grad_wo = grad_wa[:, 3 * hc :].T
    grad_bq = jnp.sum(grad_q.astype(f32), axis=0)
    grad_bv = jnp.sum(grad_kv[:, heads_all:].astype(f32), axis=0)

    grad_normed = mm_nt(grad_q, w_query) + mm_nt(grad_own, w_kv) + returned
    grad_join_part, grad_g1, grad_s1 = norm_backward(
        grad_normed, standard_one, inverse_one, norm1_gain
    )
    grad_joined = grad_residual + grad_join_part
    grad_up = jnp.sum(grad_joined.reshape(-1, UP, model) * coarse[:, None, :], axis=0)
    grad_input = from_micro(grad_joined.astype(bf16)).astype(f32)
    grad_coarse = jnp.sum(grad_input.reshape(micro, -1, UP, model) * up_gain, axis=2)

    def absolute(value, width):
        return jnp.roll(value.reshape(head_size, width), here, axis=0).reshape(-1)

    pieces = [
        grad_up.reshape(-1),
        grad_g1,
        grad_s1,
        absolute(grad_bq, hc),
        absolute(grad_bv, hc),
        grad_bo,
        grad_g2,
        grad_s2,
        absolute(grad_b1, fc),
        grad_b2,
    ]
    sizes = [p.shape[0] for p in pieces]
    total = jnp.concatenate(pieces).reshape(-1, model)
    for axis, size in (("dp", dp_size), ("head", head_size)):
        for i in range(size.bit_length() - 1):
            total = total + xor_swap(total, axis, 1 << i)
    total = total.reshape(-1)
    sums, at = [], 0
    for size in sizes:
        sums.append(total[at : at + size])
        at += size
    s_up, s_g1, s_s1, s_bq, s_bv, s_bo, s_g2, s_s2, s_b1, s_b2 = sums
    return (
        layer_out,
        grad_input,
        grad_coarse,
        s_up.reshape(UP, model),
        s_g1,
        s_s1,
        grad_wqkv,
        jnp.stack([s_bq, s_bv]),
        grad_wo,
        s_bo,
        s_g2,
        s_s2,
        grad_w1,
        s_b1,
        grad_w2,
        s_b2,
    )


def solution(mesh):
    rows = P(None, ("dp", "head"), None)
    return jax.shard_map(
        local,
        mesh=mesh,
        in_specs=(
            rows,
            rows,
            rows,
            P(),
            P(),
            P(),
            P(),
            P(None, None, "head"),
            P(None, "head"),
            P("head", None),
            P(),
            P(),
            P(),
            P(None, "head"),
            P("head"),
            P("head", None),
            P(),
        ),
        out_specs=(
            rows,
            rows,
            rows,
            P(),
            P(),
            P(),
            P(None, "dp", "head"),
            P(),
            P("head", "dp"),
            P(),
            P(),
            P(),
            P("dp", "head"),
            P(),
            P("head", "dp"),
            P(),
        ),
        check_vma=False,
    )
```

time: 2150 us -> 1580 us (0.73)
  waiting for transfers between devices: 1480 us -> 298 us
  Pallas kernels: 0 us -> 820 us
  matrix products: 281 us -> 162 us
  local copies, waits for them, and re-layouts: 199 us -> 97.2 us
  starting transfers between devices: 25.1 us -> 119 us
  other arithmetic: 134 us -> 75.9 us
    pallas_call x0 -> x6, Pallas kernels: none -> 820 us  [the longest x2 767 us: assemble(): pl.pallas_call(functools.partial(assemble_kernel, copies, len(ins)), grid...]
    all_gather x24 -> x0, waiting for transfers between devices: 791 us -> none  [the longest x4 148 us: one_batch(): normed_all = lax.all_gather(normed, 'head', axis=0, tiled=True)]
    reduce_scatter x18 -> x0, waiting for transfers between devices: 625 us -> none  [the longest x4 241 us: one_batch(): lax.psum_scatter(jnp.dot(attended, w_out, preferred_element_type=jnp.floa...]
    ppermute x0 -> x81, waiting for transfers between devices: none -> 298 us  [the longest x51 234 us: xor_swap(): return lax.ppermute(value, axis, [(i, i ^ mask) for i in range(size)])]
    dot_general x76 -> x33, matrix products: 281 us -> 162 us  [the longest x11 63.5 us: mm(): return jnp.dot(left, right, preferred_element_type=f32)]
    ppermute x0 -> x81, starting transfers between devices: none -> 119 us  [the longest x51 46.4 us: xor_swap(): return lax.ppermute(value, axis, [(i, i ^ mask) for i in range(size)])]
    reshape x40 -> x5, local copies, waits for them, and re-layouts: 84.2 us -> 4.51 us  [the longest x1 2.55 us: local(): grad_joined.reshape(-1, UP, model) * coarse[:, None, :]]
    unnamed x7 -> x0, waiting for transfers between devices: 64.6 us -> none
  transfers between devices with their start and end apart: 45 -> 81, of which waited for: 44 -> 29; matrix products, arithmetic and copies ran while one was open for 13% -> 14% of each run, Pallas kernels for 0% -> 18%
where the time goes in v1:
time: 1580 us; the launch traced here: 1570 us
  Pallas kernels  820 us (52%)
  waiting for transfers between devices  298 us (19%)
  matrix products  162 us (10%)
  starting transfers between devices  119 us (8%)
  local copies, waits for them, and re-layouts  97.2 us (6%)
  other arithmetic  75.9 us (5%)
    pallas_call x2, Pallas kernels, assemble(): pl.pallas_call(functools.partial(assemble_kernel, copies, len(ins)), grid...  767 us
    ppermute x51, waiting for transfers between devices, xor_swap(): return lax.ppermute(value, axis, [(i, i ^ mask) for i in range(size)])  234 us
    dot_general x11, matrix products, mm(): return jnp.dot(left, right, preferred_element_type=f32)  63.5 us
    ppermute x12, waiting for transfers between devices, send(): lax.ppermute(value, 'head', pairs)  60.3 us
    dot_general x16, matrix products, mm_tn(): lax.dot_general(left, right, (((0,), (0,)), ((), ())), preferred_element_...  56.3 us
    ppermute x51, starting transfers between devices, xor_swap(): return lax.ppermute(value, axis, [(i, i ^ mask) for i in range(size)])  46.4 us
    dot_general x6, matrix products, mm_nt(): lax.dot_general(left, right, (((1,), (1,)), ((), ())), preferred_element_...  41.9 us
    unnamed x254, local copies, waits for them, and re-layouts  35.7 us
  transfers between devices with their start and end apart: 81, of which 29 were waited for; matrix products, arithmetic and copies ran while one was open for 14% of the time, Pallas kernels for 18%

profile of v1, /device:TPU:0, one launch (start us, length us, event | category | flops | bytes accessed | tf_op | source)
XLA Modules:
  0.0 1574.4 jit_solution(2040187541217017302)
XLA Ops:
  46.9 19.6 %collective-permute-done.32 = bf16[192,1024]{1,0:T(8,128)(2,1)S(1)} collective-permute-done((bf16[192,1024]{1,0:T(8,128)(2,1)}, bf16[192,1024]{1,0:T(8,128)(2,1)S(1)}, u32[]{:S(2)}, u32[]{:S(2)}) %collective-permute-start.32) | collective-permute-done | bytes 393248 | tf_op jit(solution)/shard_map/ppermute | solution.py:354
  66.5 10.3 collective-permute-start.2
  83.3 11.3 collective-permute-start.21
  96.9 31.2 %collective-permute-done = bf16[240,1024]{1,0:T(8,128)(2,1)S(1)} collective-permute-done((bf16[240,1024]{1,0:T(8,128)(2,1)}, bf16[240,1024]{1,0:T(8,128)(2,1)S(1)}, u32[]{:S(2)}, u32[]{:S(2)}) %collective-permute-start) | collective-permute-done | bytes 491552 | tf_op jit(solution)/shard_map/ppermute | solution.py:354
  156.8 11.4 collective-permute-done.15
  186.9 10.7 collective-permute-done.25
  200.4 47.7 %collective-permute-done.7 = bf16[2,3,64,1024]{3,2,1,0:T(8,128)(2,1)S(1)} collective-permute-done((bf16[2,3,64,1024]{3,2,1,0:T(8,128)(2,1)S(1)}, bf16[2,3,64,1024]{3,2,1,0:T(8,128)(2,1)S(1)}, u32[]{:S(2)}, u32[]{:S(2)}) %collective-permute-start.7) | collective-permute-done | bytes 786464 | tf_op jit(solution)/shard_map/ppermute | solution.py:25
  260.6 9.4 shard_map.298
  287.9 257.0 %shard_map.297 = (bf16[1024,1024]{1,0:T(8,128)(2,1)}, bf16[1024,2048]{1,0:T(8,128)(2,1)}, bf16[1024,1024]{1,0:T(8,128)(2,1)}) custom-call(s32[1]{0:T(128)} %bitcast.5.dp_index, bf16[4,3,64,1024]{3,2,1,0:T(8,128)(2,1)} %copy-done.20, bf16[4,3,64,1024]{3,2,1,0:T(8,128)(2,1)} %pad_maximum_fusion.6.refs_1_, ...), custom_call_target="tpu_custom_call" | custom-call | bytes 16777216 | tf_op jit(solution)/shard_map/pallas_call | solution.py:254
  559.9 11.3 shard_map.299
  580.3 510.2 %shard_map.300 = (bf16[1024,4096]{1,0:T(8,128)(2,1)}, bf16[1024,4096]{1,0:T(8,128)(2,1)}) custom-call(s32[1]{0:T(128)} %bitcast.5.dp_index, bf16[4,3,64,2048]{3,2,1,0:T(8,128)(2,1)} %pad_maximum_fusion.2.refs_0_, bf16[4,3,64,2048]{3,2,1,0:T(8,128)(2,1)} %pad_maximum_fusion.3.refs_1_, bf16[4,3,64,2048]{3,2,1,0:T(8,128)(2,1)} %collective-permute-done.27.refs_2_, ...), custom_call_target="tpu_custom_call" | custom-call | bytes 33554432 | tf_op jit(solution)/shard_map/pallas_call | solution.py:254
  1090.6 17.4 %multiply_convert_fusion.1 = (bf16[768,4096]{1,0:T(8,128)(2,1)}, f32[768,4096]{1,0:T(8,128)}) fusion(f32[4096]{0:T(1024)S(1)} %copy-done.76, bf16[1024,4096]{1,0:T(8,128)(2,1)} %get-tuple-element.30, f32[768,1024]{1,0:T(8,128)} %copy-done.10, f32[1024]{0:T(1024)S(1)} %copy-done.97, f32[1024]{0:T(1024)S(1)} %copy-done.81, f32[768]{0:T(1024)S(1)} %copy-done.75, ...), kind=kOutput, calls=%fused_computation.11 | convolution fusion | flops 6477840384 | bytes 30439424 | tf_op jit(solution)/shard_map/dot_general | solution.py:46
  1108.0 18.3 %convert_reduce_fusion = (f32[4096]{0:T(1024)}, bf16[768,4096]{1,0:T(8,128)(2,1)S(1)}) fusion(f32[768,4096]{1,0:T(8,128)} %get-tuple-element.178, f32[4096]{0:T(1024)S(1)} %copy-done.76, bf16[1024,4096]{1,0:T(8,128)(2,1)} %get-tuple-element.31, bf16[192,1024]{1,0:T(8,128)(2,1)S(1)} %copy-done.45, bf16[192,1024]{1,0:T(8,128)(2,1)S(1)} %copy-done.47, ...), kind=kOutput, calls=%fused_computation.9 | convolution fusion | flops 6524235776 | bytes 28868608 | tf_op jit(solution)/shard_map/dot_general | solution.py:46
  1126.3 12.8 multiply_reduce_fusion
  1144.6 23.2 %shard_map.301 = (bf16[768,1024]{1,0:T(8,128)(2,1)S(1)}, bf16[768,2048]{1,0:T(8,128)(2,1)}, bf16[768,2048]{1,0:T(8,128)(2,1)}) custom-call(s32[6]{0:T(128)S(1)} %get-tuple-element.73.has_far, bf16[768,1024]{1,0:T(8,128)(2,1)S(1)} %add_convert_fusion.11.q_ref, bf16[768,2048]{1,0:T(8,128)(2,1)} %add_convert_fusion.1.own_ref, ...), custom_call_target="tpu_custom_call" | custom-call | flops 1610612736 | bytes 12582912 | tf_op jit(solution)/shard_map/pallas_call | solution.py:126
  1190.0 11.3 add_convert_fusion.8
  1296.5 9.7 collective-permute-done.49
  1333.2 9.6 collective-permute-done.31
  1345.5 8.9 shard_map.302
  1405.8 18.2 %collective-permute-done.68 = bf16[2,128,2048]{2,1,0:T(8,128)(2,1)} collective-permute-done((bf16[2,128,2048]{2,1,0:T(8,128)(2,1)}, bf16[2,128,2048]{2,1,0:T(8,128)(2,1)}, u32[]{:S(2)}, u32[]{:S(2)}) %collective-permute-start.68) | collective-permute-done | bytes 1048608 | tf_op jit(solution)/shard_map/ppermute | solution.py:25
  1429.2 17.2 %collective-permute-done.77 = bf16[2,128,2048]{1,2,0:T(8,128)(2,1)} collective-permute-done((bf16[2,128,2048]{1,2,0:T(8,128)(2,1)}, bf16[2,128,2048]{1,2,0:T(8,128)(2,1)}, u32[]{:S(2)}, u32[]{:S(2)}) %collective-permute-start.77) | collective-permute-done | bytes 1048608 | tf_op jit(solution)/shard_map/ppermute | solution.py:25
  1451.4 19.9 %collective-permute-done.69 = bf16[128,2048]{1,0:T(8,128)(2,1)S(1)} collective-permute-done((bf16[128,2048]{1,0:T(8,128)(2,1)S(1)}, bf16[128,2048]{1,0:T(8,128)(2,1)S(1)}, u32[]{:S(2)}, u32[]{:S(2)}) %collective-permute-start.69) | collective-permute-done | bytes 524320 | tf_op jit(solution)/shard_map/ppermute | solution.py:25
  1519.1 14.6 collective-permute-done.46
  1538.7 26.9 %collective-permute-done.47 = f32[16,1024]{1,0:T(8,128)S(1)} collective-permute-done((f32[16,1024]{1,0:T(8,128)S(1)}, f32[16,1024]{1,0:T(8,128)S(1)}, u32[]{:S(2)}, u32[]{:S(2)}) %collective-permute-start.47) | collective-permute-done | bytes 65568 | tf_op jit(solution)/shard_map/ppermute | solution.py:25
  (606 shorter events, 433.6 us)
Async XLA Ops:
  44.6 83.5 %collective-permute-start = (bf16[240,1024]{1,0:T(8,128)(2,1)}, bf16[240,1024]{1,0:T(8,128)(2,1)S(1)}, u32[]{:S(2)}, u32[]{:S(2)}) collective-permute-start(bf16[240,1024]{1,0:T(8,128)(2,1)} %get-tuple-element.99), channel_id=1, source_target_pairs={{0,2},{1,3},{2,0},{3,1},{4,6},{5,7},{6,4},{7,5},{8,10},{9,11},{10,... | collective-permute-start | bytes 1474568 | tf_op jit(solution)/shard_map/ppermute | solution.py:354
  45.7 82.6 %collective-permute-start.1 = (bf16[240,1024]{1,0:T(8,128)(2,1)}, bf16[240,1024]{1,0:T(8,128)(2,1)S(1)}, u32[]{:S(2)}, u32[]{:S(2)}) collective-permute-start(bf16[240,1024]{1,0:T(8,128)(2,1)} %get-tuple-element.98), channel_id=1, source_target_pairs={{0,1},{1,2},{2,3},{3,0},{4,5},{5,6},{6,7},{7,4},{8,9},{9,10},{10,1... | collective-permute-start | bytes 1474568 | tf_op jit(solution)/shard_map/ppermute | solution.py:354
  66.5 63.4 %collective-permute-start.2 = (bf16[240,1024]{1,0:T(8,128)(2,1)S(1)}, bf16[240,1024]{1,0:T(8,128)(2,1)S(1)}, u32[]{:S(2)}, u32[]{:S(2)}) collective-permute-start(bf16[240,1024]{1,0:T(8,128)(2,1)S(1)} %get-tuple-element.97), channel_id=1, source_target_pairs={{0,3},{1,0},{2,1},{3,2},{4,7},{5,4},{6,5},{7,6},{8,11},{9,8},{10,9... | collective-permute-start | bytes 1474568 | tf_op jit(solution)/shard_map/ppermute | solution.py:354
  77.7 74.1 %collective-permute-start.22 = (bf16[128,2048]{1,0:T(8,128)(2,1)}, bf16[128,2048]{1,0:T(8,128)(2,1)}, u32[]{:S(2)}, u32[]{:S(2)}) collective-permute-start(bf16[128,2048]{1,0:T(8,128)(2,1)} %pad_maximum_fusion.27), channel_id=1, source_target_pairs={{3,0},{0,1},{1,2},{2,3},{7,4},{4,5},{5,6},{6,7},{11,8},{8,9},{9,10... | collective-permute-start | bytes 1572872 | tf_op jit(solution)/shard_map/ppermute | solution.py:213
  83.3 70.1 %collective-permute-start.21 = (bf16[128,2048]{1,0:T(8,128)(2,1)}, bf16[128,2048]{1,0:T(8,128)(2,1)}, u32[]{:S(2)}, u32[]{:S(2)}) collective-permute-start(bf16[128,2048]{1,0:T(8,128)(2,1)} %pad_maximum_fusion.27), channel_id=1, source_target_pairs={{2,0},{3,1},{0,2},{1,3},{6,4},{7,5},{4,6},{5,7},{10,8},{11,9},{8,1... | collective-permute-start | bytes 1572872 | tf_op jit(solution)/shard_map/ppermute | solution.py:213
  169.9 82.1 %collective-permute-start.16 = (bf16[12,128,512]{2,1,0:T(8,128)(2,1)S(1)}, bf16[12,128,512]{2,1,0:T(8,128)(2,1)S(1)}, u32[]{:S(2)}, u32[]{:S(2)}) collective-permute-start(bf16[12,128,512]{2,1,0:T(8,128)(2,1)S(1)} %pad_maximum_fusion.7), channel_id=1, source_target_pairs={{0,16},{4,20},{8,24},{12,28},{16,0},{20,4},{24,8},{28,12},{1,17},{... | collective-permute-start | bytes 4718600 | tf_op jit(solution)/shard_map/ppermute | solution.py:25
  172.8 75.3 %collective-permute-start.7 = (bf16[2,3,64,1024]{3,2,1,0:T(8,128)(2,1)S(1)}, bf16[2,3,64,1024]{3,2,1,0:T(8,128)(2,1)S(1)}, u32[]{:S(2)}, u32[]{:S(2)}) collective-permute-start(bf16[2,3,64,1024]{3,2,1,0:T(8,128)(2,1)S(1)} %pad_maximum_fusion.25), channel_id=1, source_target_pairs={{0,16},{4,20},{8,24},{12,28},{16,0},{20,4},{24,8},{28,12},{1,17},{... | collective-permute-start | bytes 2359304 | tf_op jit(solution)/shard_map/ppermute | solution.py:25
  180.7 69.7 %collective-permute-start.9 = (bf16[2,3,64,1024]{3,2,1,0:T(8,128)(2,1)S(1)}, bf16[2,3,64,1024]{3,2,1,0:T(8,128)(2,1)S(1)}, u32[]{:S(2)}, u32[]{:S(2)}) collective-permute-start(bf16[2,3,64,1024]{3,2,1,0:T(8,128)(2,1)S(1)} %pad_maximum_fusion.26), channel_id=1, source_target_pairs={{0,8},{4,12},{8,0},{12,4},{16,24},{20,28},{24,16},{28,20},{1,9},{5... | collective-permute-start | bytes 2359304 | tf_op jit(solution)/shard_map/ppermute | solution.py:25
  185.1 73.6 %collective-permute-start.18 = (bf16[12,128,512]{2,1,0:T(8,128)(2,1)S(1)}, bf16[12,128,512]{2,1,0:T(8,128)(2,1)S(1)}, u32[]{:S(2)}, u32[]{:S(2)}) collective-permute-start(bf16[12,128,512]{2,1,0:T(8,128)(2,1)S(1)} %pad_maximum_fusion.8), channel_id=1, source_target_pairs={{0,8},{4,12},{8,0},{12,4},{16,24},{20,28},{24,16},{28,20},{1,9},{5... | collective-permute-start | bytes 4718600 | tf_op jit(solution)/shard_map/ppermute | solution.py:25
  197.6 83.0 %collective-permute-start.24 = (bf16[2,3,64,2048]{3,2,1,0:T(8,128)(2,1)}, bf16[2,3,64,2048]{3,2,1,0:T(8,128)(2,1)}, u32[]{:S(2)}, u32[]{:S(2)}) collective-permute-start(bf16[2,3,64,2048]{3,2,1,0:T(8,128)(2,1)} %pad_maximum_fusion.10), channel_id=1, source_target_pairs={{0,16},{4,20},{8,24},{12,28},{16,0},{20,4},{24,8},{28,12},{1,17},{... | collective-permute-start | bytes 4718600 | tf_op jit(solution)/shard_map/ppermute | solution.py:25
  272.9 280.5 %collective-permute-start.19 = (bf16[6,128,1024]{2,1,0:T(8,128)(2,1)}, bf16[6,128,1024]{2,1,0:T(8,128)(2,1)}, u32[]{:S(2)}, u32[]{:S(2)}) collective-permute-start(bf16[6,128,1024]{2,1,0:T(8,128)(2,1)} %slice.562), channel_id=1, source_target_pairs={{0,4},{4,0},{8,12},{12,8},{16,20},{20,16},{24,28},{28,24},{1,5},{5... | collective-permute-start | bytes 4718600 | tf_op jit(solution)/shard_map/ppermute | solution.py:25
  283.9 296.3 %collective-permute-start.27 = (bf16[4,3,64,2048]{3,2,1,0:T(8,128)(2,1)}, bf16[4,3,64,2048]{3,2,1,0:T(8,128)(2,1)}, u32[]{:S(2)}, u32[]{:S(2)}) collective-permute-start(bf16[4,3,64,2048]{3,2,1,0:T(8,128)(2,1)} %pad_maximum_fusion.2.refs_0_), channel_id=1, source_target_pairs={{0,4},{4,0},{8,12},{12,8},{16,20},{20,16},{24,28},{28,24},{1,5},{5... | collective-permute-start | bytes 9437192 | tf_op jit(solution)/shard_map/ppermute | solution.py:25
  287.4 292.9 %collective-permute-start.28 = (bf16[4,3,64,2048]{3,2,1,0:T(8,128)(2,1)}, bf16[4,3,64,2048]{3,2,1,0:T(8,128)(2,1)}, u32[]{:S(2)}, u32[]{:S(2)}) collective-permute-start(bf16[4,3,64,2048]{3,2,1,0:T(8,128)(2,1)} %pad_maximum_fusion.3.refs_1_), channel_id=1, source_target_pairs={{0,4},{4,0},{8,12},{12,8},{16,20},{20,16},{24,28},{28,24},{1,5},{5... | collective-permute-start | bytes 9437192 | tf_op jit(solution)/shard_map/ppermute | solution.py:25
  1202.5 126.8 %collective-permute-start.29 = (bf16[192,1024]{1,0:T(8,128)(2,1)}, bf16[192,1024]{1,0:T(8,128)(2,1)S(1)}, u32[]{:S(2)}, u32[]{:S(2)}) collective-permute-start(bf16[192,1024]{1,0:T(8,128)(2,1)} %get-tuple-element.113), channel_id=1, source_target_pairs={{2,0},{3,1},{0,2},{1,3},{6,4},{7,5},{4,6},{5,7},{10,8},{11,9},{8,1... | collective-permute-start | bytes 1179656 | tf_op jit(solution)/shard_map/ppermute | solution.py:354
  1211.1 118.2 %collective-permute-start.30 = (bf16[192,1024]{1,0:T(8,128)(2,1)}, bf16[192,1024]{1,0:T(8,128)(2,1)}, u32[]{:S(2)}, u32[]{:S(2)}) collective-permute-start(bf16[192,1024]{1,0:T(8,128)(2,1)} %get-tuple-element.112), channel_id=1, source_target_pairs={{1,0},{2,1},{3,2},{0,3},{5,4},{6,5},{7,6},{4,7},{9,8},{10,9},{11,1... | collective-permute-start | bytes 1179656 | tf_op jit(solution)/shard_map/ppermute | solution.py:354
  1219.3 123.5 %collective-permute-start.35 = (bf16[6,128,1024]{2,1,0:T(8,128)(2,1)}, bf16[6,128,1024]{2,1,0:T(8,128)(2,1)}, u32[]{:S(2)}, u32[]{:S(2)}) collective-permute-start(bf16[6,128,1024]{2,1,0:T(8,128)(2,1)} %bitcast.43.mine_ref), channel_id=1, source_target_pairs={{0,4},{4,0},{8,12},{12,8},{16,20},{20,16},{24,28},{28,24},{1,5},{5... | collective-permute-start | bytes 4718600 | tf_op jit(solution)/shard_map/ppermute | solution.py:25
  1311.9 52.1 %collective-permute-start.67 = (bf16[512,2048]{1,0:T(8,128)(2,1)}, bf16[512,2048]{1,0:T(8,128)(2,1)}, u32[]{:S(2)}, u32[]{:S(2)}) collective-permute-start(bf16[512,2048]{1,0:T(8,128)(2,1)} %convolution_convert_fusion.2), channel_id=1, source_target_pairs={{0,4},{4,0},{8,12},{12,8},{16,20},{20,16},{24,28},{28,24},{1,5},{5... | collective-permute-start | bytes 6291464 | tf_op jit(solution)/shard_map/ppermute | solution.py:25
  1371.6 52.4 %collective-permute-start.68 = (bf16[2,128,2048]{2,1,0:T(8,128)(2,1)}, bf16[2,128,2048]{2,1,0:T(8,128)(2,1)}, u32[]{:S(2)}, u32[]{:S(2)}) collective-permute-start(bf16[2,128,2048]{2,1,0:T(8,128)(2,1)} %bitcast.88), channel_id=1, source_target_pairs={{0,16},{4,20},{8,24},{12,28},{16,0},{20,4},{24,8},{28,12},{1,17},{... | collective-permute-start | bytes 3145736 | tf_op jit(solution)/shard_map/ppermute | solution.py:25
  1378.1 48.1 %collective-permute-start.64 = (bf16[2,128,2048]{2,1,0:T(8,128)(2,1)}, bf16[2,128,2048]{2,1,0:T(8,128)(2,1)}, u32[]{:S(2)}, u32[]{:S(2)}) collective-permute-start(bf16[2,128,2048]{2,1,0:T(8,128)(2,1)} %slice_bitcast_fusion), channel_id=1, source_target_pairs={{0,8},{4,12},{8,0},{12,4},{16,24},{20,28},{24,16},{28,20},{1,9},{5... | collective-permute-start | bytes 3145736 | tf_op jit(solution)/shard_map/ppermute | solution.py:25
  1387.5 59.0 %collective-permute-start.77 = (bf16[2,128,2048]{1,2,0:T(8,128)(2,1)}, bf16[2,128,2048]{1,2,0:T(8,128)(2,1)}, u32[]{:S(2)}, u32[]{:S(2)}) collective-permute-start(bf16[2,128,2048]{1,2,0:T(8,128)(2,1)} %copy.50), channel_id=1, source_target_pairs={{0,16},{4,20},{8,24},{12,28},{16,0},{20,4},{24,8},{28,12},{1,17},{... | collective-permute-start | bytes 3145736 | tf_op jit(solution)/shard_map/ppermute | solution.py:25
  1398.4 51.1 %collective-permute-start.73 = (bf16[2,128,2048]{1,2,0:T(8,128)(2,1)}, bf16[2,128,2048]{1,2,0:T(8,128)(2,1)S(1)}, u32[]{:S(2)}, u32[]{:S(2)}) collective-permute-start(bf16[2,128,2048]{1,2,0:T(8,128)(2,1)} %bitcast.357), channel_id=1, source_target_pairs={{0,8},{4,12},{8,0},{12,4},{16,24},{20,28},{24,16},{28,20},{1,9},{5... | collective-permute-start | bytes 3145736 | tf_op jit(solution)/shard_map/ppermute | solution.py:25
  1402.2 81.0 %collective-permute-start.39 = (bf16[6,128,512]{2,1,0:T(8,128)(2,1)S(1)}, bf16[6,128,512]{2,1,0:T(8,128)(2,1)S(1)}, u32[]{:S(2)}, u32[]{:S(2)}) collective-permute-start(bf16[6,128,512]{2,1,0:T(8,128)(2,1)S(1)} %slice.571), channel_id=1, source_target_pairs={{0,16},{4,20},{8,24},{12,28},{16,0},{20,4},{24,8},{28,12},{1,17},{... | collective-permute-start | bytes 2359304 | tf_op jit(solution)/shard_map/ppermute | solution.py:25
  1424.0 60.8 %collective-permute-start.37 = (bf16[6,128,512]{2,1,0:T(8,128)(2,1)S(1)}, bf16[6,128,512]{2,1,0:T(8,128)(2,1)S(1)}, u32[]{:S(2)}, u32[]{:S(2)}) collective-permute-start(bf16[6,128,512]{2,1,0:T(8,128)(2,1)S(1)} %slice.569), channel_id=1, source_target_pairs={{0,8},{4,12},{8,0},{12,4},{16,24},{20,28},{24,16},{28,20},{1,9},{5... | collective-permute-start | bytes 2359304 | tf_op jit(solution)/shard_map/ppermute | solution.py:25
  1513.3 54.8 %collective-permute-start.40 = (bf16[192,1024]{1,0:T(8,128)(2,1)S(1)}, bf16[192,1024]{1,0:T(8,128)(2,1)S(1)}, u32[]{:S(2)}, u32[]{:S(2)}) collective-permute-start(bf16[192,1024]{1,0:T(8,128)(2,1)S(1)} %get-tuple-element.107), channel_id=1, source_target_pairs={{2,0},{3,1},{0,2},{1,3},{6,4},{7,5},{4,6},{5,7},{10,8},{11,9},{8,1... | collective-permute-start | bytes 1179656 | tf_op jit(solution)/shard_map/ppermute | solution.py:354
  (169 other events, 5203.6 us)

commit v2 on v1

--- a/solution.py
+++ b/solution.py
@@ -228,58 +228,65 @@
     return [sum(m for bit, m in enumerate(masks) if k >> bit & 1) for k in range(1 << len(masks))]
 
 
-def assemble_kernel(copies, n_in, dp_index, *refs):
-    ins, outs, sem = refs[:n_in], refs[n_in:-1], refs[-1]
-    me = dp_index[0]
-    started = []
-    for which, index, target, row_xor, half, c0, width, t0 in copies:
-        src = ins[which]
-        for at in index:
-            src = src.at[at]
-        if c0 is not None:
-            src = src.at[:, pl.ds(c0, width)]
-        dst = outs[target]
-        if row_xor is not None:
-            rows = src.shape[0]
-            dst = dst.at[pl.ds(pl.multiple_of((me ^ row_xor) * 2 * rows + half * rows, rows), rows)]
-        dst = dst.at[:, pl.ds(t0, width)]
-        copy = pltpu.make_async_copy(src, dst, sem.at[len(started)])
-        copy.start()
-        started.append(copy)
-    for copy in started:
-        copy.wait()
-
-
-def assemble(dp_index, ins, copies, shapes):
+def assemble_kernel(columns, n_own, n_out, dp_index, *refs):
+    tables, own, outs = refs[:4], refs[4 : 4 + n_own], refs[4 + n_own :]
+    slots, half = tables[0].shape[1], tables[0].shape[2]
+
+    def fill(first, second):
+        for color, table in enumerate((first, second)):
+            rows = slice(color * half, (color + 1) * half)
+            for c0, width, target, t0 in columns:
+                for s in range(slots):
+                    at = t0 + (s + 1) * width
+                    outs[target][rows, at : at + width] = table[0, s, :, c0 : c0 + width]
+
+    core = pl.program_id(0)
+
+    @pl.when(core == 0)
+    def _():
+        fill(tables[0], tables[1])
+
+    @pl.when(core == 1)
+    def _():
+        fill(tables[2], tables[3])
+
+    for ref, (c0, width, target, t0) in zip(own, columns):
+        outs[target][:, t0 : t0 + width] = ref[...]
+
+
+def assemble(dp_index, tables, own, columns, masks, widths):
+    bits = len(masks)
+    count, slots, half, width = tables[0].shape
+    model = 2 * count * 2 * half
+
+    def reverse(k):
+        return sum(((k >> i) & 1) << (bits - 1 - i) for i in range(bits))
+
+    def table_spec(which):
+        def index(core, k, dp):
+            k = jnp.where(core == which // 2, k, 0 if which >= 2 else count - 1)
+            return (reverse(k) if which % 2 else k, 0, 0, 0)
+
+        return pl.BlockSpec((1, slots, half, width), index)
+
+    def row(core, k, dp):
+        return (dp[0] ^ ((k << 1) | core), 0)
+
     return pl.pallas_call(
-        functools.partial(assemble_kernel, copies, len(ins)),
+        functools.partial(assemble_kernel, columns, len(own), len(widths)),
         grid_spec=pltpu.PrefetchScalarGridSpec(
             num_scalar_prefetch=1,
-            grid=(1,),
-            in_specs=[ANY] * len(ins),
-            out_specs=[ANY] * len(shapes),
-            scratch_shapes=[pltpu.SemaphoreType.DMA((len(copies),))],
-        ),
-        out_shape=[jax.ShapeDtypeStruct(s, bf16) for s in shapes],
+            grid=(2, count),
+            in_specs=[table_spec(i) for i in range(4)]
+            + [pl.BlockSpec((2 * half, o.shape[1]), row) for o in own],
+            out_specs=[pl.BlockSpec((2 * half, w), row) for w in widths],
+        ),
+        out_shape=[jax.ShapeDtypeStruct((model, w), bf16) for w in widths],
+        compiler_params=pltpu.CompilerParams(vmem_limit_bytes=48 << 20),
         cost_estimate=pl.CostEstimate(
-            flops=0,
-            bytes_accessed=sum(4 * math.prod(s) for s in shapes),
-            transcendentals=0,
-        ),
-    )(dp_index, *ins)
-
-
-def strip_copies(masks, slots, columns):
-    out = []
-    for which in range(4):
-        order = masks if which % 2 == 0 else masks[::-1]
-        for k, mask in enumerate(relative_masks(order)):
-            for s in range(slots):
-                for c0, width, target, place in columns:
-                    out.append(
-                        (which, (k, s), target, mask | (which // 2), which % 2, c0, width, place(s + 1))
-                    )
-    return out
+            flops=0, bytes_accessed=4 * model * sum(widths), transcendentals=0
+        ),
+    )(dp_index, *tables, *own)
 
 
 def reduce_over_dp(left, right, masks, color):
@@ -340,7 +347,6 @@
     blocks = tokens // BLOCK
     slab = model // dp_size
     masks = [1 << i for i in range(1, dp_size.bit_length() - 1)]
-    remote = head_size - 1
     heads_all, hidden_all = head_cols * head_size, hidden_cols * head_size
 
     src_rank = here % micro
@@ -393,31 +399,22 @@
     dp_index = me.reshape(1).astype(jnp.int32)
     hc, fc = head_cols, hidden_cols
     got_a = gather_strips(strip_a, masks)
-    own_a = [(4, (t,), 0 if t == 0 else 1, None, 0, 0, hc, (t == 2) * heads_all) for t in range(3)]
-    own_a += [(5, (), 2, None, 0, 0, hc, 0)]
     w_query, w_kv, w_out_t = assemble(
         dp_index,
-        got_a + [w_qkv, w_out.T],
-        strip_copies(
-            masks,
-            remote,
-            [
-                (0, hc, 0, lambda s: s * hc),
-                (hc, hc, 1, lambda s: s * hc),
-                (2 * hc, hc, 1, lambda s: heads_all + s * hc),
-                (3 * hc, hc, 2, lambda s: s * hc),
-            ],
-        )
-        + own_a,
-        [(model, heads_all), (model, 2 * heads_all), (model, heads_all)],
+        got_a,
+        [w_qkv[0], w_qkv[1], w_qkv[2], w_out.T],
+        [(0, hc, 0, 0), (hc, hc, 1, 0), (2 * hc, hc, 1, heads_all), (3 * hc, hc, 2, 0)],
+        masks,
+        [heads_all, 2 * heads_all, heads_all],
     )
     got_f = gather_strips(strip_f, masks)
     w_one, w_two_t = assemble(
         dp_index,
-        got_f + [w_fc1, w_fc2.T],
-        strip_copies(masks, remote, [(0, fc, 0, lambda s: s * fc), (fc, fc, 1, lambda s: s * fc)])
-        + [(4, (), 0, None, 0, 0, fc, 0), (5, (), 1, None, 0, 0, fc, 0)],
-        [(model, hidden_all), (model, hidden_all)],
+        got_f,
+        [w_fc1, w_fc2.T],
+        [(0, fc, 0, 0), (fc, fc, 1, 0)],
+        masks,
+        [hidden_all, hidden_all],
     )
     small = jnp.concatenate([b_qv.reshape(-1), b_fc1])
     biases = [small] + [

time: 1580 us -> 847 us (0.54)
  Pallas kernels: 820 us -> 75.1 us
    pallas_call x2, Pallas kernels: 767 us -> 23.1 us  [assemble(): pl.pallas_call(functools.partial(assemble_kernel, columns, len(own), len(...]
    unnamed x254 -> x260, local copies, waits for them, and re-layouts: 35.7 us -> 32.9 us
  transfers between devices with their start and end apart: 81 -> 81, of which waited for: 29 -> 30; matrix products, arithmetic and copies ran while one was open for 14% -> 27% of each run, Pallas kernels for 18% -> 5%
where the time goes in v2:
time: 847 us; the launch traced here: 841 us
  waiting for transfers between devices  301 us (36%)
  matrix products  167 us (20%)
  starting transfers between devices  121 us (14%)
  local copies, waits for them, and re-layouts  98.1 us (12%)
  other arithmetic  76.1 us (9%)
  Pallas kernels  75.1 us (9%)
    ppermute x51, waiting for transfers between devices, xor_swap(): return lax.ppermute(value, axis, [(i, i ^ mask) for i in range(size)])  233 us
    dot_general x11, matrix products, mm(): return jnp.dot(left, right, preferred_element_type=f32)  67.4 us
    ppermute x12, waiting for transfers between devices, send(): lax.ppermute(value, 'head', pairs)  62.1 us
    dot_general x16, matrix products, mm_tn(): lax.dot_general(left, right, (((0,), (0,)), ((), ())), preferred_element_...  55.6 us
    ppermute x51, starting transfers between devices, xor_swap(): return lax.ppermute(value, axis, [(i, i ^ mask) for i in range(size)])  46.4 us
    dot_general x6, matrix products, mm_nt(): lax.dot_general(left, right, (((1,), (1,)), ((), ())), preferred_element_...  43.9 us
    pallas_call x2, Pallas kernels, attention_call(): pl.pallas_call(functools.partial(kernel, width // PAIR), grid_spec=pltpu....  34.2 us
    unnamed x260, local copies, waits for them, and re-layouts  32.9 us
  transfers between devices with their start and end apart: 81, of which 30 were waited for; matrix products, arithmetic and copies ran while one was open for 27% of the time, Pallas kernels for 5%

profile of v2, /device:TPU:0, one launch (start us, length us, event | category | flops | bytes accessed | tf_op | source)
XLA Modules:
  0.0 840.8 jit_solution(9709486694892540016)
XLA Ops:
  44.4 21.4 %collective-permute-done.32 = bf16[192,1024]{1,0:T(8,128)(2,1)S(1)} collective-permute-done((bf16[192,1024]{1,0:T(8,128)(2,1)}, bf16[192,1024]{1,0:T(8,128)(2,1)S(1)}, u32[]{:S(2)}, u32[]{:S(2)}) %collective-permute-start.32) | collective-permute-done | bytes 393248 | tf_op jit(solution)/shard_map/ppermute | solution.py:360
  65.8 10.4 %collective-permute-start.2 = (bf16[240,1024]{1,0:T(8,128)(2,1)}, bf16[240,1024]{1,0:T(8,128)(2,1)S(1)}, u32[]{:S(2)}, u32[]{:S(2)}) collective-permute-start(bf16[240,1024]{1,0:T(8,128)(2,1)} %get-tuple-element.97), channel_id=1, source_target_pairs={{0,3},{1,0},{2,1},{3,2},{4,7},{5,4},{6,5},{7,6},{8,11},{9,8},{10,9... | collective-permute-start | bytes 1474568 | tf_op jit(solution)/shard_map/ppermute | solution.py:360
  82.6 11.4 %collective-permute-start.21 = (bf16[128,2048]{1,0:T(8,128)(2,1)}, bf16[128,2048]{1,0:T(8,128)(2,1)}, u32[]{:S(2)}, u32[]{:S(2)}) collective-permute-start(bf16[128,2048]{1,0:T(8,128)(2,1)} %pad_maximum_fusion.27), channel_id=1, source_target_pairs={{2,0},{3,1},{0,2},{1,3},{6,4},{7,5},{4,6},{5,7},{10,8},{11,9},{8,1... | collective-permute-start | bytes 1572872 | tf_op jit(solution)/shard_map/ppermute | solution.py:213
  96.3 31.1 %collective-permute-done = bf16[240,1024]{1,0:T(8,128)(2,1)S(1)} collective-permute-done((bf16[240,1024]{1,0:T(8,128)(2,1)}, bf16[240,1024]{1,0:T(8,128)(2,1)S(1)}, u32[]{:S(2)}, u32[]{:S(2)}) %collective-permute-start) | collective-permute-done | bytes 491552 | tf_op jit(solution)/shard_map/ppermute | solution.py:360
  161.9 11.6 %collective-permute-done.15 = bf16[6,128,512]{2,1,0:T(8,128)(2,1)S(1)} collective-permute-done((bf16[6,128,512]{2,1,0:T(8,128)(2,1)S(1)}, bf16[6,128,512]{2,1,0:T(8,128)(2,1)S(1)}, u32[]{:S(2)}, u32[]{:S(2)}) %collective-permute-start.15) | collective-permute-done | bytes 786464 | tf_op jit(solution)/shard_map/ppermute | solution.py:25
  192.2 10.8 %collective-permute-done.25 = bf16[1,3,64,2048]{3,2,1,0:T(8,128)(2,1)S(1)} collective-permute-done((bf16[1,3,64,2048]{3,2,1,0:T(8,128)(2,1)S(1)}, bf16[1,3,64,2048]{3,2,1,0:T(8,128)(2,1)S(1)}, u32[]{:S(2)}, u32[]{:S(2)}) %collective-permute-start.25) | collective-permute-done | bytes 786464 | tf_op jit(solution)/shard_map/ppermute | solution.py:25
  205.8 47.7 %collective-permute-done.7 = bf16[2,3,64,1024]{3,2,1,0:T(8,128)(2,1)S(1)} collective-permute-done((bf16[2,3,64,1024]{3,2,1,0:T(8,128)(2,1)S(1)}, bf16[2,3,64,1024]{3,2,1,0:T(8,128)(2,1)S(1)}, u32[]{:S(2)}, u32[]{:S(2)}) %collective-permute-start.7) | collective-permute-done | bytes 786464 | tf_op jit(solution)/shard_map/ppermute | solution.py:25
  290.9 9.9 %shard_map.297 = (bf16[1024,1024]{1,0:T(8,128)(2,1)}, bf16[1024,2048]{1,0:T(8,128)(2,1)}, bf16[1024,1024]{1,0:T(8,128)(2,1)}) custom-call(s32[1]{0:T(128)} %bitcast.5.dp_index, bf16[4,3,64,1024]{3,2,1,0:T(8,128)(2,1)} %pad_maximum_fusion.5.refs_0_, bf16[4,3,64,1024]{3,2,1,0:T(8,128)(2,1)} %pad_maximum_fusion.6.refs_1_, ...), custom_call_target="tpu_custom_call" | custom-call | bytes 16777216 | tf_op jit(solution)/shard_map/pallas_call | solution.py:275
  316.3 11.1 %shard_map.299 = bf16[768,1024]{1,0:T(8,128)(2,1)S(1)} custom-call(s32[6]{0:T(128)S(1)} %get-tuple-element.73.has_far, bf16[768,1024]{1,0:T(8,128)(2,1)S(1)} %add_convert_fusion.11.q_ref, bf16[768,2048]{1,0:T(8,128)(2,1)} %add_convert_fusion.1.own_ref, bf16[768,2048]{1,0:T(8,128)(2,1)} %add_convert_fusion.far_ref), custom_call_target="tpu_custom_call" | custom-call | flops 1610612736 | bytes 12582912 | tf_op jit(solution)/shard_map/pallas_call | solution.py:126
  340.3 13.2 %shard_map.300 = (bf16[1024,4096]{1,0:T(8,128)(2,1)}, bf16[1024,4096]{1,0:T(8,128)(2,1)}) custom-call(s32[1]{0:T(128)} %bitcast.5.dp_index, bf16[4,3,64,2048]{3,2,1,0:T(8,128)(2,1)} %copy-done.12, bf16[4,3,64,2048]{3,2,1,0:T(8,128)(2,1)} %copy-done.13, bf16[4,3,64,2048]{3,2,1,0:T(8,128)(2,1)} %collective-permute-done.27.refs_2_, ...), custom_call_target="tpu_custom_call" | custom-call | bytes 33554432 | tf_op jit(solution)/shard_map/pallas_call | solution.py:275
  353.5 16.8 %multiply_convert_fusion.1 = (bf16[768,4096]{1,0:T(8,128)(2,1)}, f32[768,4096]{1,0:T(8,128)}) fusion(f32[4096]{0:T(1024)S(1)} %copy-done.81, bf16[1024,4096]{1,0:T(8,128)(2,1)} %get-tuple-element.30, f32[768,1024]{1,0:T(8,128)S(1)} %copy-done.16, f32[1024]{0:T(1024)S(1)} %copy-done.100, f32[1024]{0:T(1024)S(1)} %copy-done.86, f32[768]{0:T(1024)S(1)} %add_rsqrt_fusion, ...), kind=kOutput, calls=%fused_computation.11 | convolution fusion | flops 6477840384 | bytes 30439424 | tf_op jit(solution)/shard_map/dot_general | solution.py:46
  370.4 22.3 %convert_reduce_fusion = (f32[4096]{0:T(1024)}, bf16[768,4096]{1,0:T(8,128)(2,1)}) fusion(f32[768,4096]{1,0:T(8,128)} %get-tuple-element.181, f32[4096]{0:T(1024)S(1)} %copy-done.81, bf16[1024,4096]{1,0:T(8,128)(2,1)} %get-tuple-element.31, bf16[192,1024]{1,0:T(8,128)(2,1)S(1)} %copy-done.51, bf16[192,1024]{1,0:T(8,128)(2,1)S(1)} %copy-done.53, ...), kind=kOutput, calls=%fused_computation.9 | convolution fusion | flops 6524235776 | bytes 28868608 | tf_op jit(solution)/shard_map/dot_general | solution.py:46
  392.6 12.4 %multiply_reduce_fusion = (f32[1024]{0:T(1024)}, f32[768]{0:T(1024)S(1)}, f32[768]{0:T(1024)S(1)}, f32[1024]{0:T(1024)}, f32[768,1024]{1,0:T(8,128)S(1)}) fusion(f32[768,1024]{1,0:T(8,128)S(1)} %copy-done.16, f32[768]{0:T(1024)S(1)} %add_rsqrt_fusion, f32[768]{0:T(1024)S(1)} %broadcast_multiply_fusion.5, f32[1024]{0:T(1024)S(1)} %copy-done.86, ...), kind=kOutput, calls=%fused_computation.33 | convolution fusion | flops 6449524736 | bytes 20996096 | tf_op jit(solution)/shard_map/dot_general | solution.py:50
  410.1 23.1 %shard_map.301 = (bf16[768,1024]{1,0:T(8,128)(2,1)S(1)}, bf16[768,2048]{1,0:T(8,128)(2,1)}, bf16[768,2048]{1,0:T(8,128)(2,1)}) custom-call(s32[6]{0:T(128)S(1)} %get-tuple-element.73.has_far, bf16[768,1024]{1,0:T(8,128)(2,1)S(1)} %add_convert_fusion.11.q_ref, bf16[768,2048]{1,0:T(8,128)(2,1)} %add_convert_fusion.1.own_ref, ...), custom_call_target="tpu_custom_call" | custom-call | flops 1610612736 | bytes 12582912 | tf_op jit(solution)/shard_map/pallas_call | solution.py:126
  455.3 11.6 %add_convert_fusion.8 = bf16[768,1024]{1,0:T(8,128)(2,1)S(1)} fusion(f32[768,1024]{1,0:T(8,128)S(1)} %copy-done.16, bf16[768,4096]{1,0:T(8,128)(2,1)} %get-tuple-element.180, bf16[1024,4096]{1,0:T(8,128)(2,1)} %get-tuple-element.31, f32[1024]{0:T(1024)S(1)} %copy-done.101), kind=kOutput, calls=%fused_computation.44 | convolution fusion | flops 6444810240 | bytes 19402752 | tf_op jit(solution)/shard_map/dot_general | solution.py:50
  468.0 9.1 %collective-permute-start.29 = (bf16[192,1024]{1,0:T(8,128)(2,1)}, bf16[192,1024]{1,0:T(8,128)(2,1)S(1)}, u32[]{:S(2)}, u32[]{:S(2)}) collective-permute-start(bf16[192,1024]{1,0:T(8,128)(2,1)} %get-tuple-element.113), channel_id=1, source_target_pairs={{2,0},{3,1},{0,2},{1,3},{6,4},{7,5},{4,6},{5,7},{10,8},{11,9},{8,1... | collective-permute-start | bytes 1179656 | tf_op jit(solution)/shard_map/ppermute | solution.py:360
  562.8 9.6 %collective-permute-done.49 = bf16[2,128,1024]{1,2,0:T(8,128)(2,1)S(1)} collective-permute-done((bf16[2,128,1024]{1,2,0:T(8,128)(2,1)}, bf16[2,128,1024]{1,2,0:T(8,128)(2,1)S(1)}, u32[]{:S(2)}, u32[]{:S(2)}) %collective-permute-start.49) | collective-permute-done | bytes 524320 | tf_op jit(solution)/shard_map/ppermute | solution.py:25
  599.3 9.6 %collective-permute-done.31 = bf16[192,1024]{1,0:T(8,128)(2,1)S(1)} collective-permute-done((bf16[192,1024]{1,0:T(8,128)(2,1)S(1)}, bf16[192,1024]{1,0:T(8,128)(2,1)S(1)}, u32[]{:S(2)}, u32[]{:S(2)}) %collective-permute-start.31) | collective-permute-done | bytes 393248 | tf_op jit(solution)/shard_map/ppermute | solution.py:360
  611.6 9.0 %shard_map.302 = (bf16[24,128,512]{2,1,0:T(8,128)(2,1)S(1)}, bf16[24,128,512]{2,1,0:T(8,128)(2,1)S(1)}) custom-call(s32[12]{0:T(128)S(1)} %get-tuple-element.69.where_a, s32[12]{0:T(128)S(1)} %get-tuple-element.65.where_b, bf16[6,128,1024]{2,1,0:T(8,128)(2,1)} %bitcast.46.mine_ref, bf16[6,128,1024]{2,1,0:T(8,128)(2,1)} %collective-permute-done.35.other_ref), custom_call_target="tpu_custom_call" | custom-call | bytes 6291456 | tf_op jit(solution)/shard_map/pallas_call | solution.py:192
  671.9 18.3 %collective-permute-done.68 = bf16[2,128,2048]{2,1,0:T(8,128)(2,1)} collective-permute-done((bf16[2,128,2048]{2,1,0:T(8,128)(2,1)}, bf16[2,128,2048]{2,1,0:T(8,128)(2,1)}, u32[]{:S(2)}, u32[]{:S(2)}) %collective-permute-start.68) | collective-permute-done | bytes 1048608 | tf_op jit(solution)/shard_map/ppermute | solution.py:25
  695.7 17.0 %collective-permute-done.77 = bf16[2,128,2048]{1,2,0:T(8,128)(2,1)} collective-permute-done((bf16[2,128,2048]{1,2,0:T(8,128)(2,1)}, bf16[2,128,2048]{1,2,0:T(8,128)(2,1)}, u32[]{:S(2)}, u32[]{:S(2)}) %collective-permute-start.77) | collective-permute-done | bytes 1048608 | tf_op jit(solution)/shard_map/ppermute | solution.py:25
  717.6 19.8 %collective-permute-done.69 = bf16[128,2048]{1,0:T(8,128)(2,1)S(1)} collective-permute-done((bf16[128,2048]{1,0:T(8,128)(2,1)S(1)}, bf16[128,2048]{1,0:T(8,128)(2,1)S(1)}, u32[]{:S(2)}, u32[]{:S(2)}) %collective-permute-start.69) | collective-permute-done | bytes 524320 | tf_op jit(solution)/shard_map/ppermute | solution.py:25
  785.5 14.5 %collective-permute-done.46 = f32[16,1024]{1,0:T(8,128)S(1)} collective-permute-done((f32[16,1024]{1,0:T(8,128)S(1)}, f32[16,1024]{1,0:T(8,128)S(1)}, u32[]{:S(2)}, u32[]{:S(2)}) %collective-permute-start.46) | collective-permute-done | bytes 65568 | tf_op jit(solution)/shard_map/ppermute | solution.py:25
  805.1 27.0 %collective-permute-done.47 = f32[16,1024]{1,0:T(8,128)S(1)} collective-permute-done((f32[16,1024]{1,0:T(8,128)S(1)}, f32[16,1024]{1,0:T(8,128)S(1)}, u32[]{:S(2)}, u32[]{:S(2)}) %collective-permute-start.47) | collective-permute-done | bytes 65568 | tf_op jit(solution)/shard_map/ppermute | solution.py:25
  (612 shorter events, 439.5 us)
Async XLA Ops:
  42.6 84.7 %collective-permute-start = (bf16[240,1024]{1,0:T(8,128)(2,1)}, bf16[240,1024]{1,0:T(8,128)(2,1)S(1)}, u32[]{:S(2)}, u32[]{:S(2)}) collective-permute-start(bf16[240,1024]{1,0:T(8,128)(2,1)} %get-tuple-element.99), channel_id=1, source_target_pairs={{0,2},{1,3},{2,0},{3,1},{4,6},{5,7},{6,4},{7,5},{8,10},{9,11},{10,... | collective-permute-start | bytes 1474568 | tf_op jit(solution)/shard_map/ppermute | solution.py:360
  42.6 84.7 %collective-permute-start.1 = (bf16[240,1024]{1,0:T(8,128)(2,1)}, bf16[240,1024]{1,0:T(8,128)(2,1)S(1)}, u32[]{:S(2)}, u32[]{:S(2)}) collective-permute-start(bf16[240,1024]{1,0:T(8,128)(2,1)} %get-tuple-element.98), channel_id=1, source_target_pairs={{0,1},{1,2},{2,3},{3,0},{4,5},{5,6},{6,7},{7,4},{8,9},{9,10},{10,1... | collective-permute-start | bytes 1474568 | tf_op jit(solution)/shard_map/ppermute | solution.py:360
  65.8 63.1 %collective-permute-start.2 = (bf16[240,1024]{1,0:T(8,128)(2,1)}, bf16[240,1024]{1,0:T(8,128)(2,1)S(1)}, u32[]{:S(2)}, u32[]{:S(2)}) collective-permute-start(bf16[240,1024]{1,0:T(8,128)(2,1)} %get-tuple-element.97), channel_id=1, source_target_pairs={{0,3},{1,0},{2,1},{3,2},{4,7},{5,4},{6,5},{7,6},{8,11},{9,8},{10,9... | collective-permute-start | bytes 1474568 | tf_op jit(solution)/shard_map/ppermute | solution.py:360
  77.1 80.1 %collective-permute-start.22 = (bf16[128,2048]{1,0:T(8,128)(2,1)}, bf16[128,2048]{1,0:T(8,128)(2,1)}, u32[]{:S(2)}, u32[]{:S(2)}) collective-permute-start(bf16[128,2048]{1,0:T(8,128)(2,1)} %pad_maximum_fusion.27), channel_id=1, source_target_pairs={{3,0},{0,1},{1,2},{2,3},{7,4},{4,5},{5,6},{6,7},{11,8},{8,9},{9,10... | collective-permute-start | bytes 1572872 | tf_op jit(solution)/shard_map/ppermute | solution.py:213
  82.6 76.1 %collective-permute-start.21 = (bf16[128,2048]{1,0:T(8,128)(2,1)}, bf16[128,2048]{1,0:T(8,128)(2,1)}, u32[]{:S(2)}, u32[]{:S(2)}) collective-permute-start(bf16[128,2048]{1,0:T(8,128)(2,1)} %pad_maximum_fusion.27), channel_id=1, source_target_pairs={{2,0},{3,1},{0,2},{1,3},{6,4},{7,5},{4,6},{5,7},{10,8},{11,9},{8,1... | collective-permute-start | bytes 1572872 | tf_op jit(solution)/shard_map/ppermute | solution.py:213
  127.3 47.9 %collective-permute-start.6 = (bf16[1,3,64,1024]{3,2,1,0:T(8,128)(2,1)}, bf16[1,3,64,1024]{3,2,1,0:T(8,128)(2,1)}, u32[]{:S(2)}, u32[]{:S(2)}) collective-permute-start(bf16[1,3,64,1024]{3,2,1,0:T(8,128)(2,1)} %get-tuple-element.133), channel_id=1, source_target_pairs={{0,8},{4,12},{8,0},{12,4},{16,24},{20,28},{24,16},{28,20},{1,9},{5... | collective-permute-start | bytes 1179656 | tf_op jit(solution)/shard_map/ppermute | solution.py:25
  175.2 83.1 %collective-permute-start.16 = (bf16[12,128,512]{2,1,0:T(8,128)(2,1)S(1)}, bf16[12,128,512]{2,1,0:T(8,128)(2,1)S(1)}, u32[]{:S(2)}, u32[]{:S(2)}) collective-permute-start(bf16[12,128,512]{2,1,0:T(8,128)(2,1)S(1)} %pad_maximum_fusion.7), channel_id=1, source_target_pairs={{0,16},{4,20},{8,24},{12,28},{16,0},{20,4},{24,8},{28,12},{1,17},{... | collective-permute-start | bytes 4718600 | tf_op jit(solution)/shard_map/ppermute | solution.py:25
  178.1 75.4 %collective-permute-start.7 = (bf16[2,3,64,1024]{3,2,1,0:T(8,128)(2,1)S(1)}, bf16[2,3,64,1024]{3,2,1,0:T(8,128)(2,1)S(1)}, u32[]{:S(2)}, u32[]{:S(2)}) collective-permute-start(bf16[2,3,64,1024]{3,2,1,0:T(8,128)(2,1)S(1)} %pad_maximum_fusion.25), channel_id=1, source_target_pairs={{0,16},{4,20},{8,24},{12,28},{16,0},{20,4},{24,8},{28,12},{1,17},{... | collective-permute-start | bytes 2359304 | tf_op jit(solution)/shard_map/ppermute | solution.py:25
  186.1 70.9 %collective-permute-start.9 = (bf16[2,3,64,1024]{3,2,1,0:T(8,128)(2,1)S(1)}, bf16[2,3,64,1024]{3,2,1,0:T(8,128)(2,1)S(1)}, u32[]{:S(2)}, u32[]{:S(2)}) collective-permute-start(bf16[2,3,64,1024]{3,2,1,0:T(8,128)(2,1)S(1)} %pad_maximum_fusion.26), channel_id=1, source_target_pairs={{0,8},{4,12},{8,0},{12,4},{16,24},{20,28},{24,16},{28,20},{1,9},{5... | collective-permute-start | bytes 2359304 | tf_op jit(solution)/shard_map/ppermute | solution.py:25
  190.4 74.7 %collective-permute-start.18 = (bf16[12,128,512]{2,1,0:T(8,128)(2,1)S(1)}, bf16[12,128,512]{2,1,0:T(8,128)(2,1)S(1)}, u32[]{:S(2)}, u32[]{:S(2)}) collective-permute-start(bf16[12,128,512]{2,1,0:T(8,128)(2,1)S(1)} %pad_maximum_fusion.8), channel_id=1, source_target_pairs={{0,8},{4,12},{8,0},{12,4},{16,24},{20,28},{24,16},{28,20},{1,9},{5... | collective-permute-start | bytes 4718600 | tf_op jit(solution)/shard_map/ppermute | solution.py:25
  203.0 83.0 %collective-permute-start.24 = (bf16[2,3,64,2048]{3,2,1,0:T(8,128)(2,1)}, bf16[2,3,64,2048]{3,2,1,0:T(8,128)(2,1)}, u32[]{:S(2)}, u32[]{:S(2)}) collective-permute-start(bf16[2,3,64,2048]{3,2,1,0:T(8,128)(2,1)} %pad_maximum_fusion.10), channel_id=1, source_target_pairs={{0,16},{4,20},{8,24},{12,28},{16,0},{20,4},{24,8},{28,12},{1,17},{... | collective-permute-start | bytes 4718600 | tf_op jit(solution)/shard_map/ppermute | solution.py:25
  287.7 52.6 %collective-permute-start.27 = (bf16[4,3,64,2048]{3,2,1,0:T(8,128)(2,1)S(1)}, bf16[4,3,64,2048]{3,2,1,0:T(8,128)(2,1)}, u32[]{:S(2)}, u32[]{:S(2)}) collective-permute-start(bf16[4,3,64,2048]{3,2,1,0:T(8,128)(2,1)S(1)} %pad_maximum_fusion.2.refs_0_), channel_id=1, source_target_pairs={{0,4},{4,0},{8,12},{12,8},{16,20},{20,16},{24,28},{28,24},{1,5},{5... | collective-permute-start | bytes 9437192 | tf_op jit(solution)/shard_map/ppermute | solution.py:25
  290.8 49.5 %collective-permute-start.28 = (bf16[4,3,64,2048]{3,2,1,0:T(8,128)(2,1)S(1)}, bf16[4,3,64,2048]{3,2,1,0:T(8,128)(2,1)}, u32[]{:S(2)}, u32[]{:S(2)}) collective-permute-start(bf16[4,3,64,2048]{3,2,1,0:T(8,128)(2,1)S(1)} %pad_maximum_fusion.3.refs_1_), channel_id=1, source_target_pairs={{0,4},{4,0},{8,12},{12,8},{16,20},{20,16},{24,28},{28,24},{1,5},{5... | collective-permute-start | bytes 9437192 | tf_op jit(solution)/shard_map/ppermute | solution.py:25
  468.0 127.3 %collective-permute-start.29 = (bf16[192,1024]{1,0:T(8,128)(2,1)}, bf16[192,1024]{1,0:T(8,128)(2,1)S(1)}, u32[]{:S(2)}, u32[]{:S(2)}) collective-permute-start(bf16[192,1024]{1,0:T(8,128)(2,1)} %get-tuple-element.113), channel_id=1, source_target_pairs={{2,0},{3,1},{0,2},{1,3},{6,4},{7,5},{4,6},{5,7},{10,8},{11,9},{8,1... | collective-permute-start | bytes 1179656 | tf_op jit(solution)/shard_map/ppermute | solution.py:360
  477.1 118.3 %collective-permute-start.30 = (bf16[192,1024]{1,0:T(8,128)(2,1)}, bf16[192,1024]{1,0:T(8,128)(2,1)}, u32[]{:S(2)}, u32[]{:S(2)}) collective-permute-start(bf16[192,1024]{1,0:T(8,128)(2,1)} %get-tuple-element.112), channel_id=1, source_target_pairs={{1,0},{2,1},{3,2},{0,3},{5,4},{6,5},{7,6},{4,7},{9,8},{10,9},{11,1... | collective-permute-start | bytes 1179656 | tf_op jit(solution)/shard_map/ppermute | solution.py:360
  485.1 123.8 %collective-permute-start.35 = (bf16[6,128,1024]{2,1,0:T(8,128)(2,1)}, bf16[6,128,1024]{2,1,0:T(8,128)(2,1)}, u32[]{:S(2)}, u32[]{:S(2)}) collective-permute-start(bf16[6,128,1024]{2,1,0:T(8,128)(2,1)} %bitcast.46.mine_ref), channel_id=1, source_target_pairs={{0,4},{4,0},{8,12},{12,8},{16,20},{20,16},{24,28},{28,24},{1,5},{5... | collective-permute-start | bytes 4718600 | tf_op jit(solution)/shard_map/ppermute | solution.py:25
  578.0 52.2 %collective-permute-start.67 = (bf16[512,2048]{1,0:T(8,128)(2,1)}, bf16[512,2048]{1,0:T(8,128)(2,1)}, u32[]{:S(2)}, u32[]{:S(2)}) collective-permute-start(bf16[512,2048]{1,0:T(8,128)(2,1)} %convolution_convert_fusion.2), channel_id=1, source_target_pairs={{0,4},{4,0},{8,12},{12,8},{16,20},{20,16},{24,28},{28,24},{1,5},{5... | collective-permute-start | bytes 6291464 | tf_op jit(solution)/shard_map/ppermute | solution.py:25
  637.6 52.7 %collective-permute-start.68 = (bf16[2,128,2048]{2,1,0:T(8,128)(2,1)}, bf16[2,128,2048]{2,1,0:T(8,128)(2,1)}, u32[]{:S(2)}, u32[]{:S(2)}) collective-permute-start(bf16[2,128,2048]{2,1,0:T(8,128)(2,1)} %bitcast.91), channel_id=1, source_target_pairs={{0,16},{4,20},{8,24},{12,28},{16,0},{20,4},{24,8},{28,12},{1,17},{... | collective-permute-start | bytes 3145736 | tf_op jit(solution)/shard_map/ppermute | solution.py:25
  644.0 48.4 %collective-permute-start.64 = (bf16[2,128,2048]{2,1,0:T(8,128)(2,1)}, bf16[2,128,2048]{2,1,0:T(8,128)(2,1)}, u32[]{:S(2)}, u32[]{:S(2)}) collective-permute-start(bf16[2,128,2048]{2,1,0:T(8,128)(2,1)} %slice_bitcast_fusion), channel_id=1, source_target_pairs={{0,8},{4,12},{8,0},{12,4},{16,24},{20,28},{24,16},{28,20},{1,9},{5... | collective-permute-start | bytes 3145736 | tf_op jit(solution)/shard_map/ppermute | solution.py:25
  653.3 59.4 %collective-permute-start.77 = (bf16[2,128,2048]{1,2,0:T(8,128)(2,1)}, bf16[2,128,2048]{1,2,0:T(8,128)(2,1)}, u32[]{:S(2)}, u32[]{:S(2)}) collective-permute-start(bf16[2,128,2048]{1,2,0:T(8,128)(2,1)} %copy.50), channel_id=1, source_target_pairs={{0,16},{4,20},{8,24},{12,28},{16,0},{20,4},{24,8},{28,12},{1,17},{... | collective-permute-start | bytes 3145736 | tf_op jit(solution)/shard_map/ppermute | solution.py:25
  664.5 51.2 %collective-permute-start.73 = (bf16[2,128,2048]{1,2,0:T(8,128)(2,1)}, bf16[2,128,2048]{1,2,0:T(8,128)(2,1)S(1)}, u32[]{:S(2)}, u32[]{:S(2)}) collective-permute-start(bf16[2,128,2048]{1,2,0:T(8,128)(2,1)} %bitcast.363), channel_id=1, source_target_pairs={{0,8},{4,12},{8,0},{12,4},{16,24},{20,28},{24,16},{28,20},{1,9},{5... | collective-permute-start | bytes 3145736 | tf_op jit(solution)/shard_map/ppermute | solution.py:25
  668.4 81.0 %collective-permute-start.39 = (bf16[6,128,512]{2,1,0:T(8,128)(2,1)S(1)}, bf16[6,128,512]{2,1,0:T(8,128)(2,1)S(1)}, u32[]{:S(2)}, u32[]{:S(2)}) collective-permute-start(bf16[6,128,512]{2,1,0:T(8,128)(2,1)S(1)} %slice.574), channel_id=1, source_target_pairs={{0,16},{4,20},{8,24},{12,28},{16,0},{20,4},{24,8},{28,12},{1,17},{... | collective-permute-start | bytes 2359304 | tf_op jit(solution)/shard_map/ppermute | solution.py:25
  690.3 60.6 %collective-permute-start.37 = (bf16[6,128,512]{2,1,0:T(8,128)(2,1)S(1)}, bf16[6,128,512]{2,1,0:T(8,128)(2,1)S(1)}, u32[]{:S(2)}, u32[]{:S(2)}) collective-permute-start(bf16[6,128,512]{2,1,0:T(8,128)(2,1)S(1)} %slice.572), channel_id=1, source_target_pairs={{0,8},{4,12},{8,0},{12,4},{16,24},{20,28},{24,16},{28,20},{1,9},{5... | collective-permute-start | bytes 2359304 | tf_op jit(solution)/shard_map/ppermute | solution.py:25
  779.7 54.8 %collective-permute-start.40 = (bf16[192,1024]{1,0:T(8,128)(2,1)S(1)}, bf16[192,1024]{1,0:T(8,128)(2,1)S(1)}, u32[]{:S(2)}, u32[]{:S(2)}) collective-permute-start(bf16[192,1024]{1,0:T(8,128)(2,1)S(1)} %get-tuple-element.107), channel_id=1, source_target_pairs={{2,0},{3,1},{0,2},{1,3},{6,4},{7,5},{4,6},{5,7},{10,8},{11,9},{8,1... | collective-permute-start | bytes 1179656 | tf_op jit(solution)/shard_map/ppermute | solution.py:360
  (172 other events, 2862.2 us)

commit v3 on v2

v3 whole, which is shorter than its diff:
```python
import functools
import math

import jax
import jax.numpy as jnp
from jax import lax
from jax.experimental import pallas as pl
from jax.experimental.pallas import tpu as pltpu
from jax.sharding import PartitionSpec as P

HEAD_DIM = 64
BLOCK = 128
UP = 4
HALVES = 2
VMEM_LIMIT = 58 << 20
PAIR = 2 * HEAD_DIM
NEGATIVE = -1e30
epsilon = 1e-05
f32 = jnp.float32
bf16 = jnp.bfloat16
ROOT_2_PI = math.sqrt(2.0 / math.pi)
LONG_COST = pl.CostEstimate(flops=1 << 36, bytes_accessed=1 << 26, transcendentals=0)


def xor_swap(value, axis, mask):
    size = lax.axis_size(axis)
    return lax.ppermute(value, axis, [(i, i ^ mask) for i in range(size)])


def pause_kernel(value_ref, out_ref):
    out_ref[...] = value_ref[...]


class Order:
    def __init__(self):
        self.last = ()
        self.token = None

    def __call__(self, *values):
        tied = lax.optimization_barrier(tuple(values) + self.last)[: len(values)]
        return tied[0] if len(values) == 1 else tied

    def mark(self, *values):
        self.last = values

    def pause(self):
        self.token = self(jnp.zeros((8, 128), f32) if self.token is None else self.token)
        self.token = pl.pallas_call(
            pause_kernel, out_shape=jax.ShapeDtypeStruct((8, 128), f32), cost_estimate=LONG_COST
        )(self.token)
        self.mark(self.token)


def norm_forward(values, gain, shift):
    centered = values - jnp.mean(values, axis=-1, keepdims=True)
    inverse = lax.rsqrt(jnp.mean(centered * centered, axis=-1, keepdims=True) + epsilon)
    standard = centered * inverse
    return (standard * gain + shift, standard, inverse)


def norm_backward(upstream, standard, inverse, gain):
    scaled = upstream * gain
    inner = (
        scaled
        - jnp.mean(scaled, axis=-1, keepdims=True)
        - standard * jnp.mean(scaled * standard, axis=-1, keepdims=True)
    )
    return (inner * inverse, jnp.sum(upstream * standard, axis=0), jnp.sum(upstream, axis=0))


def mm(left, right):
    return jnp.dot(left, right, preferred_element_type=f32)


def mm_nt(left, right):
    return lax.dot_general(left, right, (((1,), (1,)), ((), ())), preferred_element_type=f32)


def mm_tn(left, right):
    return lax.dot_general(left, right, (((0,), (0,)), ((), ())), preferred_element_type=f32)


def pair_probs(q_pair, k_cat, allowed):
    low_half = lax.broadcasted_iota(jnp.int32, (BLOCK, PAIR), 1) < HEAD_DIM
    zero = jnp.zeros_like(q_pair)
    q_stack = jnp.concatenate(
        [jnp.where(low_half, q_pair, zero), jnp.where(low_half, zero, q_pair)], axis=0
    )
    scores = mm_nt(k_cat, q_stack) * (1.0 / math.sqrt(HEAD_DIM))
    scores = jnp.where(allowed, scores, NEGATIVE)
    top = jnp.max(scores, axis=0, keepdims=True)
    raised = jnp.exp(scores - top)
    probs = raised * (1.0 / jnp.sum(raised, axis=0, keepdims=True))
    return q_stack, probs, low_half


def allowed_mask(far_flag):
    key_at = lax.broadcasted_iota(jnp.int32, (2 * BLOCK, 2 * BLOCK), 0)
    query_at = lax.broadcasted_iota(jnp.int32, (2 * BLOCK, 2 * BLOCK), 1)
    query_at = jnp.where(query_at >= BLOCK, query_at - BLOCK, query_at)
    first = jnp.where(far_flag > 0, BLOCK, 2 * BLOCK)
    return (key_at <= query_at) | (key_at >= first)


def pair_columns(p, width):
    return [slice(t * width + p * PAIR, t * width + (p + 1) * PAIR) for t in range(3)]


def key_value(own_ref, far_ref, columns, width):
    out = []
    for cols in columns[1:]:
        far_cols = slice(cols.start - width, cols.stop - width)
        out.append(jnp.concatenate([own_ref[:, cols], far_ref[:, far_cols]], axis=0))
    return out


def attention_forward_kernel(pairs, has_far, own_ref, far_ref, out_ref):
    allowed = allowed_mask(has_far[pl.program_id(0)])
    width = pairs * PAIR
    for p in range(pairs):
        columns = pair_columns(p, width)
        k_cat, v_cat = key_value(own_ref, far_ref, columns, width)
        _, probs, low_half = pair_probs(own_ref[:, columns[0]], k_cat, allowed)
        mixed = mm_tn(probs.astype(bf16), v_cat)
        out_ref[:, columns[0]] = jnp.where(low_half, mixed[:BLOCK], mixed[BLOCK:]).astype(bf16)


def attention_forward(has_far, own, far, width):
    blocks = has_far.shape[0]
    row_block = lambda array: pl.BlockSpec((BLOCK, array.shape[1]), lambda b, flags: (b, 0))
    shape = jax.ShapeDtypeStruct((blocks * BLOCK, width), bf16)
    return pl.pallas_call(
        functools.partial(attention_forward_kernel, width // PAIR),
        grid_spec=pltpu.PrefetchScalarGridSpec(
            num_scalar_prefetch=1,
            grid=(blocks,),
            in_specs=[row_block(own), row_block(far)],
            out_specs=row_block(shape),
        ),
        out_shape=shape,
        compiler_params=pltpu.CompilerParams(vmem_limit_bytes=16 << 20),
        cost_estimate=LONG_COST,
    )(has_far, own, far)


def attention_backward_kernel(pairs, has_far, own_ref, far_ref, grad_ref, out_ref):
    allowed = allowed_mask(has_far[pl.program_id(0)])
    width = pairs * PAIR
    scale = 1.0 / math.sqrt(HEAD_DIM)
    out_ref[1, :, :width] = jnp.zeros((BLOCK, width), bf16)
    for p in range(pairs):
        columns = pair_columns(p, width)
        k_cat, v_cat = key_value(own_ref, far_ref, columns, width)
        q_stack, probs, low_half = pair_probs(own_ref[:, columns[0]], k_cat, allowed)
        grad = grad_ref[:, columns[0]]
        zero = jnp.zeros_like(grad)
        grad_stack = jnp.concatenate(
            [jnp.where(low_half, grad, zero), jnp.where(low_half, zero, grad)], axis=0
        )
        grad_probs = mm_nt(v_cat, grad_stack)
        total = jnp.sum(probs * grad_probs, axis=0, keepdims=True)
        grad_scores = (probs * (grad_probs - total)).astype(bf16)
        dq = mm_tn(grad_scores, k_cat) * scale
        out_ref[0, :, columns[0]] = jnp.where(low_half, dq[:BLOCK], dq[BLOCK:]).astype(bf16)
        dk = (mm(grad_scores, q_stack) * scale).astype(bf16)
        dv = mm(probs.astype(bf16), grad_stack).astype(bf16)
        for half in range(2):
            rows = slice(half * BLOCK, (half + 1) * BLOCK)
            out_ref[half, :, columns[1]] = dk[rows]
            out_ref[half, :, columns[2]] = dv[rows]


def attention_backward(has_far, own, far, grad):
    blocks, width = has_far.shape[0], grad.shape[1]
    row_block = lambda array: pl.BlockSpec((BLOCK, array.shape[1]), lambda b, flags: (b, 0))
    return pl.pallas_call(
        functools.partial(attention_backward_kernel, width // PAIR),
        grid_spec=pltpu.PrefetchScalarGridSpec(
            num_scalar_prefetch=1,
            grid=(blocks,),
            in_specs=[row_block(own), row_block(far), row_block(grad)],
            out_specs=pl.BlockSpec((2, BLOCK, 3 * width), lambda b, flags: (0, b, 0)),
        ),
        out_shape=jax.ShapeDtypeStruct((2, blocks * BLOCK, 3 * width), bf16),
        compiler_params=pltpu.CompilerParams(vmem_limit_bytes=20 << 20),
        cost_estimate=LONG_COST,
    )(has_far, own, far, grad)


def join_kernel(rows, first, *refs):
    got, (tile_ref, gain_ref, shift_ref, joined_ref, normed_ref, coarse_ref, held_ref) = (
        refs[:-7],
        refs[-7:],
    )
    pieces = len(got)
    which = (first[0] + pieces - pl.program_id(0)) % pieces
    for s in range(pieces):

        @pl.when(which == s)
        def _():
            held_ref[...] = got[s][...]

    coarse = held_ref[rows:, :]
    coarse_ref[...] = coarse
    up_row = lax.broadcasted_iota(jnp.int32, (rows, rows // UP), 0) // UP
    up_col = lax.broadcasted_iota(jnp.int32, (rows, rows // UP), 1)
    spread = mm((up_row == up_col).astype(f32).astype(bf16), coarse)
    joined = held_ref[:rows, :].astype(f32) + spread * tile_ref[...]
    joined_ref[...] = joined
    normed_ref[...] = norm_forward(joined, gain_ref[...], shift_ref[...])[0].astype(bf16)


def join(first, got, tile, gain, shift):
    pieces, rows, model = len(got), tile.shape[0], tile.shape[1]
    small = rows // UP
    fixed = lambda array: pl.BlockSpec(array.shape, lambda p, f: (0, 0))
    piece = lambda count: pl.BlockSpec((count, model), lambda p, f: (p, 0))
    return pl.pallas_call(
        functools.partial(join_kernel, rows),
        grid_spec=pltpu.PrefetchScalarGridSpec(
            num_scalar_prefetch=1,
            grid=(pieces,),
            in_specs=[fixed(g) for g in got] + [fixed(tile), fixed(gain), fixed(shift)],
            out_specs=[piece(rows), piece(rows), piece(small)],
            scratch_shapes=[pltpu.VMEM((rows + small, model), bf16)],
        ),
        out_shape=[
            jax.ShapeDtypeStruct((pieces * rows, model), f32),
            jax.ShapeDtypeStruct((pieces * rows, model), bf16),
            jax.ShapeDtypeStruct((pieces * small, model), bf16),
        ],
        compiler_params=pltpu.CompilerParams(vmem_limit_bytes=16 << 20),
        cost_estimate=LONG_COST,
    )(first, *got, tile, gain, shift)


def fill_chunk(masks, me, tables, out_ref):
    half = tables[0].shape[2]
    for which, table in enumerate(tables):
        order = masks if which % 2 == 0 else masks[::-1]
        for k, mask in enumerate(relative_masks(order)):
            row = (me ^ (mask | (which // 2))) * 2 * half + (which % 2) * half
            out_ref[pl.ds(pl.multiple_of(row, half), half), :] = table[k, 0]


def load_chunk(masks, me, chunk, n_own, own_ref, tables, out_ref):
    @pl.when(chunk < n_own)
    def _():
        out_ref[...] = own_ref[...]

    @pl.when(chunk >= n_own)
    def _():
        fill_chunk(masks, me, tables, out_ref)


def by_parity(step, buffers, body):
    for parity in range(2):

        @pl.when(step % 2 == parity)
        def _():
            body(buffers[1 - parity], buffers[parity])


def scatter_rows(masks, color, me, value, held_ref):
    count = 2 << len(masks)
    slab = value.shape[0] // count
    last = len(masks) - 1
    for b in range(count):
        away = me ^ b
        at = (away & 1) << len(masks)
        for i, mask in enumerate(masks):
            place = last - i if isinstance(color, int) and color == 0 else i
            if not isinstance(color, int):
                place = jnp.where(color == 0, last - i, i)
            at = at + (((away >> (mask.bit_length() - 1)) & 1) << place)
        row = pl.multiple_of(at * slab, slab)
        held_ref[pl.ds(row, slab), :] = value[b * slab : (b + 1) * slab].astype(bf16)


def split_rows(held_ref, keep_ref, send_ref):
    half = held_ref.shape[0] // 2
    keep_ref[0] = held_ref[:half, :]
    send_ref[0] = held_ref[half:, :]


def feed_forward_kernel(masks, n_own, n, me, *refs):
    one_tables, two_tables = refs[:4], refs[4:8]
    (own_one, own_two, x_ref, bias_ref, residual_ref, last_ref, left_ref) = refs[8:15]
    slope_ref, out_ref, keep_ref, send_ref = refs[15:19]
    w_one, w_two, even_ref, odd_ref, act_ref, held_ref, acc_ref = refs[19:]
    step = pl.program_id(0)
    load_chunk(masks, me[0], jnp.minimum(step, n - 1), n_own, own_one, one_tables, w_one)
    load_chunk(masks, me[0], jnp.maximum(step - 1, 0), n_own, own_two, two_tables, w_two)
    ratio = ROOT_2_PI * 0.044715
    rows = x_ref.shape[0] // 2

    def body(before, now):
        for r in range(2):
            at = slice(r * rows, (r + 1) * rows)
            h = before[at, :]
            square = h * h
            gate = 0.5 + 0.5 * jnp.tanh(h * (ROOT_2_PI + ratio * square))
            act = (h * gate).astype(bf16)
            act_ref[at, :] = act
            slope_ref[at, :] = (
                gate * (1.0 + 2.0 * h * (1.0 - gate) * (ROOT_2_PI + 3.0 * ratio * square))
            ).astype(bf16)
            now[at, :] = mm(x_ref[at, :], w_one[...]) + bias_ref[...]
            acc_ref[at, :] += mm_nt(act, w_two[...])
        scatter_rows(masks, jnp.maximum(step - 1, 0) % n_own, me[0], mm(left_ref[...], act_ref[...]), held_ref)

    by_parity(step, (even_ref, odd_ref), body)
    split_rows(held_ref, keep_ref, send_ref)

    @pl.when(step == 0)
    def _():
        acc_ref[...] = jnp.zeros_like(acc_ref)

    @pl.when(step == n)
    def _():
        out_ref[...] = (residual_ref[...] + (acc_ref[...] + last_ref[...])).astype(bf16)


def feed_backward_kernel(masks, n_own, n, me, *refs):
    two_tables, one_tables = refs[:4], refs[4:8]
    own_two, own_one, g_ref, slope_ref, left_ref = refs[8:13]
    bias_ref, out_ref, keep_ref, send_ref = refs[13:17]
    w_two, w_one, even_ref, odd_ref, grad_ref, held_ref = refs[17:]
    step = pl.program_id(0)
    load_chunk(masks, me[0], jnp.minimum(step, n - 1), n_own, own_two, two_tables, w_two)
    load_chunk(masks, me[0], jnp.maximum(step - 1, 0), n_own, own_one, one_tables, w_one)
    rows = g_ref.shape[0] // 2

    def body(before, now):
        sums = []
        for r in range(2):
            at = slice(r * rows, (r + 1) * rows)
            grad = (before[at, :] * slope_ref[at, :].astype(f32)).astype(bf16)
            grad_ref[at, :] = grad
            sums.append(jnp.sum(grad.astype(f32), axis=0, keepdims=True))
            now[at, :] = mm(g_ref[at, :], w_two[...])
            out_ref[at, :] += mm_nt(grad, w_one[...])
        bias_ref[...] = sums[0] + sums[1]
        scatter_rows(masks, jnp.maximum(step - 1, 0) % n_own, me[0], mm(left_ref[...], grad_ref[...]), held_ref)

    by_parity(step, (even_ref, odd_ref), body)
    split_rows(held_ref, keep_ref, send_ref)

    @pl.when(step == 0)
    def _():
        out_ref[...] = jnp.zeros_like(out_ref)


def feed_call(kernel, masks, me, tables, own_first, own_second, first_part, arrays, outs, scratch):
    count, slots, half, both = tables[0].shape
    model, width = own_first.shape
    n_own = HALVES
    chunk = width // n_own
    n = n_own * (slots + 1)

    def at(j, lag):
        return jnp.clip(j - lag, 0, n - 1)

    def by_head(j, lag, me):
        c = at(j, lag)
        return ((c // n_own) ^ me[1]) * n_own + c % n_own

    def by_half(j, me):
        c = at(j, 1)
        return c % n_own * (slots + 1) + ((c // n_own) ^ me[1])

    def table_spec(part, lag):
        def index(j, me):
            c = jnp.maximum(at(j, lag), n_own)
            return (0, c // n_own - 1, 0, part * n_own + c % n_own)

        return pl.BlockSpec((count, 1, half, chunk), index)

    def own_spec(lag):
        return pl.BlockSpec((model, chunk), lambda j, me: (0, jnp.minimum(at(j, lag), n_own - 1)))

    def spec(array, lag):
        if lag is None:
            return pl.BlockSpec(array.shape, lambda j, me: (0, 0))
        lag, absolute = lag
        return pl.BlockSpec(
            (array.shape[0], chunk), lambda j, me: (0, by_head(j, lag, me) if absolute else at(j, lag))
        )

    rows = arrays[0][0].shape[0]
    weight = jax.ShapeDtypeStruct((n, model // 2, chunk), bf16)
    weight_spec = pl.BlockSpec((1, model // 2, chunk), lambda j, me: (by_half(j, me), 0, 0))
    return pl.pallas_call(
        functools.partial(kernel, masks, n_own, n),
        grid_spec=pltpu.PrefetchScalarGridSpec(
            num_scalar_prefetch=1,
            grid=(n + 1,),
            in_specs=[table_spec(first_part, 0)] * 4
            + [table_spec(1 - first_part, 1)] * 4
            + [own_spec(0), own_spec(1)]
            + [spec(a, lag) for a, lag in arrays],
            out_specs=[spec(o, lag) for o, lag in outs] + [weight_spec, weight_spec],
            scratch_shapes=[
                pltpu.VMEM((model, chunk), bf16),
                pltpu.VMEM((model, chunk), bf16),
                pltpu.VMEM((rows, chunk), f32),
                pltpu.VMEM((rows, chunk), f32),
                pltpu.VMEM((rows, chunk), bf16),
                pltpu.VMEM((model, chunk), bf16),
            ]
            + scratch,
        ),
        out_shape=[o for o, _ in outs] + [weight, weight],
        compiler_params=pltpu.CompilerParams(vmem_limit_bytes=54 << 20),
        cost_estimate=LONG_COST,
    )(me, *tables, *tables, own_first, own_second, *[a for a, _ in arrays])


def far_pick_kernel(limit, where_a, where_b, *refs):
    ins, outs = refs[:8], refs[8:]
    count, half = pl.num_programs(0), ins[0].shape[2]
    for who in range(2):
        for color, where_ref in enumerate((where_a, where_b)):
            held, got = ins[4 * who + 2 * color : 4 * who + 2 * color + 2]
            beyond = where_ref[pl.program_id(0) + who * count] >= limit
            outs[who][0, :, color * half : (color + 1) * half] = jnp.where(beyond, got[0], held[0])


def far_pick(tables, where_a, where_b):
    count = where_a.shape[0] // 2
    limit, _, half = tables[0][0].shape

    def spec(who, color):
        def index(j, wa, wb):
            return ((wa, wb)[color][j + who * count] % limit, 0, 0)

        return pl.BlockSpec((1, BLOCK, half), index)

    out = pl.BlockSpec((1, BLOCK, 2 * half), lambda j, wa, wb: (j, 0, 0))
    shape = jax.ShapeDtypeStruct((count, BLOCK, 2 * half), bf16)
    return pl.pallas_call(
        functools.partial(far_pick_kernel, limit),
        grid_spec=pltpu.PrefetchScalarGridSpec(
            num_scalar_prefetch=2,
            grid=(count,),
            in_specs=[spec(who, color) for who in range(2) for color in range(2) for _ in range(2)],
            out_specs=[out, out],
        ),
        out_shape=[shape, shape],
        compiler_params=pltpu.CompilerParams(vmem_limit_bytes=VMEM_LIMIT),
        cost_estimate=LONG_COST,
    )(where_a, where_b, *[t for _ in range(2) for table in tables for t in table])


def far_route_kernel(count, where_a, where_b, mine_ref, other_ref, *refs):
    outs, acc_ref = refs[:4], refs[4]
    half = outs[0].shape[2]
    acc_ref[...] = jnp.zeros_like(acc_ref)
    for part in range(2):
        step = pl.program_id(0) + part * pl.num_programs(0)
        for source, base in ((mine_ref, 0), (other_ref, count)):
            for j in range(count):

                @pl.when(where_a[base + j] == step)
                def _():
                    acc_ref[part, :, :half] += source[j, :, :half].astype(f32)

                @pl.when(where_b[base + j] == step)
                def _():
                    acc_ref[part, :, half:] += source[j, :, half:].astype(f32)

        outs[part][0] = acc_ref[part, :, :half].astype(bf16)
        outs[2 + part][0] = acc_ref[part, :, half:].astype(bf16)


def far_route(mine, other, where_a, where_b, limit):
    count, _, width = mine.shape
    whole = pl.BlockSpec(mine.shape, lambda k, wa, wb: (0, 0, 0))
    out = pl.BlockSpec((1, BLOCK, width // 2), lambda k, wa, wb: (k, 0, 0))
    shape = jax.ShapeDtypeStruct((limit, BLOCK, width // 2), bf16)
    return pl.pallas_call(
        functools.partial(far_route_kernel, count),
        grid_spec=pltpu.PrefetchScalarGridSpec(
            num_scalar_prefetch=2,
            grid=(limit,),
            in_specs=[whole, whole],
            out_specs=[out] * 4,
            scratch_shapes=[pltpu.VMEM((2, BLOCK, width), f32)],
        ),
        out_shape=[shape] * 4,
        compiler_params=pltpu.CompilerParams(vmem_limit_bytes=18 << 20),
        cost_estimate=LONG_COST,
    )(where_a, where_b, mine, other)


def leave_kernel(n_a, n_b, own_ref, joined_ref, res_ref, coarse_ref, gain_ref, *refs):
    part_a, part_b = refs[:n_a], refs[n_a : n_a + n_b]
    out_ref, up_ref, gain_out, shift_out = refs[n_a + n_b :]

    @pl.when(pl.program_id(0) == 0)
    def _():
        for ref in (up_ref, gain_out, shift_out):
            ref[...] = jnp.zeros_like(ref)

    back = jnp.concatenate(
        [sum(r[0].astype(f32) for r in parts) for parts in (part_a, part_b)], axis=1
    )
    upstream = own_ref[...] + back
    gain = gain_ref[...]
    joined = joined_ref[...]
    _, standard, inverse = norm_forward(joined, gain, gain)
    scaled = upstream * gain
    inner = (
        scaled
        - jnp.mean(scaled, axis=-1, keepdims=True)
        - standard * jnp.mean(scaled * standard, axis=-1, keepdims=True)
    )
    total = res_ref[...] + inner * inverse
    out_ref[...] = total.astype(bf16)
    gain_out[...] += jnp.sum(upstream * standard, axis=0, keepdims=True)
    shift_out[...] += jnp.sum(upstream, axis=0, keepdims=True)
    up_row = lax.broadcasted_iota(jnp.int32, (BLOCK, BLOCK // UP), 0) // UP
    up_col = lax.broadcasted_iota(jnp.int32, (BLOCK, BLOCK // UP), 1)
    weighted = total * mm((up_row == up_col).astype(f32).astype(bf16), coarse_ref[...])
    phase = lax.broadcasted_iota(jnp.int32, weighted.shape, 0) % UP
    for p in range(UP):
        picked = jnp.where(phase == p, weighted, 0.0)
        up_ref[p : p + 1, :] += jnp.sum(picked, axis=0, keepdims=True)


def leave(own, joined, residual, coarse, gain, part_a, part_b):
    tokens, model = own.shape
    rows = pl.BlockSpec((BLOCK, model), lambda b: (b, 0))
    fixed = lambda count: pl.BlockSpec((count, model), lambda b: (0, 0))
    part = pl.BlockSpec((1, BLOCK, model // 2), lambda b: (b, 0, 0))
    return pl.pallas_call(
        functools.partial(leave_kernel, len(part_a), len(part_b)),
        grid=(tokens // BLOCK,),
        in_specs=[rows, rows, rows, pl.BlockSpec((BLOCK // UP, model), lambda b: (b, 0)), fixed(1)]
        + [part] * (len(part_a) + len(part_b)),
        out_specs=[rows, fixed(UP), fixed(1), fixed(1)],
        out_shape=[
            jax.ShapeDtypeStruct((tokens, model), bf16),
            jax.ShapeDtypeStruct((UP, model), f32),
            jax.ShapeDtypeStruct((1, model), f32),
            jax.ShapeDtypeStruct((1, model), f32),
        ],
        compiler_params=pltpu.CompilerParams(vmem_limit_bytes=VMEM_LIMIT),
        cost_estimate=LONG_COST,
    )(own, joined, residual, coarse, gain, *part_a, *part_b)


def relative_masks(masks):
    return [sum(m for bit, m in enumerate(masks) if k >> bit & 1) for k in range(1 << len(masks))]


def assemble_kernel(columns, n_own, n_out, dp_index, *refs):
    tables, own, outs = refs[:4], refs[4 : 4 + n_own], refs[4 + n_own :]
    slots, half = tables[0].shape[1], tables[0].shape[2]

    def fill(first, second):
        for color, table in enumerate((first, second)):
            rows = slice(color * half, (color + 1) * half)
            for c0, width, target, t0 in columns:
                for s in range(slots):
                    at = t0 + (s + 1) * width
                    outs[target][rows, at : at + width] = table[0, s, :, c0 : c0 + width]

    core = pl.program_id(0)

    @pl.when(core == 0)
    def _():
        fill(tables[0], tables[1])

    @pl.when(core == 1)
    def _():
        fill(tables[2], tables[3])

    for ref, (c0, width, target, t0) in zip(own, columns):
        outs[target][:, t0 : t0 + width] = ref[...]


def assemble(dp_index, tables, own, columns, masks, widths):
    bits = len(masks)
    count, slots, half, width = tables[0].shape
    model = 2 * count * 2 * half

    def reverse(k):
        return sum(((k >> i) & 1) << (bits - 1 - i) for i in range(bits))

    def table_spec(which):
        def index(core, k, dp):
            k = jnp.where(core == which // 2, k, 0 if which >= 2 else count - 1)
            return (reverse(k) if which % 2 else k, 0, 0, 0)

        return pl.BlockSpec((1, slots, half, width), index)

    def row(core, k, dp):
        return (dp[0] ^ ((k << 1) | core), 0)

    return pl.pallas_call(
        functools.partial(assemble_kernel, columns, len(own), len(widths)),
        grid_spec=pltpu.PrefetchScalarGridSpec(
            num_scalar_prefetch=1,
            grid=(2, count),
            in_specs=[table_spec(i) for i in range(4)]
            + [pl.BlockSpec((2 * half, o.shape[1]), row) for o in own],
            out_specs=[pl.BlockSpec((2 * half, w), row) for w in widths],
        ),
        out_shape=[jax.ShapeDtypeStruct((model, w), bf16) for w in widths],
        compiler_params=pltpu.CompilerParams(vmem_limit_bytes=16 << 20),
        cost_estimate=LONG_COST,
    )(dp_index, *tables, *own)


def attention_weights_kernel(masks, heads, me, own_t, far_t, branch_t, grad_own, grad_far, attended, *refs):
    keep_ref, send_ref, total_ref, held_ref = refs
    tile = pl.program_id(0)
    kind = tile // heads

    @pl.when(kind == 0)
    def _():
        total_ref[...] = mm(own_t[...], grad_own[...])

    @pl.when((kind == 1) | (kind == 2))
    def _():
        total_ref[...] = mm(own_t[...], grad_own[...]) + mm(far_t[...], grad_far[...])

    @pl.when(kind == 3)
    def _():
        total_ref[...] = mm(branch_t[...], attended[...])

    for color in range(2):

        @pl.when(kind // 2 == color)
        def _():
            scatter_rows(masks, color, me[0], total_ref[...], held_ref)

    split_rows(held_ref, keep_ref, send_ref)


def attention_weights(masks, me, own_t, far_t, branch_t, grad, attended, width):
    model, tokens = own_t.shape
    heads = attended.shape[1] // width
    whole = pl.BlockSpec((model, tokens), lambda j, me: (0, 0))
    part = lambda p: pl.BlockSpec(
        (None, tokens, width), lambda j, me: (p, 0, jnp.minimum(j, 3 * heads - 1))
    )
    out = pl.BlockSpec((1, model // 2, width), lambda j, me: (j, 0, 0))
    shape = jax.ShapeDtypeStruct((4 * heads, model // 2, width), bf16)
    return pl.pallas_call(
        functools.partial(attention_weights_kernel, masks, heads),
        grid_spec=pltpu.PrefetchScalarGridSpec(
            num_scalar_prefetch=1,
            grid=(4 * heads,),
            in_specs=[whole] * 3
            + [
                part(0),
                part(1),
                pl.BlockSpec((tokens, width), lambda j, me: (0, jnp.maximum(j - 3 * heads, 0))),
            ],
            out_specs=[out, out],
            scratch_shapes=[pltpu.VMEM((model, width), f32), pltpu.VMEM((model, width), bf16)],
        ),
        out_shape=[shape, shape],
        compiler_params=pltpu.CompilerParams(vmem_limit_bytes=24 << 20),
        cost_estimate=LONG_COST,
    )(me, own_t, far_t, branch_t, grad, grad, attended)


class DpSum:
    def __init__(self, tie, terms, order):
        self.tie, self.terms, self.order = tie, list(terms), order
        self.rows = terms[0].shape[1]

    def upto(self, low, high):
        first, *others = self.terms
        total = self.tie(first)[:, low:high].astype(f32)
        for value in others:
            total = total + value[:, low:high].astype(f32)
        total = total.astype(bf16)
        self.tie.mark(total)
        return total

    def stage(self, step):
        sent = self.upto(self.rows >> (step + 1), self.rows >> step)
        self.terms.append(xor_swap(sent, "dp", self.order[step]))

    def final(self):
        return self.upto(0, self.rows >> len(self.order))


def local(
    activations,
    conditioning,
    cotangent,
    block_targets,
    up_gain,
    norm1_gain,
    norm1_shift,
    w_qkv,
    b_qv,
    w_out,
    b_out,
    norm2_gain,
    norm2_shift,
    w_fc1,
    b_fc1,
    w_fc2,
    b_fc2,
):
    micro, rows, model = activations.shape
    head_cols = w_qkv.shape[2]
    hidden_cols = w_fc1.shape[1]
    dp_size, head_size = lax.axis_size("dp"), lax.axis_size("head")
    me, here = lax.axis_index("dp"), lax.axis_index("head")
    group = head_size // micro
    tokens = rows * micro
    blocks = tokens // BLOCK
    slab = model // dp_size
    masks = [1 << i for i in range(1, dp_size.bit_length() - 1)]
    heads_all, hidden_all = head_cols * head_size, hidden_cols * head_size

    src_rank = here % micro
    my_micro, my_sub = here // group, here % group
    shifts = [
        [(hs * micro + hr, ((hr + s) % micro) * group + hs) for hs in range(group) for hr in range(micro)]
        for s in range(micro)
    ]

    def send(value, pairs):
        return value if all(a == b for a, b in pairs) else lax.ppermute(value, "head", pairs)

    def choose(options, index):
        out = options[-1]
        for k in range(len(options) - 1):
            out = jnp.where(index == k, options[k], out)
        return out

    def to_micro(value):
        return [
            lax.dynamic_index_in_dim(value, (src_rank + s) % micro, 0, False) for s in range(micro)
        ]

    def sent(pieces, *others):
        pieces = lax.optimization_barrier(tuple(pieces) + others)[: len(pieces)]
        return [send(piece, pairs) for piece, pairs in zip(pieces, shifts)]

    def in_rank_order(got):
        return jnp.concatenate([choose(got, (my_micro - p) % micro) for p in range(micro)], axis=0)

    def from_micro(value):
        pieces = value.reshape(micro, rows, -1)
        return [
            lax.dynamic_index_in_dim(pieces, (my_micro - s) % micro, 0, False) for s in range(micro)
        ]

    def back(pieces):
        return [send(piece, [(b, a) for a, b in pairs]) for piece, pairs in zip(pieces, shifts)]

    def in_micro_order(got):
        return jnp.stack([choose(got, (m - src_rank) % micro) for m in range(micro)])

    def my_slab(value, axis):
        return lax.dynamic_slice_in_dim(value, me * slab, slab, axis)

    tie = Order()
    hc, fc = head_cols, hidden_cols
    half = model // 2

    small = jnp.concatenate([b_qv.reshape(-1), b_fc1])
    per_row = 4 * hc
    small_rows = -(-small.shape[0] // per_row)
    padded = jnp.pad(small, (0, small_rows * per_row - small.shape[0])).reshape(small_rows, per_row)
    thirds, rest = [], padded
    for _ in range(3):
        third = lax.reduce_precision(rest, 8, 7)
        thirds.append(third.astype(bf16))
        rest = rest - third
    extra = jnp.pad(jnp.concatenate(thirds), ((0, 16 - 3 * small_rows), (0, 0)))
    strip_a = jnp.concatenate(
        [my_slab(w_qkv[0], 0), my_slab(w_qkv[1], 0), my_slab(w_qkv[2], 0), my_slab(w_out, 1).T],
        axis=1,
    )
    strip_a = jnp.concatenate([strip_a, extra], axis=0)
    tie.mark(strip_a)
    head_masks = [1 << i for i in range(head_size.bit_length() - 1)]
    head_places = [0]
    for mask in head_masks[::-1]:
        head_places = head_places + [p ^ mask for p in head_places]

    def over_head(strip):
        held = strip[None]
        for mask in head_masks[::-1]:
            held = jnp.concatenate([held, xor_swap(held, "head", mask)], axis=0)
        return [held[head_places.index(s)] for s in range(1, head_size)]

    slots_a = over_head(strip_a)
    strip_f = jnp.concatenate([my_slab(tie(w_fc1), 0), my_slab(w_fc2, 1).T], axis=1)
    own_two_t = tie(w_fc2).T
    own_out_t = tie(w_out).T
    up_tile = jnp.broadcast_to(tie(up_gain)[None], (rows // UP, UP, model)).reshape(rows, model)
    acts_out = to_micro(tie(jnp.concatenate([activations, conditioning], axis=1)))
    cot_out = to_micro(tie(cotangent))
    tie.mark(strip_f, own_two_t, own_out_t, up_tile, *acts_out, *cot_out)
    dp_orders = (masks, masks[::-1])
    dp_index = jnp.stack([me, here]).astype(jnp.int32)

    def colors_of(slots):
        rows_half = slab // 2
        held = [
            jnp.stack([v[c * rows_half : (c + 1) * rows_half] for v in slots])[None] for c in (0, 1)
        ]
        tie.mark(*held)
        return held

    def swap_stage(held, step):
        return [xor_swap(v, "dp", order[step]) for v, order in zip(held, dp_orders)]

    def widen(held, got):
        wider = [jnp.concatenate([a, b], axis=0) for a, b in zip(tie(*held), got)]
        tie.mark(*wider)
        return wider

    held_a = colors_of(tie(*slots_a))
    got_a = swap_stage(held_a, 0)
    got_acts = sent(acts_out, *held_a)
    for step in range(1, len(masks)):
        held_a = widen(held_a, got_a)
        got_a = swap_stage(held_a, step)
    held_a = widen(held_a, got_a)
    tables_a = held_a + [xor_swap(v, "dp", 1) for v in held_a]
    joined, normed, coarse = join(
        my_micro.reshape(1).astype(jnp.int32),
        tie(*got_acts),
        up_tile,
        norm1_gain.reshape(1, -1),
        norm1_shift.reshape(1, -1),
    )
    tie.mark(normed)

    stages_sub = [("head", 1 << i) for i in range(group.bit_length() - 1)]
    stage_lists = [stages_sub + [("dp", m) for m in order] for order in dp_orders]
    stages = len(stage_lists[0])
    shaped = tie(normed).reshape(blocks, BLOCK, model)
    far_held = [shaped[:, :, c * half : (c + 1) * half] for c in (0, 1)]
    tie.mark(*far_held)
    far_got = [xor_swap(v, *stage_lists[c][0]) for c, v in enumerate(far_held)]
    for step in range(1, stages):
        far_held = widen(far_held, far_got)
        far_got = [xor_swap(v, *stage_lists[c][step]) for c, v in enumerate(far_held)]
    limit = far_held[0].shape[0]
    table_row = lax.dynamic_index_in_dim(block_targets, my_micro, 0, False)

    def targets_of(device):
        return lax.dynamic_slice_in_dim(table_row, (device * group + my_sub) * blocks, blocks)

    targets = targets_of(me)
    targets_both = jnp.concatenate([targets, targets_of(me ^ 1)])
    owner = jnp.maximum(targets_both, 0) // blocks
    away = (owner // group) ^ me
    away_sub = (owner % group) ^ my_sub

    def table_index(stage_list):
        index = jnp.zeros_like(owner)
        for bit, (axis, mask) in enumerate(stage_list):
            far_bits = away if axis == "dp" else away_sub
            index = index + (((far_bits & mask) != 0).astype(jnp.int32) << bit)
        return index * blocks + jnp.maximum(targets_both, 0) % blocks

    index_a, index_b = table_index(stage_lists[0]), table_index(stage_lists[1])
    on_my_core = (away & 1) == 0
    has_far = (targets >= 0).astype(jnp.int32)
    valid = on_my_core & (targets_both >= 0)
    route_a = jnp.where(valid, index_a, -1)
    route_b = jnp.where(valid, index_b, -1)

    biases = [small]
    for value in slots_a:
        rows3 = value[slab : slab + 3 * small_rows].astype(f32).reshape(3, -1)
        biases.append(rows3[0] + rows3[1] + rows3[2])
    bias_q = jnp.concatenate([b[:hc] for b in biases])
    bias_v = jnp.concatenate([b[hc : 2 * hc] for b in biases])
    bias_one = jnp.concatenate([b[2 * hc : 2 * hc + fc] for b in biases])
    bias_kv = jnp.concatenate([jnp.zeros_like(bias_v), bias_v])
    w_qkv_all, w_out_t = assemble(
        dp_index,
        list(tie(*tables_a)),
        [w_qkv[0], w_qkv[1], w_qkv[2], own_out_t],
        [(t * hc, hc, 0, t * heads_all) for t in range(3)] + [(3 * hc, hc, 1, 0)],
        masks,
        [3 * heads_all, heads_all],
    )
    tie.mark(w_qkv_all, w_out_t)
    strip_f = tie(strip_f)
    slots_f = over_head(strip_f)
    qkv = (mm(normed, w_qkv_all) + jnp.concatenate([bias_q, bias_kv])).astype(bf16)
    tie.mark(qkv)

    kept, passed = far_pick(list(zip(tie(*far_held), far_got)), index_a, index_b)
    tie.mark(kept, passed)
    passed_got = xor_swap(passed, "dp", 1)
    held_f = colors_of(tie(*slots_f))
    got_f = swap_stage(held_f, 0)
    got_cot = sent(cot_out, passed_got)
    passed = passed_got
    for step in range(1, len(masks)):
        held_f = widen(held_f, got_f)
        got_f = swap_stage(held_f, step)
    far = jnp.where(on_my_core[:blocks, None, None], tie(kept), passed).reshape(tokens, model)
    kv_far = (mm(far, w_qkv_all[:, heads_all:]) + bias_kv).astype(bf16)
    tie.mark(kv_far)
    attended = attention_forward(has_far, qkv, tie(kv_far), heads_all)
    tie.mark(attended, *got_cot[1::2])
    residual = joined + (mm_nt(tie(attended), w_out_t) + b_out)
    normed2_f, standard_two, inverse_two = norm_forward(residual, norm2_gain, norm2_shift)
    normed_two = normed2_f.astype(bf16)
    tie.mark(residual, normed_two)

    incoming = in_rank_order(tie(*got_cot))
    incoming_f = incoming.astype(f32)
    grad_b2 = jnp.sum(incoming_f, axis=0, keepdims=True)
    normed_t, far_t = tie(normed).T, tie(far).T
    incoming_t, normed_two_t = incoming.T, tie(normed_two).T
    tie.mark(grad_b2, normed_t, far_t, incoming_t, normed_two_t)
    held_f = widen(held_f, got_f)
    tables_f = held_f + [xor_swap(v, "dp", 1) for v in held_f]

    shape = jax.ShapeDtypeStruct
    slope, out, keep_two, send_two = feed_call(
        feed_forward_kernel,
        masks,
        dp_index,
        tables_f,
        w_fc1,
        own_two_t,
        0,
        [
            (normed_two, None),
            (bias_one.reshape(1, -1), (0, False)),
            (residual, None),
            (b_fc2.reshape(1, -1), None),
            (incoming_t, None),
        ],
        [(shape((tokens, hidden_all), bf16), (1, False)), (shape((tokens, model), bf16), None)],
        [pltpu.VMEM((tokens, model), f32)],
    )
    tie.mark(slope)
    got_two = xor_swap(send_two, "dp", 1)
    out_pieces = from_micro(tie(out))
    tie.mark(*out_pieces)
    got_out = back(out_pieces)

    reversed_bits = [
        sum(m for m, back_m in zip(head_masks, head_masks[::-1]) if p & back_m) for p in range(head_size)
    ]

    class HeadSum:
        def __init__(self, piece):
            self.held = jnp.stack([piece(here ^ p) for p in reversed_bits])
            tie.mark(self.held)
            self.masks = list(head_masks)
            self.send()

        def send(self):
            half = self.held.shape[0] // 2
            self.got = xor_swap(self.held[half:], "head", self.masks.pop(0))

        def step(self):
            tie.pause()
            half = self.held.shape[0] // 2
            total = tie(self.held)[:half].astype(f32) + self.got.astype(f32)
            if half == 1:
                return total[0]
            self.held = total.astype(bf16)
            tie.mark(self.held)
            self.send()
            return None

        def finish(self):
            out = None
            while out is None:
                out = self.step()
            return out

    grad_b1, grad_normed_two, keep_one, send_one = feed_call(
        feed_backward_kernel,
        masks,
        dp_index,
        tables_f,
        own_two_t,
        w_fc1,
        1,
        [(tie(incoming), None), (slope, (1, False)), (normed_two_t, None)],
        [(shape((1, hidden_all), f32), (1, True)), (shape((tokens, model), f32), None)],
        [],
    )
    tie.mark(grad_b1)
    got_one = xor_swap(send_one, "dp", 1)

    def halves(keep, got):
        return [
            DpSum(tie, [v[c * head_size : (c + 1) * head_size] for v in (keep, got)], dp_orders[c])
            for c in range(HALVES)
        ]

    sums_two = halves(keep_two, got_two)
    for part in sums_two:
        part.stage(0)
    grad_res_part, grad_g2, grad_s2 = norm_backward(
        tie(grad_normed_two), standard_two, inverse_two, norm2_gain
    )
    grad_residual = incoming_f + grad_res_part
    grad_branch = grad_residual.astype(bf16)
    grad_bo = jnp.sum(grad_branch.astype(f32), axis=0)
    grad_att = mm(grad_branch, w_out_t).astype(bf16)
    tie.mark(grad_att)
    grad_qkv = attention_backward(has_far, qkv, kv_far, tie(grad_att))
    tie.mark(grad_qkv, *[part.terms[-1] for part in sums_two], *got_out)
    sums_one = halves(keep_one, got_one)
    far_back = (
        mm_nt(tie(grad_qkv)[1, :, heads_all:], w_qkv_all[:, heads_all:])
        .astype(bf16)
        .reshape(blocks, BLOCK, model)
    )
    tie.mark(far_back)
    far_other = xor_swap(far_back, "dp", 1)
    for part in sums_one:
        part.stage(0)
    tie.mark(*tie.last, far_other)
    for step in range(1, len(masks)):
        for c in range(HALVES):
            pair = (sums_two[c], sums_one[c])
            low, high = pair[0].rows >> (step + 1), pair[0].rows >> step
            moved = jnp.concatenate([part.upto(low, high) for part in pair], axis=0)
            tie.mark(moved)
            moved = xor_swap(moved, "dp", dp_orders[c][step])
            for part, value in zip(pair, (moved[:head_size], moved[head_size:])):
                part.terms.append(value)
    layer_out = in_micro_order(tie(*got_out))
    branch_t = tie(grad_branch).T
    tie.mark(layer_out, branch_t)
    tie.pause()
    routed = far_route(tie(far_back), far_other, route_a, route_b, limit)
    tie.mark(*routed)
    terms = [[routed[0]], [routed[2]]]
    for color in range(2):
        axis, mask = stage_lists[color][-1]
        terms[color].append(xor_swap(routed[2 * color + 1], axis, mask))
    keep_att, send_att = attention_weights(
        masks, dp_index, normed_t, far_t, branch_t, tie(grad_qkv), attended, hc
    )
    tie.mark(send_att)
    got_att = xor_swap(send_att, "dp", 1)
    ends_f = [part.final() for part in sums_two + sums_one]
    sum_f = HeadSum(
        lambda a: jnp.stack([lax.dynamic_index_in_dim(v, a, 0, False) for v in ends_f])
    )
    grad_own = mm_nt(tie(grad_qkv)[0], w_qkv_all)
    grad_bq = jnp.sum(tie(grad_qkv)[0, :, :heads_all].astype(f32), axis=0)
    grad_bv = jnp.sum(tie(grad_qkv)[:, :, 2 * heads_all :].astype(f32), axis=(0, 1))
    tie.mark(grad_own, grad_bq, grad_bv)
    for step in range(stages - 2, -1, -1):
        low, high = blocks << step, blocks << (step + 1)
        moved = []
        tie.pause()
        for color in range(2):
            value = sum(t[low:high].astype(f32) for t in tie(*terms[color]))
            moved.append(value.astype(bf16))
        tie.mark(*moved)
        for color in range(2):
            terms[color].append(xor_swap(moved[color], *stage_lists[color][step]))
    groups = 2 * head_size
    sums_att = [
        DpSum(tie, [v[c * groups : (c + 1) * groups] for v in (keep_att, got_att)], dp_orders[c])
        for c in (0, 1)
    ]
    for part in sums_att:
        part.stage(0)
    tie.pause()
    grad_input, grad_up, grad_g1, grad_s1 = leave(
        tie(grad_own), joined, grad_residual, coarse, norm1_gain.reshape(1, -1), *terms
    )

    by_slot = jnp.concatenate([grad_bq.reshape(-1, hc), grad_bv.reshape(-1, hc)], axis=1)
    by_head = jnp.concatenate(
        [choose([by_slot[s] for s in range(head_size)], a ^ here) for a in range(head_size)]
    )
    total = jnp.concatenate(
        [grad_up, grad_g1, grad_s1]
        + [v.reshape(1, -1) for v in (grad_bo, grad_g2, grad_s2)]
        + [grad_b2, grad_b1.reshape(-1, model), by_head.reshape(-1, model)]
    )
    in_pieces = from_micro(tie(grad_input))
    tie.mark(*in_pieces)
    got_input = back(in_pieces)
    for step in range(1, len(masks)):
        tie.pause()
        for part in sums_att:
            part.stage(step)
    tie.pause()
    ends = [part.final().reshape(2, head_size, slab, hc) for part in sums_att]
    sum_att = HeadSum(
        lambda a: jnp.concatenate(
            [lax.dynamic_index_in_dim(v, a ^ here, 1, False) for v in ends], axis=0
        )
    )
    sum_f.step()
    tie.pause()
    got_input = tie(*got_input)
    grad_input = in_micro_order(got_input).astype(f32)
    grad_coarse = jnp.sum(grad_input.reshape(micro, -1, UP, model) * up_gain, axis=2)
    tie.mark(grad_input, grad_coarse)
    sum_att.step()
    for axis, mask in [("dp", m) for m in [1] + masks] + [("head", m) for m in head_masks]:
        total = tie(total)
        tie.mark(total)
        got = xor_swap(total, axis, mask)
        tie.pause()
        total = tie(total) + got
    grad_wf = sum_f.finish()
    grad_wa = sum_att.finish()
    grad_w2 = jnp.concatenate([grad_wf[c].T for c in range(HALVES)], axis=0)
    grad_w1 = jnp.concatenate([grad_wf[HALVES + c] for c in range(HALVES)], axis=1)
    grad_wqkv, grad_wo = grad_wa[:3], grad_wa[3].T
    s_g1, s_s1, s_bo, s_g2, s_s2, s_b2 = [total[UP + i] for i in range(6)]
    hidden_rows = hidden_all // model
    s_b1 = total[UP + 6 : UP + 6 + hidden_rows].reshape(-1)
    by_head = total[UP + 6 + hidden_rows :].reshape(head_size, 2 * hc)
    s_bq, s_bv = by_head[:, :hc].reshape(-1), by_head[:, hc:].reshape(-1)
    return (
        layer_out,
        grad_input,
        grad_coarse,
        total[:UP],
        s_g1,
        s_s1,
        grad_wqkv,
        jnp.stack([s_bq, s_bv]),
        grad_wo,
        s_bo,
        s_g2,
        s_s2,
        grad_w1,
        s_b1,
        grad_w2,
        s_b2,
    )


def solution(mesh):
    rows = P(None, ("dp", "head"), None)
    return jax.shard_map(
        local,
        mesh=mesh,
        in_specs=(
            rows,
            rows,
            rows,
            P(),
            P(),
            P(),
            P(),
            P(None, None, "head"),
            P(None, "head"),
            P("head", None),
            P(),
            P(),
            P(),
            P(None, "head"),
            P("head"),
            P("head", None),
            P(),
        ),
        out_specs=(
            rows,
            rows,
            rows,
            P(),
            P(),
            P(),
            P(None, "dp", "head"),
            P(),
            P("head", "dp"),
            P(),
            P(),
            P(),
            P("dp", "head"),
            P(),
            P("head", "dp"),
            P(),
        ),
        check_vma=False,
    )
```

time: 847 us -> 620 us (0.73)
  matrix products: 167 us -> 24.4 us
  waiting for transfers between devices: 301 us -> 201 us
  Pallas kernels: 75.1 us -> 152 us
  starting transfers between devices: 121 us -> 66.4 us
  local copies, waits for them, and re-layouts: 98.1 us -> 79.9 us
    pallas_call x3 -> x8, Pallas kernels: 43.1 us -> 140 us  [the longest x2 73 us: feed_call(): pl.pallas_call(functools.partial(kernel, masks, n_own, n), grid_spec=pltp...]
    ppermute x51 -> x48, waiting for transfers between devices: 233 us -> 159 us  [xor_swap(): return lax.ppermute(value, axis, [(i, i ^ mask) for i in range(size)])]
    dot_general x16 -> x0, matrix products: 55.6 us -> none  [mm_tn(): lax.dot_general(left, right, (((0,), (0,)), ((), ())), preferred_element_...]
    dot_general x11 -> x3, matrix products: 67.4 us -> 12.4 us  [mm(): return jnp.dot(left, right, preferred_element_type=f32)]
    ppermute x18 -> x0, starting transfers between devices: 43.4 us -> none  [the longest x6 23.8 us: gather_strips(): lax.ppermute(strip, 'head', [((i + s) % head_size, i) for i in range(head...]
    dot_general x6 -> x3, matrix products: 43.9 us -> 12.1 us  [mm_nt(): lax.dot_general(left, right, (((1,), (1,)), ((), ())), preferred_element_...]
    pallas_call x2 -> x1, Pallas kernels: 23.1 us -> 1.52 us  [assemble(): pl.pallas_call(functools.partial(assemble_kernel, columns, len(own), len(...]
    convert_element_type x24 -> x27, other arithmetic: 21.9 us -> 42.5 us  [the longest x18 33.7 us: upto(): total = total.astype(bf16)]
  transfers between devices with their start and end apart: 81 -> 60, of which waited for: 30 -> 27; matrix products, arithmetic and copies ran while one was open for 27% -> 27% of each run, Pallas kernels for 5% -> 19%
where the time goes in v3:
time: 620 us; the launch traced here: 610 us
  waiting for transfers between devices  201 us (32%)
  Pallas kernels  152 us (25%)
  other arithmetic  83.5 us (13%)
  local copies, waits for them, and re-layouts  79.9 us (13%)
  starting transfers between devices  66.4 us (11%)
  matrix products  24.4 us (4%)
    ppermute x48, waiting for transfers between devices, xor_swap(): return lax.ppermute(value, axis, [(i, i ^ mask) for i in range(size)])  159 us
    pallas_call x2, Pallas kernels, feed_call(): pl.pallas_call(functools.partial(kernel, masks, n_own, n), grid_spec=pltp...  73 us
    ppermute x48, starting transfers between devices, xor_swap(): return lax.ppermute(value, axis, [(i, i ^ mask) for i in range(size)])  42.6 us
    ppermute x12, waiting for transfers between devices, send(): lax.ppermute(value, 'head', pairs)  41.9 us
    convert_element_type x18, other arithmetic, upto(): total = total.astype(bf16)  33.7 us
    unnamed x261, local copies, waits for them, and re-layouts  27.8 us
    ppermute x12, starting transfers between devices, send(): lax.ppermute(value, 'head', pairs)  23.7 us
    pallas_call x1, Pallas kernels, attention_backward(): pl.pallas_call(functools.partial(attention_backward_kernel, width // PAIR...  21.7 us
  transfers between devices with their start and end apart: 60, of which 27 were waited for; matrix products, arithmetic and copies ran while one was open for 27% of the time, Pallas kernels for 19%

profile of v3, /device:TPU:0, one launch (start us, length us, event | category | flops | bytes accessed | tf_op | source)
XLA Modules:
  0.0 610.2 jit_solution(14175614855739613068)
XLA Ops:
  29.3 11.3 %collective-permute-done.1 = bf16[2,144,1024]{2,1,0:T(8,128)(2,1)S(1)} collective-permute-done((bf16[2,144,1024]{2,1,0:T(8,128)(2,1)S(1)}, bf16[2,144,1024]{2,1,0:T(8,128)(2,1)S(1)}, u32[]{:S(2)}, u32[]{:S(2)}) %collective-permute-start.1) | collective-permute-done | bytes 589856 | tf_op jit(solution)/shard_map/ppermute | solution.py:27
  54.9 14.7 %collective-permute-done.5 = bf16[2,3,64,1024]{3,2,1,0:T(8,128)(2,1)S(1)} collective-permute-done((bf16[2,3,64,1024]{3,2,1,0:T(8,128)(2,1)S(1)}, bf16[2,3,64,1024]{3,2,1,0:T(8,128)(2,1)S(1)}, u32[]{:S(2)}, u32[]{:S(2)}) %collective-permute-start.5) | collective-permute-done | bytes 786464 | tf_op jit(solution)/shard_map/ppermute | solution.py:27
  70.4 18.4 %collective-permute-done.9.refs_2_ = bf16[240,1024]{1,0:T(8,128)(2,1)S(1)} collective-permute-done((bf16[240,1024]{1,0:T(8,128)(2,1)S(1)}, bf16[240,1024]{1,0:T(8,128)(2,1)S(1)}, u32[]{:S(2)}, u32[]{:S(2)}) %collective-permute-start.9) | collective-permute-done | bytes 491552 | tf_op jit(solution)/shard_map/ppermute | solution.py:732
  93.5 15.7 %collective-permute-done.12 = bf16[6,128,512]{2,1,0:T(8,128)(2,1)S(1)} collective-permute-done((bf16[6,128,512]{2,1,0:T(8,128)(2,1)S(1)}, bf16[6,128,512]{2,1,0:T(8,128)(2,1)S(1)}, u32[]{:S(2)}, u32[]{:S(2)}) %collective-permute-start.12) | collective-permute-done | bytes 786464 | tf_op jit(solution)/shard_map/ppermute | solution.py:27
  114.6 6.9 %add_convert_fusion.own_ref = bf16[768,3072]{1,0:T(8,128)(2,1)} fusion(bf16[768,1024]{1,0:T(8,128)(2,1)S(1)} %get-tuple-element.209, bf16[1024,3072]{1,0:T(8,128)(2,1)S(1)} %get-tuple-element.185, f32[3072]{0:T(1024)S(1)} %get-tuple-element.448), kind=kOutput, calls=%fused_computation | convolution fusion | flops 4836556800 | bytes 12595200 | tf_op jit(solution)/shard_map/dot_general | solution.py:72
  121.5 12.5 %collective-permute-done.13 = bf16[1,128,2048]{2,1,0:T(8,128)(2,1)S(1)} collective-permute-done((bf16[1,128,2048]{2,1,0:T(8,128)(2,1)S(1)}, bf16[1,128,2048]{2,1,0:T(8,128)(2,1)S(1)}, u32[]{:S(2)}, u32[]{:S(2)}) %collective-permute-start.13) | collective-permute-done | bytes 524320 | tf_op jit(solution)/shard_map/ppermute | solution.py:27
  134.1 8.5 %collective-permute-done.16.refs_3_.refs_7_ = bf16[12,128,512]{2,1,0:T(8,128)(2,1)S(1)} collective-permute-done((bf16[12,128,512]{2,1,0:T(8,128)(2,1)S(1)}, bf16[12,128,512]{2,1,0:T(8,128)(2,1)S(1)}, u32[]{:S(2)}, u32[]{:S(2)}) %collective-permute-start.16) | collective-permute-done | bytes 1572896 | tf_op jit(solution)/shard_map/ppermute | solution.py:27
  145.0 6.6 %shard_map.290 = (bf16[6,128,1024]{2,1,0:T(8,128)(2,1)}, bf16[6,128,1024]{2,1,0:T(8,128)(2,1)}) custom-call(s32[12]{0:T(128)} %get-tuple-element.340.where_a, s32[12]{0:T(128)} %get-tuple-element.336.where_b, bf16[12,128,512]{2,1,0:T(8,128)(2,1)} %copy-done.55, bf16[12,128,512]{2,1,0:T(8,128)(2,1)} %copy-done.97, bf16[12,128,512]{2,1,0:T(8,128)(2,1)} %copy-done.56, ...), custom_call_target="tpu_custom_call" | custom-call | flops 68719476736 | bytes 67108864 | tf_op jit(solution)/shard_map/pallas_call | solution.py:441
  163.4 10.5 %collective-permute-done.18 = bf16[1,3,64,2048]{3,2,1,0:T(8,128)(2,1)} collective-permute-done((bf16[1,3,64,2048]{3,2,1,0:T(8,128)(2,1)S(1)}, bf16[1,3,64,2048]{3,2,1,0:T(8,128)(2,1)}, u32[]{:S(2)}, u32[]{:S(2)}) %collective-permute-start.18) | collective-permute-done | bytes 786464 | tf_op jit(solution)/shard_map/ppermute | solution.py:27
  193.2 9.8 %shard_map.291.attended = bf16[768,1024]{1,0:T(8,128)(2,1)S(1)} custom-call(s32[6]{0:T(128)S(1)} %get-tuple-element.343.has_far, bf16[768,3072]{1,0:T(8,128)(2,1)S(1)} %bitcast.263, bf16[768,2048]{1,0:T(8,128)(2,1)S(1)} %add_convert_fusion.1.far_ref), custom_call_target="tpu_custom_call" | custom-call | flops 68719476736 | bytes 67108864 | tf_op jit(solution)/shard_map/pallas_call | solution.py:132
  217.2 7.0 %collective-permute-done.21 = bf16[192,1024]{1,0:T(8,128)(2,1)} collective-permute-done((bf16[192,1024]{1,0:T(8,128)(2,1)}, bf16[192,1024]{1,0:T(8,128)(2,1)}, u32[]{:S(2)}, u32[]{:S(2)}) %collective-permute-start.21) | collective-permute-done | bytes 393248 | tf_op jit(solution)/shard_map/ppermute | solution.py:732
  246.0 38.8 %shard_map.292 = (bf16[768,4096]{1,0:T(8,128)(2,1)}, bf16[768,1024]{1,0:T(8,128)(2,1)}, bf16[8,512,512]{2,1,0:T(8,128)(2,1)}, bf16[8,512,512]{2,1,0:T(8,128)(2,1)}) custom-call(s32[2]{0:T(128)} %copy-done.14, bf16[4,3,64,2048]{3,2,1,0:T(8,128)(2,1)} %constant_dynamic-update-slice_fusion.18.refs_0_.refs_4_, ...), custom_call_target="tpu_custom_call" | custom-call | flops 68719476736 | bytes 67108864 | tf_op jit(solution)/shard_map/pallas_call | solution.py:393
  299.5 34.2 %shard_map.293 = (f32[1,4096]{1,0:T(1,128)}, f32[768,1024]{1,0:T(8,128)}, bf16[8,512,512]{2,1,0:T(8,128)(2,1)}, bf16[8,512,512]{2,1,0:T(8,128)(2,1)}) custom-call(s32[2]{0:T(128)} %copy-done.14, bf16[4,3,64,2048]{3,2,1,0:T(8,128)(2,1)} %constant_dynamic-update-slice_fusion.18.refs_0_.refs_4_, ...), custom_call_target="tpu_custom_call" | custom-call | flops 68719476736 | bytes 67108864 | tf_op jit(solution)/shard_map/pallas_call | solution.py:393
  348.7 21.7 %shard_map.294.grad_own.grad_far = bf16[2,768,3072]{2,1,0:T(8,128)(2,1)S(1)} custom-call(s32[6]{0:T(128)S(1)} %copy-done.9, bf16[768,3072]{1,0:T(8,128)(2,1)S(1)} %bitcast.265, bf16[768,2048]{1,0:T(8,128)(2,1)S(1)} %copy-done.25, bf16[768,1024]{1,0:T(8,128)(2,1)S(1)} %convolution_convert_fusion.grad_ref), custom_call_target="tpu_custom_call" | custom-call | flops 68719476736 | bytes 67108864 | tf_op jit(solution)/shard_map/pallas_call | solution.py:176
  388.7 17.6 %collective-permute-done.35 = bf16[4,256,512]{2,1,0:T(8,128)(2,1)} collective-permute-done((bf16[4,256,512]{2,1,0:T(8,128)(2,1)}, bf16[4,256,512]{2,1,0:T(8,128)(2,1)}, u32[]{:S(2)}, u32[]{:S(2)}) %collective-permute-start.35) | collective-permute-done | bytes 1048608 | tf_op jit(solution)/shard_map/ppermute | solution.py:27
  420.0 10.3 %shard_map.295 = (bf16[12,128,512]{2,1,0:T(8,128)(2,1)S(1)}, bf16[12,128,512]{2,1,0:T(8,128)(2,1)}, bf16[12,128,512]{2,1,0:T(8,128)(2,1)S(1)}, bf16[12,128,512]{2,1,0:T(8,128)(2,1)}) custom-call(s32[12]{0:T(128)S(1)} %get-tuple-element.339.where_a, s32[12]{0:T(128)S(1)} %get-tuple-element.335.where_b, bf16[6,128,1024]{2,1,0:T(8,128)(2,1)S(1)} %bitcast.252, ...), custom_call_target="tpu_custom_call" | custom-call | flops 68719476736 | bytes 67108864 | tf_op jit(solution)/shard_map/pallas_call | solution.py:481
  434.8 17.8 %shard_map.296 = (bf16[16,512,256]{2,1,0:T(8,128)(2,1)S(1)}, bf16[16,512,256]{2,1,0:T(8,128)(2,1)}) custom-call(s32[2]{0:T(128)S(1)} %copy-done.15, bf16[1024,768]{1,0:T(8,128)(2,1)S(1)} %bitcast.249, bf16[1024,768]{1,0:T(8,128)(2,1)S(1)} %bitcast.248, bf16[1024,768]{1,0:T(8,128)(2,1)S(1)} %copy.59.branch_t, bf16[2,768,3072]{2,1,0:T(8,128)(2,1)S(1)} %bitcast.247, ...), custom_call_target="tpu_custom_call" | custom-call | flops 68719476736 | bytes 67108864 | tf_op jit(solution)/shard_map/pallas_call | solution.py:651
  465.1 6.7 %fusion.own_ref = f32[768,1024]{1,0:T(8,128)} fusion(bf16[1024,3072]{1,0:T(8,128)(2,1)S(1)} %bitcast.261, bf16[2,768,3072]{2,1,0:T(8,128)(2,1)S(1)} %bitcast.247), kind=kOutput, calls=%fused_computation.3 | convolution fusion | flops 4831838208 | bytes 14155776 | tf_op jit(solution)/shard_map/dot_general | solution.py:76
  487.4 9.9 %collective-permute-done.43.refs_5_ = bf16[6,128,512]{2,1,0:T(8,128)(2,1)S(1)} collective-permute-done((bf16[6,128,512]{2,1,0:T(8,128)(2,1)S(1)}, bf16[6,128,512]{2,1,0:T(8,128)(2,1)S(1)}, u32[]{:S(2)}, u32[]{:S(2)}) %collective-permute-start.43) | collective-permute-done | bytes 786464 | tf_op jit(solution)/shard_map/ppermute | solution.py:27
  500.6 9.1 %shard_map.297 = (bf16[768,1024]{1,0:T(8,128)(2,1)}, f32[4,1024]{1,0:T(4,128)}, f32[1,1024]{1,0:T(1,128)}, f32[1,1024]{1,0:T(1,128)}) custom-call(f32[768,1024]{1,0:T(8,128)} %fusion.own_ref, f32[768,1024]{1,0:T(8,128)} %copy-done.19, f32[768,1024]{1,0:T(8,128)} %get-tuple-element.334.res_ref, bf16[192,1024]{1,0:T(8,128)(2,1)} %copy-done.26, ...), custom_call_target="tpu_custom_call" | custom-call | flops 68719476736 | bytes 67108864 | tf_op jit(solution)/shard_map/pallas_call | solution.py:536
  515.9 5.7 collective-permute-done.47
  526.5 9.8 %collective-permute-done.49 = bf16[8,128,256]{2,1,0:T(8,128)(2,1)S(1)} collective-permute-done((bf16[8,128,256]{2,1,0:T(8,128)(2,1)S(1)}, bf16[8,128,256]{2,1,0:T(8,128)(2,1)S(1)}, u32[]{:S(2)}, u32[]{:S(2)}) %collective-permute-start.49) | collective-permute-done | bytes 524320 | tf_op jit(solution)/shard_map/ppermute | solution.py:27
  547.4 12.5 %collective-permute-done.45 = bf16[192,1024]{1,0:T(8,128)(2,1)} collective-permute-done((bf16[192,1024]{1,0:T(8,128)(2,1)}, bf16[192,1024]{1,0:T(8,128)(2,1)}, u32[]{:S(2)}, u32[]{:S(2)}) %collective-permute-start.45) | collective-permute-done | bytes 393248 | tf_op jit(solution)/shard_map/ppermute | solution.py:732
  569.4 12.6 %collective-permute-done.52 = bf16[2,4,128,256]{3,2,1,0:T(8,128)(2,1)S(1)} collective-permute-done((bf16[2,4,128,256]{3,2,1,0:T(8,128)(2,1)S(1)}, bf16[2,4,128,256]{3,2,1,0:T(8,128)(2,1)S(1)}, u32[]{:S(2)}, u32[]{:S(2)}) %collective-permute-start.52) | collective-permute-done | bytes 524320 | tf_op jit(solution)/shard_map/ppermute | solution.py:27
  (544 shorter events, 278.6 us)
Async XLA Ops:
  47.0 41.8 %collective-permute-start.9 = (bf16[240,1024]{1,0:T(8,128)(2,1)S(1)}, bf16[240,1024]{1,0:T(8,128)(2,1)S(1)}, u32[]{:S(2)}, u32[]{:S(2)}) collective-permute-start(bf16[240,1024]{1,0:T(8,128)(2,1)S(1)} %get-tuple-element.171), channel_id=1, source_target_pairs={{0,2},{1,3},{2,0},{3,1},{4,6},{5,7},{6,4},{7,5},{8,10},{9,11},{10,... | collective-permute-start | bytes 1474568 | tf_op jit(solution)/shard_map/ppermute | solution.py:732
  69.7 43.2 %collective-permute-start.7 = (bf16[4,3,64,1024]{3,2,1,0:T(8,128)(2,1)S(1)}, bf16[4,3,64,1024]{3,2,1,0:T(8,128)(2,1)S(1)}, u32[]{:S(2)}, u32[]{:S(2)}) collective-permute-start(bf16[4,3,64,1024]{3,2,1,0:T(8,128)(2,1)S(1)} %constant_dynamic-update-slice_fusion.6.refs_1_), channel_id=1, source_target_pairs={{0,4},{4,0},{8,12},{12,8},{16,20},{20,16},{24,28},{28,24},{1,5},{5... | collective-permute-start | bytes 4718600 | tf_op jit(solution)/shard_map/ppermute | solution.py:27
  70.2 42.7 %collective-permute-start.6 = (bf16[4,3,64,1024]{3,2,1,0:T(8,128)(2,1)S(1)}, bf16[4,3,64,1024]{3,2,1,0:T(8,128)(2,1)S(1)}, u32[]{:S(2)}, u32[]{:S(2)}) collective-permute-start(bf16[4,3,64,1024]{3,2,1,0:T(8,128)(2,1)S(1)} %constant_dynamic-update-slice_fusion.4.refs_0_), channel_id=1, source_target_pairs={{0,4},{4,0},{8,12},{12,8},{16,20},{20,16},{24,28},{28,24},{1,5},{5... | collective-permute-start | bytes 4718600 | tf_op jit(solution)/shard_map/ppermute | solution.py:27
  109.3 33.4 %collective-permute-start.16 = (bf16[12,128,512]{2,1,0:T(8,128)(2,1)S(1)}, bf16[12,128,512]{2,1,0:T(8,128)(2,1)S(1)}, u32[]{:S(2)}, u32[]{:S(2)}) collective-permute-start(bf16[12,128,512]{2,1,0:T(8,128)(2,1)S(1)} %constant_dynamic-update-slice_fusion.10.refs_2_.refs_6_), channel_id=1, source_target_pairs={{0,8},{4,12},{8,0},{12,4},{16,24},{20,28},{24,16},{28,20},{1,9},{5... | collective-permute-start | bytes 4718600 | tf_op jit(solution)/shard_map/ppermute | solution.py:27
  110.3 32.4 %collective-permute-start.15 = (bf16[12,128,512]{2,1,0:T(8,128)(2,1)S(1)}, bf16[12,128,512]{2,1,0:T(8,128)(2,1)S(1)}, u32[]{:S(2)}, u32[]{:S(2)}) collective-permute-start(bf16[12,128,512]{2,1,0:T(8,128)(2,1)S(1)} %constant_dynamic-update-slice_fusion.8.refs_0_.refs_4_), channel_id=1, source_target_pairs={{0,16},{4,20},{8,24},{12,28},{16,0},{20,4},{24,8},{28,12},{1,17},{... | collective-permute-start | bytes 4718600 | tf_op jit(solution)/shard_map/ppermute | solution.py:27
  176.0 56.7 %collective-permute-start.24 = (bf16[2,3,64,2048]{3,2,1,0:T(8,128)(2,1)}, bf16[2,3,64,2048]{3,2,1,0:T(8,128)(2,1)}, u32[]{:S(2)}, u32[]{:S(2)}) collective-permute-start(bf16[2,3,64,2048]{3,2,1,0:T(8,128)(2,1)} %constant_dynamic-update-slice_fusion.15), channel_id=1, source_target_pairs={{0,8},{4,12},{8,0},{12,4},{16,24},{20,28},{24,16},{28,20},{1,9},{5... | collective-permute-start | bytes 4718600 | tf_op jit(solution)/shard_map/ppermute | solution.py:27
  179.9 55.6 %collective-permute-start.23 = (bf16[2,3,64,2048]{3,2,1,0:T(8,128)(2,1)}, bf16[2,3,64,2048]{3,2,1,0:T(8,128)(2,1)}, u32[]{:S(2)}, u32[]{:S(2)}) collective-permute-start(bf16[2,3,64,2048]{3,2,1,0:T(8,128)(2,1)} %constant_dynamic-update-slice_fusion.13), channel_id=1, source_target_pairs={{0,16},{4,20},{8,24},{12,28},{16,0},{20,4},{24,8},{28,12},{1,17},{... | collective-permute-start | bytes 4718600 | tf_op jit(solution)/shard_map/ppermute | solution.py:27
  192.1 32.1 %collective-permute-start.21 = (bf16[192,1024]{1,0:T(8,128)(2,1)}, bf16[192,1024]{1,0:T(8,128)(2,1)}, u32[]{:S(2)}, u32[]{:S(2)}) collective-permute-start(bf16[192,1024]{1,0:T(8,128)(2,1)} %get-tuple-element.199), channel_id=1, source_target_pairs={{0,2},{1,3},{2,0},{3,1},{4,6},{5,7},{6,4},{7,5},{8,10},{9,11},{10,... | collective-permute-start | bytes 1179656 | tf_op jit(solution)/shard_map/ppermute | solution.py:732
  287.3 61.1 %collective-permute-start.27 = (bf16[192,1024]{1,0:T(8,128)(2,1)}, bf16[192,1024]{1,0:T(8,128)(2,1)S(1)}, u32[]{:S(2)}, u32[]{:S(2)}) collective-permute-start(bf16[192,1024]{1,0:T(8,128)(2,1)} %get-tuple-element.369), channel_id=1, source_target_pairs={{1,0},{2,1},{3,2},{0,3},{5,4},{6,5},{7,6},{4,7},{9,8},{10,9},{11,1... | collective-permute-start | bytes 1179656 | tf_op jit(solution)/shard_map/ppermute | solution.py:732
  289.4 81.1 %collective-permute-start.28 = (bf16[192,1024]{1,0:T(8,128)(2,1)}, bf16[192,1024]{1,0:T(8,128)(2,1)}, u32[]{:S(2)}, u32[]{:S(2)}) collective-permute-start(bf16[192,1024]{1,0:T(8,128)(2,1)} %get-tuple-element.368), channel_id=1, source_target_pairs={{2,0},{3,1},{0,2},{1,3},{6,4},{7,5},{4,6},{5,7},{10,8},{11,9},{8,1... | collective-permute-start | bytes 1179656 | tf_op jit(solution)/shard_map/ppermute | solution.py:732
  293.4 77.1 %collective-permute-start.29 = (bf16[192,1024]{1,0:T(8,128)(2,1)}, bf16[192,1024]{1,0:T(8,128)(2,1)}, u32[]{:S(2)}, u32[]{:S(2)}) collective-permute-start(bf16[192,1024]{1,0:T(8,128)(2,1)} %get-tuple-element.367), channel_id=1, source_target_pairs={{3,0},{0,1},{1,2},{2,3},{7,4},{4,5},{5,6},{6,7},{11,8},{8,9},{9,10... | collective-permute-start | bytes 1179656 | tf_op jit(solution)/shard_map/ppermute | solution.py:732
  299.5 34.8 %collective-permute-start.30 = (bf16[8,512,512]{2,1,0:T(8,128)(2,1)S(1)}, bf16[8,512,512]{2,1,0:T(8,128)(2,1)}, u32[]{:S(2)}, u32[]{:S(2)}) collective-permute-start(bf16[8,512,512]{2,1,0:T(8,128)(2,1)S(1)} %copy-done.95), channel_id=1, source_target_pairs={{0,4},{4,0},{8,12},{12,8},{16,20},{20,16},{24,28},{28,24},{1,5},{5... | collective-permute-start | bytes 12582920 | tf_op jit(solution)/shard_map/ppermute | solution.py:27
  333.7 44.2 %collective-permute-start.33 = (bf16[8,512,512]{2,1,0:T(8,128)(2,1)}, bf16[8,512,512]{2,1,0:T(8,128)(2,1)}, u32[]{:S(2)}, u32[]{:S(2)}) collective-permute-start(bf16[8,512,512]{2,1,0:T(8,128)(2,1)} %get-tuple-element.228), channel_id=1, source_target_pairs={{0,4},{4,0},{8,12},{12,8},{16,20},{20,16},{24,28},{28,24},{1,5},{5... | collective-permute-start | bytes 12582920 | tf_op jit(solution)/shard_map/ppermute | solution.py:27
  337.9 32.6 %collective-permute-start.32 = (bf16[4,256,512]{2,1,0:T(8,128)(2,1)S(1)}, bf16[4,256,512]{2,1,0:T(8,128)(2,1)S(1)}, u32[]{:S(2)}, u32[]{:S(2)}) collective-permute-start(bf16[4,256,512]{2,1,0:T(8,128)(2,1)S(1)} %add_convert_fusion.8), channel_id=1, source_target_pairs={{0,16},{4,20},{8,24},{12,28},{16,0},{20,4},{24,8},{28,12},{1,17},{... | collective-permute-start | bytes 3145736 | tf_op jit(solution)/shard_map/ppermute | solution.py:27
  409.0 46.1 %collective-permute-start.37 = (bf16[8,128,512]{2,1,0:T(8,128)(2,1)}, bf16[8,128,512]{2,1,0:T(8,128)(2,1)}, u32[]{:S(2)}, u32[]{:S(2)}) collective-permute-start(bf16[8,128,512]{2,1,0:T(8,128)(2,1)} %pad_maximum_fusion.5), channel_id=1, source_target_pairs={{0,16},{4,20},{8,24},{12,28},{16,0},{20,4},{24,8},{28,12},{1,17},{... | collective-permute-start | bytes 3145736 | tf_op jit(solution)/shard_map/ppermute | solution.py:27
  413.9 43.0 %collective-permute-start.38 = (bf16[8,128,512]{2,1,0:T(8,128)(2,1)}, bf16[8,128,512]{2,1,0:T(8,128)(2,1)}, u32[]{:S(2)}, u32[]{:S(2)}) collective-permute-start(bf16[8,128,512]{2,1,0:T(8,128)(2,1)} %pad_maximum_fusion.6), channel_id=1, source_target_pairs={{0,8},{4,12},{8,0},{12,4},{16,24},{20,28},{24,16},{28,20},{1,9},{5... | collective-permute-start | bytes 3145736 | tf_op jit(solution)/shard_map/ppermute | solution.py:27
  432.6 42.8 %collective-permute-start.40 = (bf16[12,128,512]{2,1,0:T(8,128)(2,1)}, bf16[12,128,512]{2,1,0:T(8,128)(2,1)}, u32[]{:S(2)}, u32[]{:S(2)}) collective-permute-start(bf16[12,128,512]{2,1,0:T(8,128)(2,1)} %get-tuple-element.244), channel_id=1, source_target_pairs={{0,8},{4,12},{8,0},{12,4},{16,24},{20,28},{24,16},{28,20},{1,9},{5... | collective-permute-start | bytes 4718600 | tf_op jit(solution)/shard_map/ppermute | solution.py:27
  433.7 41.7 %collective-permute-start.39 = (bf16[12,128,512]{2,1,0:T(8,128)(2,1)}, bf16[12,128,512]{2,1,0:T(8,128)(2,1)}, u32[]{:S(2)}, u32[]{:S(2)}) collective-permute-start(bf16[12,128,512]{2,1,0:T(8,128)(2,1)} %get-tuple-element.242), channel_id=1, source_target_pairs={{0,16},{4,20},{8,24},{12,28},{16,0},{20,4},{24,8},{28,12},{1,17},{... | collective-permute-start | bytes 4718600 | tf_op jit(solution)/shard_map/ppermute | solution.py:27
  475.3 67.3 %collective-permute-start.51 = (bf16[2,4,128,512]{3,2,1,0:T(8,128)(2,1)}, bf16[2,4,128,512]{3,2,1,0:T(8,128)(2,1)}, u32[]{:S(2)}, u32[]{:S(2)}) collective-permute-start(bf16[2,4,128,512]{3,2,1,0:T(8,128)(2,1)} %pad_maximum_fusion.8), channel_id=1, source_target_pairs={{0,1},{1,0},{2,3},{3,2},{4,5},{5,4},{6,7},{7,6},{8,9},{9,8},{10,11... | collective-permute-start | bytes 3145736 | tf_op jit(solution)/shard_map/ppermute | solution.py:27
  482.7 38.8 %collective-permute-start.47 = (bf16[8,256,256]{2,1,0:T(8,128)(2,1)}, bf16[8,256,256]{2,1,0:T(8,128)(2,1)}, u32[]{:S(2)}, u32[]{:S(2)}) collective-permute-start(bf16[8,256,256]{2,1,0:T(8,128)(2,1)} %add_convert_fusion.5), channel_id=1, source_target_pairs={{0,8},{4,12},{8,0},{12,4},{16,24},{20,28},{24,16},{28,20},{1,9},{5... | collective-permute-start | bytes 3145736 | tf_op jit(solution)/shard_map/ppermute | solution.py:27
  486.3 38.0 %collective-permute-start.48 = (bf16[8,256,256]{2,1,0:T(8,128)(2,1)}, bf16[8,256,256]{2,1,0:T(8,128)(2,1)}, u32[]{:S(2)}, u32[]{:S(2)}) collective-permute-start(bf16[8,256,256]{2,1,0:T(8,128)(2,1)} %add_convert_fusion.4), channel_id=1, source_target_pairs={{0,16},{4,20},{8,24},{12,28},{16,0},{20,4},{24,8},{28,12},{1,17},{... | collective-permute-start | bytes 3145736 | tf_op jit(solution)/shard_map/ppermute | solution.py:27
  512.2 35.2 %collective-permute-start.44 = (bf16[192,1024]{1,0:T(8,128)(2,1)}, bf16[192,1024]{1,0:T(8,128)(2,1)S(1)}, u32[]{:S(2)}, u32[]{:S(2)}) collective-permute-start(bf16[192,1024]{1,0:T(8,128)(2,1)} %get-tuple-element.361), channel_id=1, source_target_pairs={{1,0},{2,1},{3,2},{0,3},{5,4},{6,5},{7,6},{4,7},{9,8},{10,9},{11,1... | collective-permute-start | bytes 1179656 | tf_op jit(solution)/shard_map/ppermute | solution.py:732
  514.0 45.9 %collective-permute-start.45 = (bf16[192,1024]{1,0:T(8,128)(2,1)}, bf16[192,1024]{1,0:T(8,128)(2,1)}, u32[]{:S(2)}, u32[]{:S(2)}) collective-permute-start(bf16[192,1024]{1,0:T(8,128)(2,1)} %get-tuple-element.360), channel_id=1, source_target_pairs={{2,0},{3,1},{0,2},{1,3},{6,4},{7,5},{4,6},{5,7},{10,8},{11,9},{8,1... | collective-permute-start | bytes 1179656 | tf_op jit(solution)/shard_map/ppermute | solution.py:732
  545.6 36.7 %collective-permute-start.59 = (bf16[1,4,128,512]{3,2,1,0:T(8,128)(2,1)}, bf16[1,4,128,512]{3,2,1,0:T(8,128)(2,1)}, u32[]{:S(2)}, u32[]{:S(2)}) collective-permute-start(bf16[1,4,128,512]{3,2,1,0:T(8,128)(2,1)} %slice.721), channel_id=1, source_target_pairs={{0,2},{1,3},{2,0},{3,1},{4,6},{5,7},{6,4},{7,5},{8,10},{9,11},{10,... | collective-permute-start | bytes 1572872 | tf_op jit(solution)/shard_map/ppermute | solution.py:27
  (150 other events, 1954.3 us)

commit v4 on v3

--- a/solution.py
+++ b/solution.py
@@ -13,6 +13,7 @@
 UP = 4
 HALVES = 2
 VMEM_LIMIT = 58 << 20
+STEPS = ["tokens_out", "feed", "two_first", "norm", "attention", "wait_two", "far_back", "one_first", "pause", "hidden_rest", "branch", "pause", "route", "weights", "hidden_head", "own", "pause", "far_rest", "att_first", "layer", "pause", "leave", "att_rest", "small", "tokens_back", "pause", "pause", "hidden_step", "att_head", "tokens_end", "pause", "att_step", "small_step", "small_end"]
 PAIR = 2 * HEAD_DIM
 NEGATIVE = -1e30
 epsilon = 1e-05
@@ -42,6 +43,11 @@
 
     def mark(self, *values):
         self.last = values
+
+    def flush(self):
+        tied = self(jnp.zeros((8, 128), f32) if self.token is None else self.token)
+        self.token = xor_swap(tied, "dp", 1)
+        self.mark(self.token)
 
     def pause(self):
         self.token = self(jnp.zeros((8, 128), f32) if self.token is None else self.token)
@@ -235,11 +241,12 @@
 
 
 def fill_chunk(masks, me, tables, out_ref):
-    half = tables[0].shape[2]
+    half, count = tables[0].shape[2], tables[0].shape[0]
     for which, table in enumerate(tables):
-        order = masks if which % 2 == 0 else masks[::-1]
-        for k, mask in enumerate(relative_masks(order)):
-            row = (me ^ (mask | (which // 2))) * 2 * half + (which % 2) * half
+        core, color, late = which // 4, which // 2 % 2, which % 2
+        order = masks if color == 0 else masks[::-1]
+        for k, mask in enumerate(relative_masks(order)[late * count : (late + 1) * count]):
+            row = (me ^ (mask | core)) * 2 * half + color * half
             out_ref[pl.ds(pl.multiple_of(row, half), half), :] = table[k, 0]
 
 
@@ -284,10 +291,10 @@
 
 
 def feed_forward_kernel(masks, n_own, n, me, *refs):
-    one_tables, two_tables = refs[:4], refs[4:8]
-    (own_one, own_two, x_ref, bias_ref, residual_ref, last_ref, left_ref) = refs[8:15]
-    slope_ref, out_ref, keep_ref, send_ref = refs[15:19]
-    w_one, w_two, even_ref, odd_ref, act_ref, held_ref, acc_ref = refs[19:]
+    one_tables, two_tables, refs = refs[:8], refs[8:16], refs[16:]
+    (own_one, own_two, x_ref, bias_ref, residual_ref, last_ref, left_ref) = refs[:7]
+    slope_ref, out_ref, keep_ref, send_ref = refs[7:11]
+    w_one, w_two, even_ref, odd_ref, act_ref, held_ref, acc_ref = refs[11:]
     step = pl.program_id(0)
     load_chunk(masks, me[0], jnp.minimum(step, n - 1), n_own, own_one, one_tables, w_one)
     load_chunk(masks, me[0], jnp.maximum(step - 1, 0), n_own, own_two, two_tables, w_two)
@@ -322,10 +329,10 @@
 
 
 def feed_backward_kernel(masks, n_own, n, me, *refs):
-    two_tables, one_tables = refs[:4], refs[4:8]
-    own_two, own_one, g_ref, slope_ref, left_ref = refs[8:13]
-    bias_ref, out_ref, keep_ref, send_ref = refs[13:17]
-    w_two, w_one, even_ref, odd_ref, grad_ref, held_ref = refs[17:]
+    two_tables, one_tables, refs = refs[:8], refs[8:16], refs[16:]
+    own_two, own_one, g_ref, slope_ref, left_ref = refs[:5]
+    bias_ref, out_ref, keep_ref, send_ref = refs[5:9]
+    w_two, w_one, even_ref, odd_ref, grad_ref, held_ref = refs[9:]
     step = pl.program_id(0)
     load_chunk(masks, me[0], jnp.minimum(step, n - 1), n_own, own_two, two_tables, w_two)
     load_chunk(masks, me[0], jnp.maximum(step - 1, 0), n_own, own_one, one_tables, w_one)
@@ -395,8 +402,8 @@
         grid_spec=pltpu.PrefetchScalarGridSpec(
             num_scalar_prefetch=1,
             grid=(n + 1,),
-            in_specs=[table_spec(first_part, 0)] * 4
-            + [table_spec(1 - first_part, 1)] * 4
+            in_specs=[table_spec(first_part, 0)] * 8
+            + [table_spec(1 - first_part, 1)] * 8
             + [own_spec(0), own_spec(1)]
             + [spec(a, lag) for a, lag in arrays],
             out_specs=[spec(o, lag) for o, lag in outs] + [weight_spec, weight_spec],
@@ -669,22 +676,23 @@
 
 
 class DpSum:
-    def __init__(self, tie, terms, order):
-        self.tie, self.terms, self.order = tie, list(terms), order
-        self.rows = terms[0].shape[1]
+    def __init__(self, tie, terms, order, group, count):
+        self.tie, self.order = tie, order
+        self.terms = [(value, group) for value in terms]
+        self.count, self.rows = count, terms[0].shape[1]
 
     def upto(self, low, high):
-        first, *others = self.terms
-        total = self.tie(first)[:, low:high].astype(f32)
-        for value in others:
-            total = total + value[:, low:high].astype(f32)
+        values = self.tie(*[value for value, _ in self.terms])
+        total = 0.0
+        for value, (_, group) in zip(values, self.terms):
+            total = total + value[group : group + self.count, low:high].astype(f32)
         total = total.astype(bf16)
         self.tie.mark(total)
         return total
 
     def stage(self, step):
         sent = self.upto(self.rows >> (step + 1), self.rows >> step)
-        self.terms.append(xor_swap(sent, "dp", self.order[step]))
+        self.terms.append((xor_swap(sent, "dp", self.order[step]), 0))
 
     def final(self):
         return self.upto(0, self.rows >> len(self.order))
@@ -789,20 +797,40 @@
     for mask in head_masks[::-1]:
         head_places = head_places + [p ^ mask for p in head_places]
 
-    def over_head(strip):
-        held = strip[None]
-        for mask in head_masks[::-1]:
-            held = jnp.concatenate([held, xor_swap(held, "head", mask)], axis=0)
-        return [held[head_places.index(s)] for s in range(1, head_size)]
-
-    slots_a = over_head(strip_a)
+    class HeadGather:
+        def __init__(self, strip):
+            self.held, self.masks = strip[None], head_masks[::-1]
+            self.send()
+
+        def send(self):
+            self.got = xor_swap(self.held, "head", self.masks.pop(0))
+
+        def step(self):
+            self.held = jnp.concatenate([tie(self.held), self.got], axis=0)
+            tie.mark(self.held)
+            if self.masks:
+                self.send()
+                return True
+            return False
+
+        def slots(self):
+            while self.step():
+                tie.pause()
+            return [self.held[head_places.index(s)] for s in range(1, head_size)]
+
+    gather_a = HeadGather(strip_a)
+    acts_out = to_micro(tie(jnp.concatenate([activations, conditioning], axis=1)))
+    tie.mark(*acts_out)
+    tie.pause()
+    gather_a.step()
     strip_f = jnp.concatenate([my_slab(tie(w_fc1), 0), my_slab(w_fc2, 1).T], axis=1)
     own_two_t = tie(w_fc2).T
     own_out_t = tie(w_out).T
     up_tile = jnp.broadcast_to(tie(up_gain)[None], (rows // UP, UP, model)).reshape(rows, model)
-    acts_out = to_micro(tie(jnp.concatenate([activations, conditioning], axis=1)))
     cot_out = to_micro(tie(cotangent))
-    tie.mark(strip_f, own_two_t, own_out_t, up_tile, *acts_out, *cot_out)
+    tie.mark(strip_f, own_two_t, own_out_t, up_tile, *cot_out)
+    tie.pause()
+    slots_a = gather_a.slots()
     dp_orders = (masks, masks[::-1])
     dp_index = jnp.stack([me, here]).astype(jnp.int32)
 
@@ -826,8 +854,10 @@
     got_a = swap_stage(held_a, 0)
     got_acts = sent(acts_out, *held_a)
     for step in range(1, len(masks)):
+        tie.pause()
         held_a = widen(held_a, got_a)
         got_a = swap_stage(held_a, step)
+    tie.pause()
     held_a = widen(held_a, got_a)
     tables_a = held_a + [xor_swap(v, "dp", 1) for v in held_a]
     joined, normed, coarse = join(
@@ -846,9 +876,12 @@
     far_held = [shaped[:, :, c * half : (c + 1) * half] for c in (0, 1)]
     tie.mark(*far_held)
     far_got = [xor_swap(v, *stage_lists[c][0]) for c, v in enumerate(far_held)]
+    gather_f = HeadGather(tie(strip_f))
     for step in range(1, stages):
+        tie.pause()
         far_held = widen(far_held, far_got)
         far_got = [xor_swap(v, *stage_lists[c][step]) for c, v in enumerate(far_held)]
+    gather_f.step()
     limit = far_held[0].shape[0]
     table_row = lax.dynamic_index_in_dim(block_targets, my_micro, 0, False)
 
@@ -892,19 +925,20 @@
         [3 * heads_all, heads_all],
     )
     tie.mark(w_qkv_all, w_out_t)
-    strip_f = tie(strip_f)
-    slots_f = over_head(strip_f)
     qkv = (mm(normed, w_qkv_all) + jnp.concatenate([bias_q, bias_kv])).astype(bf16)
     tie.mark(qkv)
 
+    tie.pause()
     kept, passed = far_pick(list(zip(tie(*far_held), far_got)), index_a, index_b)
     tie.mark(kept, passed)
     passed_got = xor_swap(passed, "dp", 1)
-    held_f = colors_of(tie(*slots_f))
+    tie.pause()
+    held_f = colors_of(gather_f.slots())
     got_f = swap_stage(held_f, 0)
     got_cot = sent(cot_out, passed_got)
     passed = passed_got
     for step in range(1, len(masks)):
+        tie.pause()
         held_f = widen(held_f, got_f)
         got_f = swap_stage(held_f, step)
     far = jnp.where(on_my_core[:blocks, None, None], tie(kept), passed).reshape(tokens, model)
@@ -923,8 +957,12 @@
     normed_t, far_t = tie(normed).T, tie(far).T
     incoming_t, normed_two_t = incoming.T, tie(normed_two).T
     tie.mark(grad_b2, normed_t, far_t, incoming_t, normed_two_t)
-    held_f = widen(held_f, got_f)
-    tables_f = held_f + [xor_swap(v, "dp", 1) for v in held_f]
+    tie.pause()
+    got_f = list(tie(*got_f))
+    tables_f = [v for pair in zip(held_f, got_f) for v in pair]
+    held_core = [xor_swap(v, "dp", 1) for v in held_f]
+    got_core = [xor_swap(v, "dp", 1) for v in got_f]
+    tables_f += [v for pair in zip(held_core, got_core) for v in pair]
 
     shape = jax.ShapeDtypeStruct
     slope, out, keep_two, send_two = feed_call(
@@ -947,9 +985,6 @@
     )
     tie.mark(slope)
     got_two = xor_swap(send_two, "dp", 1)
-    out_pieces = from_micro(tie(out))
-    tie.mark(*out_pieces)
-    got_out = back(out_pieces)
 
     reversed_bits = [
         sum(m for m, back_m in zip(head_masks, head_masks[::-1]) if p & back_m) for p in range(head_size)
@@ -967,7 +1002,6 @@
             self.got = xor_swap(self.held[half:], "head", self.masks.pop(0))
 
         def step(self):
-            tie.pause()
             half = self.held.shape[0] // 2
             total = tie(self.held)[:half].astype(f32) + self.got.astype(f32)
             if half == 1:
@@ -983,143 +1017,233 @@
                 out = self.step()
             return out
 
-    grad_b1, grad_normed_two, keep_one, send_one = feed_call(
-        feed_backward_kernel,
-        masks,
-        dp_index,
-        tables_f,
-        own_two_t,
-        w_fc1,
-        1,
-        [(tie(incoming), None), (slope, (1, False)), (normed_two_t, None)],
-        [(shape((1, hidden_all), f32), (1, True)), (shape((tokens, model), f32), None)],
-        [],
-    )
-    tie.mark(grad_b1)
-    got_one = xor_swap(send_one, "dp", 1)
-
-    def halves(keep, got):
-        return [
-            DpSum(tie, [v[c * head_size : (c + 1) * head_size] for v in (keep, got)], dp_orders[c])
-            for c in range(HALVES)
-        ]
-
-    sums_two = halves(keep_two, got_two)
-    for part in sums_two:
-        part.stage(0)
-    grad_res_part, grad_g2, grad_s2 = norm_backward(
-        tie(grad_normed_two), standard_two, inverse_two, norm2_gain
-    )
-    grad_residual = incoming_f + grad_res_part
-    grad_branch = grad_residual.astype(bf16)
-    grad_bo = jnp.sum(grad_branch.astype(f32), axis=0)
-    grad_att = mm(grad_branch, w_out_t).astype(bf16)
-    tie.mark(grad_att)
-    grad_qkv = attention_backward(has_far, qkv, kv_far, tie(grad_att))
-    tie.mark(grad_qkv, *[part.terms[-1] for part in sums_two], *got_out)
-    sums_one = halves(keep_one, got_one)
-    far_back = (
-        mm_nt(tie(grad_qkv)[1, :, heads_all:], w_qkv_all[:, heads_all:])
-        .astype(bf16)
-        .reshape(blocks, BLOCK, model)
-    )
-    tie.mark(far_back)
-    far_other = xor_swap(far_back, "dp", 1)
-    for part in sums_one:
-        part.stage(0)
-    tie.mark(*tie.last, far_other)
-    for step in range(1, len(masks)):
-        for c in range(HALVES):
-            pair = (sums_two[c], sums_one[c])
-            low, high = pair[0].rows >> (step + 1), pair[0].rows >> step
-            moved = jnp.concatenate([part.upto(low, high) for part in pair], axis=0)
-            tie.mark(moved)
-            moved = xor_swap(moved, "dp", dp_orders[c][step])
-            for part, value in zip(pair, (moved[:head_size], moved[head_size:])):
-                part.terms.append(value)
-    layer_out = in_micro_order(tie(*got_out))
-    branch_t = tie(grad_branch).T
-    tie.mark(layer_out, branch_t)
-    tie.pause()
-    routed = far_route(tie(far_back), far_other, route_a, route_b, limit)
-    tie.mark(*routed)
-    terms = [[routed[0]], [routed[2]]]
-    for color in range(2):
-        axis, mask = stage_lists[color][-1]
-        terms[color].append(xor_swap(routed[2 * color + 1], axis, mask))
-    keep_att, send_att = attention_weights(
-        masks, dp_index, normed_t, far_t, branch_t, tie(grad_qkv), attended, hc
-    )
-    tie.mark(send_att)
-    got_att = xor_swap(send_att, "dp", 1)
-    ends_f = [part.final() for part in sums_two + sums_one]
-    sum_f = HeadSum(
-        lambda a: jnp.stack([lax.dynamic_index_in_dim(v, a, 0, False) for v in ends_f])
-    )
-    grad_own = mm_nt(tie(grad_qkv)[0], w_qkv_all)
-    grad_bq = jnp.sum(tie(grad_qkv)[0, :, :heads_all].astype(f32), axis=0)
-    grad_bv = jnp.sum(tie(grad_qkv)[:, :, 2 * heads_all :].astype(f32), axis=(0, 1))
-    tie.mark(grad_own, grad_bq, grad_bv)
-    for step in range(stages - 2, -1, -1):
-        low, high = blocks << step, blocks << (step + 1)
-        moved = []
-        tie.pause()
-        for color in range(2):
-            value = sum(t[low:high].astype(f32) for t in tie(*terms[color]))
-            moved.append(value.astype(bf16))
-        tie.mark(*moved)
-        for color in range(2):
-            terms[color].append(xor_swap(moved[color], *stage_lists[color][step]))
-    groups = 2 * head_size
-    sums_att = [
-        DpSum(tie, [v[c * groups : (c + 1) * groups] for v in (keep_att, got_att)], dp_orders[c])
-        for c in (0, 1)
-    ]
-    for part in sums_att:
-        part.stage(0)
-    tie.pause()
-    grad_input, grad_up, grad_g1, grad_s1 = leave(
-        tie(grad_own), joined, grad_residual, coarse, norm1_gain.reshape(1, -1), *terms
-    )
-
-    by_slot = jnp.concatenate([grad_bq.reshape(-1, hc), grad_bv.reshape(-1, hc)], axis=1)
-    by_head = jnp.concatenate(
-        [choose([by_slot[s] for s in range(head_size)], a ^ here) for a in range(head_size)]
-    )
-    total = jnp.concatenate(
-        [grad_up, grad_g1, grad_s1]
-        + [v.reshape(1, -1) for v in (grad_bo, grad_g2, grad_s2)]
-        + [grad_b2, grad_b1.reshape(-1, model), by_head.reshape(-1, model)]
-    )
-    in_pieces = from_micro(tie(grad_input))
-    tie.mark(*in_pieces)
-    got_input = back(in_pieces)
-    for step in range(1, len(masks)):
-        tie.pause()
-        for part in sums_att:
-            part.stage(step)
-    tie.pause()
-    ends = [part.final().reshape(2, head_size, slab, hc) for part in sums_att]
-    sum_att = HeadSum(
-        lambda a: jnp.concatenate(
-            [lax.dynamic_index_in_dim(v, a ^ here, 1, False) for v in ends], axis=0
-        )
-    )
-    sum_f.step()
-    tie.pause()
-    got_input = tie(*got_input)
-    grad_input = in_micro_order(got_input).astype(f32)
-    grad_coarse = jnp.sum(grad_input.reshape(micro, -1, UP, model) * up_gain, axis=2)
-    tie.mark(grad_input, grad_coarse)
-    sum_att.step()
-    for axis, mask in [("dp", m) for m in [1] + masks] + [("head", m) for m in head_masks]:
-        total = tie(total)
-        tie.mark(total)
-        got = xor_swap(total, axis, mask)
-        tie.pause()
-        total = tie(total) + got
-    grad_wf = sum_f.finish()
-    grad_wa = sum_att.finish()
+    class Steps:
+        def tokens_out(self):
+            out_pieces = from_micro(tie(out))
+            tie.mark(*out_pieces)
+            self.got_out = back(out_pieces)
+
+        def feed(self):
+            self.grad_b1, self.grad_two, self.keep_one, self.send_one = feed_call(
+                feed_backward_kernel,
+                masks,
+                dp_index,
+                tables_f,
+                own_two_t,
+                w_fc1,
+                1,
+                [(tie(incoming), None), (slope, (1, False)), (normed_two_t, None)],
+                [(shape((1, hidden_all), f32), (1, True)), (shape((tokens, model), f32), None)],
+                [],
+            )
+            tie.mark(self.grad_b1)
+            self.got_one = xor_swap(self.send_one, "dp", 1)
+
+        def halves(self, keep, got):
+            return [
+                DpSum(tie, (keep, got), dp_orders[c], c * head_size, head_size)
+                for c in range(HALVES)
+            ]
+
+        def two_first(self):
+            self.sums_two = self.halves(keep_two, got_two)
+            for part in self.sums_two:
+                part.stage(0)
+
+        def norm(self):
+            grad_res_part, self.grad_g2, self.grad_s2 = norm_backward(
+                tie(self.grad_two), standard_two, inverse_two, norm2_gain
+            )
+            self.grad_residual = incoming_f + grad_res_part
+            self.grad_branch = self.grad_residual.astype(bf16)
+            self.grad_bo = jnp.sum(self.grad_branch.astype(f32), axis=0)
+            self.grad_att = mm(self.grad_branch, w_out_t).astype(bf16)
+            tie.mark(self.grad_att)
+
+        def attention(self):
+            self.grad_qkv = attention_backward(has_far, qkv, kv_far, tie(self.grad_att))
+            tie.mark(self.grad_qkv)
+
+        def one_first(self):
+            self.sums_one = self.halves(self.keep_one, self.got_one)
+            for part in self.sums_one:
+                part.stage(0)
+
+        def far_back(self):
+            self.far_rows = (
+                mm_nt(tie(self.grad_qkv)[1, :, heads_all:], w_qkv_all[:, heads_all:])
+                .astype(bf16)
+                .reshape(blocks, BLOCK, model)
+            )
+            tie.mark(self.far_rows)
+            self.far_other = xor_swap(self.far_rows, "dp", 1)
+
+        def branch(self):
+            self.branch_t = tie(self.grad_branch).T
+            tie.mark(self.branch_t)
+
+        def route(self):
+            routed = far_route(tie(self.far_rows), self.far_other, route_a, route_b, limit)
+            tie.mark(*routed)
+            self.terms = [[routed[0]], [routed[2]]]
+            for color in range(2):
+                axis, mask = stage_lists[color][-1]
+                self.terms[color].append(xor_swap(routed[2 * color + 1], axis, mask))
+
+        def weights(self):
+            keep, send_att = attention_weights(
+                masks, dp_index, normed_t, far_t, self.branch_t, tie(self.grad_qkv), attended, hc
+            )
+            tie.mark(send_att)
+            got = xor_swap(send_att, "dp", 1)
+            groups = 2 * head_size
+            self.sums_att = [
+                DpSum(tie, (keep, got), dp_orders[c], c * groups, groups) for c in (0, 1)
+            ]
+
+        def own(self):
+            self.grad_own = mm_nt(tie(self.grad_qkv)[0], w_qkv_all)
+            self.grad_bq = jnp.sum(tie(self.grad_qkv)[0, :, :heads_all].astype(f32), axis=0)
+            self.grad_bv = jnp.sum(
+                tie(self.grad_qkv)[:, :, 2 * heads_all :].astype(f32), axis=(0, 1)
+            )
+            tie.mark(self.grad_own, self.grad_bq, self.grad_bv)
+
+        def hidden_rest(self):
+            for step in range(1, len(masks)):
+                for c in range(HALVES):
+                    pair = (self.sums_two[c], self.sums_one[c])
+                    low, high = pair[0].rows >> (step + 1), pair[0].rows >> step
+                    moved = jnp.concatenate([part.upto(low, high) for part in pair], axis=0)
+                    tie.mark(moved)
+                    moved = xor_swap(moved, "dp", dp_orders[c][step])
+                    for i, part in enumerate(pair):
+                        part.terms.append((moved, i * head_size))
+
+        def hidden_head(self):
+            ends = [part.final() for part in self.sums_two + self.sums_one]
+            self.sum_f = HeadSum(
+                lambda a: jnp.stack([lax.dynamic_index_in_dim(v, a, 0, False) for v in ends])
+            )
+
+        def hidden_step(self):
+            self.sum_f.step()
+
+        def far_rest(self):
+            for step in range(stages - 2, -1, -1):
+                low, high = blocks << step, blocks << (step + 1)
+                moved = []
+                for color in range(2):
+                    value = sum(t[low:high].astype(f32) for t in tie(*self.terms[color]))
+                    moved.append(value.astype(bf16))
+                tie.mark(*moved)
+                for color in range(2):
+                    self.terms[color].append(xor_swap(moved[color], *stage_lists[color][step]))
+
+        def att_first(self):
+            for part in self.sums_att:
+                part.stage(0)
+
+        def att_rest(self):
+            for step in range(1, len(masks)):
+                for part in self.sums_att:
+                    part.stage(step)
+
+        def att_head(self):
+            ends = [part.final().reshape(2, head_size, slab, hc) for part in self.sums_att]
+            self.sum_att = HeadSum(
+                lambda a: jnp.concatenate(
+                    [lax.dynamic_index_in_dim(v, a ^ here, 1, False) for v in ends], axis=0
+                )
+            )
+
+        def att_step(self):
+            self.sum_att.step()
+
+        def leave(self):
+            self.grad_input, self.grad_up, self.grad_g1, self.grad_s1 = leave(
+                tie(self.grad_own),
+                joined,
+                self.grad_residual,
+                coarse,
+                norm1_gain.reshape(1, -1),
+                *self.terms,
+            )
+            tie.mark(self.grad_input)
+
+        def tokens_back(self):
+            in_pieces = from_micro(tie(self.grad_input))
+            tie.mark(*in_pieces)
+            self.got_input = back(in_pieces)
+
+        def tokens_end(self):
+            self.grad_input = in_micro_order(tie(*self.got_input)).astype(f32)
+            self.grad_coarse = jnp.sum(
+                self.grad_input.reshape(micro, -1, UP, model) * up_gain, axis=2
+            )
+            tie.mark(self.grad_input, self.grad_coarse)
+
+        def small(self):
+            by_slot = jnp.concatenate(
+                [self.grad_bq.reshape(-1, hc), self.grad_bv.reshape(-1, hc)], axis=1
+            )
+            by_head = jnp.concatenate(
+                [choose([by_slot[s] for s in range(head_size)], a ^ here) for a in range(head_size)]
+            )
+            self.total = jnp.concatenate(
+                [tie(self.grad_up), self.grad_g1, self.grad_s1]
+                + [v.reshape(1, -1) for v in (self.grad_bo, self.grad_g2, self.grad_s2)]
+                + [grad_b2, self.grad_b1.reshape(-1, model), by_head.reshape(-1, model)]
+            )
+            tie.mark(self.total)
+            self.small_stages = [("dp", m) for m in [1] + masks] + [("head", m) for m in head_masks]
+            self.small_got = None
+
+        def small_step(self):
+            if self.small_got is not None:
+                self.total = tie(self.total) + self.small_got
+                tie.mark(self.total)
+                self.small_got = None
+            if self.small_stages:
+                self.small_got = xor_swap(self.total, *self.small_stages.pop(0))
+
+        def small_end(self):
+            self.small_step()
+            while self.small_got is not None:
+                tie.pause()
+                self.small_step()
+
+        def layer(self):
+            self.layer_out = in_micro_order(tie(*self.got_out))
+            tie.mark(self.layer_out)
+
+        def wait_out(self):
+            tie.mark(*tie.last, *self.got_out)
+
+        def wait_two(self):
+            tie.mark(*tie.last, *[part.terms[-1][0] for part in self.sums_two])
+
+        def wait_one(self):
+            tie.mark(*tie.last, *[part.terms[-1][0] for part in self.sums_one])
+
+        def wait_att(self):
+            tie.mark(*tie.last, *[part.terms[-1][0] for part in self.sums_att])
+
+        def wait_far(self):
+            tie.mark(*tie.last, *[t[-1] for t in self.terms])
+
+        def pause(self):
+            tie.pause()
+
+        def flush(self):
+            tie.flush()
+
+    it = Steps()
+    for name in STEPS:
+        getattr(it, name)()
+    layer_out = it.layer_out
+    grad_input, grad_coarse, total = it.grad_input, it.grad_coarse, it.total
+    grad_wf, grad_wa = it.sum_f.finish(), it.sum_att.finish()
     grad_w2 = jnp.concatenate([grad_wf[c].T for c in range(HALVES)], axis=0)
     grad_w1 = jnp.concatenate([grad_wf[HALVES + c] for c in range(HALVES)], axis=1)
     grad_wqkv, grad_wo = grad_wa[:3], grad_wa[3].T

time: 620 us -> 606 us (0.977)
  local copies, waits for them, and re-layouts: 79.9 us -> 60.1 us
    unnamed x261 -> x249, local copies, waits for them, and re-layouts: 27.8 us -> 16.4 us
    ppermute x48 -> x50, starting transfers between devices: 42.6 us -> 53.3 us  [xor_swap(): return lax.ppermute(value, axis, [(i, i ^ mask) for i in range(size)])]
    ppermute x48 -> x50, waiting for transfers between devices: 159 us -> 167 us  [xor_swap(): return lax.ppermute(value, axis, [(i, i ^ mask) for i in range(size)])]
    concatenate x10 -> x8, local copies, waits for them, and re-layouts: 9.95 us -> 2.25 us  [widen(): wider = [jnp.concatenate([a, b], axis=0) for a, b in zip(tie(*held), got)]]
    ppermute x12, starting transfers between devices: 23.7 us -> 16 us  [send(): lax.ppermute(value, 'head', pairs)]
    slice x3 -> x2, local copies, waits for them, and re-layouts: 6.75 us -> 0.14 us  [colors_of(): v[c * rows_half:(c + 1) * rows_half]]
  transfers between devices with their start and end apart: 60 -> 62, of which waited for: 27 -> 23; matrix products, arithmetic and copies ran while one was open for 27% -> 25% of each run, Pallas kernels for 19% -> 18%
where the time goes in v4:
time: 606 us; the launch traced here: 596 us
  waiting for transfers between devices  204 us (34%)
  Pallas kernels  153 us (25%)
  other arithmetic  79.6 us (13%)
  starting transfers between devices  69.3 us (11%)
  local copies, waits for them, and re-layouts  60.1 us (10%)
  matrix products  26 us (4%)
    ppermute x50, waiting for transfers between devices, xor_swap(): return lax.ppermute(value, axis, [(i, i ^ mask) for i in range(size)])  167 us
    pallas_call x2, Pallas kernels, feed_call(): pl.pallas_call(functools.partial(kernel, masks, n_own, n), grid_spec=pltp...  73.9 us
    ppermute x50, starting transfers between devices, xor_swap(): return lax.ppermute(value, axis, [(i, i ^ mask) for i in range(size)])  53.3 us
    ppermute x12, waiting for transfers between devices, send(): lax.ppermute(value, 'head', pairs)  37.1 us
    convert_element_type x18, other arithmetic, upto(): total = total.astype(bf16)  33.9 us
    pallas_call x1, Pallas kernels, attention_backward(): pl.pallas_call(functools.partial(attention_backward_kernel, width // PAIR...  21.5 us
    pallas_call x1, Pallas kernels, attention_weights(): pl.pallas_call(functools.partial(attention_weights_kernel, masks, heads),...  17.8 us
    unnamed x249, local copies, waits for them, and re-layouts  16.4 us
  transfers between devices with their start and end apart: 62, of which 23 were waited for; matrix products, arithmetic and copies ran while one was open for 25% of the time, Pallas kernels for 18%

profile of v4, /device:TPU:0, one launch (start us, length us, event | category | flops | bytes accessed | tf_op | source)
XLA Modules:
  0.0 595.8 jit_solution(15574713025559808006)
XLA Ops:
  52.5 15.0 %collective-permute-done.8 = bf16[2,3,64,1024]{3,2,1,0:T(8,128)(2,1)S(1)} collective-permute-done((bf16[2,3,64,1024]{3,2,1,0:T(8,128)(2,1)S(1)}, bf16[2,3,64,1024]{3,2,1,0:T(8,128)(2,1)S(1)}, u32[]{:S(2)}, u32[]{:S(2)}) %collective-permute-start.8) | collective-permute-done | bytes 786464 | tf_op jit(solution)/shard_map/ppermute | solution.py:28
  68.9 8.9 %collective-permute-done.3.refs_2_ = bf16[240,1024]{1,0:T(8,128)(2,1)S(1)} collective-permute-done((bf16[240,1024]{1,0:T(8,128)(2,1)S(1)}, bf16[240,1024]{1,0:T(8,128)(2,1)S(1)}, u32[]{:S(2)}, u32[]{:S(2)}) %collective-permute-start.3) | collective-permute-done | bytes 491552 | tf_op jit(solution)/shard_map/ppermute | solution.py:740
  83.4 9.9 %collective-permute-start.11 = (bf16[1,128,2048]{2,1,0:T(8,128)(2,1)S(1)}, bf16[1,128,2048]{2,1,0:T(8,128)(2,1)S(1)}, u32[]{:S(2)}, u32[]{:S(2)}) collective-permute-start(bf16[1,128,2048]{2,1,0:T(8,128)(2,1)S(1)} %bitcast.261), channel_id=1, source_target_pairs={{0,2},{1,3},{2,0},{3,1},{4,6},{5,7},{6,4},{7,5},{8,10},{9,11},{10,... | collective-permute-start | bytes 1572872 | tf_op jit(solution)/shard_map/ppermute | solution.py:28
  93.5 7.6 %collective-permute-done.10 = bf16[6,128,512]{2,1,0:T(8,128)(2,1)S(1)} collective-permute-done((bf16[6,128,512]{2,1,0:T(8,128)(2,1)S(1)}, bf16[6,128,512]{2,1,0:T(8,128)(2,1)S(1)}, u32[]{:S(2)}, u32[]{:S(2)}) %collective-permute-start.10) | collective-permute-done | bytes 786464 | tf_op jit(solution)/shard_map/ppermute | solution.py:28
  103.1 13.6 %collective-permute-done.11 = bf16[1,128,2048]{2,1,0:T(8,128)(2,1)S(1)} collective-permute-done((bf16[1,128,2048]{2,1,0:T(8,128)(2,1)S(1)}, bf16[1,128,2048]{2,1,0:T(8,128)(2,1)S(1)}, u32[]{:S(2)}, u32[]{:S(2)}) %collective-permute-start.11) | collective-permute-done | bytes 524320 | tf_op jit(solution)/shard_map/ppermute | solution.py:28
  119.1 6.9 %add_convert_fusion.own_ref = bf16[768,3072]{1,0:T(8,128)(2,1)} fusion(bf16[768,1024]{1,0:T(8,128)(2,1)S(1)} %get-tuple-element.247, bf16[1024,3072]{1,0:T(8,128)(2,1)S(1)} %get-tuple-element.223, f32[3072]{0:T(1024)S(1)} %get-tuple-element.498), kind=kOutput, calls=%fused_computation | convolution fusion | flops 4836556800 | bytes 12595200 | tf_op jit(solution)/shard_map/dot_general | solution.py:78
  125.9 15.4 %collective-permute-done.12 = bf16[2,128,2048]{2,1,0:T(8,128)(2,1)S(1)} collective-permute-done((bf16[2,128,2048]{2,1,0:T(8,128)(2,1)S(1)}, bf16[2,128,2048]{2,1,0:T(8,128)(2,1)S(1)}, u32[]{:S(2)}, u32[]{:S(2)}) %collective-permute-start.12) | collective-permute-done | bytes 1048608 | tf_op jit(solution)/shard_map/ppermute | solution.py:28
  143.0 7.0 %shard_map.290 = (bf16[6,128,1024]{2,1,0:T(8,128)(2,1)}, bf16[6,128,1024]{2,1,0:T(8,128)(2,1)}) custom-call(s32[12]{0:T(128)} %get-tuple-element.398.where_a, s32[12]{0:T(128)} %get-tuple-element.394.where_b, bf16[12,128,512]{2,1,0:T(8,128)(2,1)} %copy-done.51, bf16[12,128,512]{2,1,0:T(8,128)(2,1)} %copy-done.91, bf16[12,128,512]{2,1,0:T(8,128)(2,1)} %copy-done.52, ...), custom_call_target="tpu_custom_call" | custom-call | flops 68719476736 | bytes 67108864 | tf_op jit(solution)/shard_map/pallas_call | solution.py:448
  155.0 13.3 %collective-permute-done.19 = bf16[1,3,64,2048]{3,2,1,0:T(8,128)(2,1)S(1)} collective-permute-done((bf16[1,3,64,2048]{3,2,1,0:T(8,128)(2,1)S(1)}, bf16[1,3,64,2048]{3,2,1,0:T(8,128)(2,1)S(1)}, u32[]{:S(2)}, u32[]{:S(2)}) %collective-permute-start.19) | collective-permute-done | bytes 786464 | tf_op jit(solution)/shard_map/ppermute | solution.py:28
  182.5 9.8 %shard_map.291.attended = bf16[768,1024]{1,0:T(8,128)(2,1)S(1)} custom-call(s32[6]{0:T(128)S(1)} %get-tuple-element.401.has_far, bf16[768,3072]{1,0:T(8,128)(2,1)S(1)} %bitcast.245, bf16[768,2048]{1,0:T(8,128)(2,1)S(1)} %add_convert_fusion.1.far_ref), custom_call_target="tpu_custom_call" | custom-call | flops 68719476736 | bytes 67108864 | tf_op jit(solution)/shard_map/pallas_call | solution.py:138
  192.6 7.8 %collective-permute-done.24 = bf16[192,1024]{1,0:T(8,128)(2,1)S(1)} collective-permute-done((bf16[192,1024]{1,0:T(8,128)(2,1)S(1)}, bf16[192,1024]{1,0:T(8,128)(2,1)S(1)}, u32[]{:S(2)}, u32[]{:S(2)}) %collective-permute-start.24) | collective-permute-done | bytes 393248 | tf_op jit(solution)/shard_map/ppermute | solution.py:740
  210.5 10.7 %collective-permute-done.23 = bf16[192,1024]{1,0:T(8,128)(2,1)} collective-permute-done((bf16[192,1024]{1,0:T(8,128)(2,1)}, bf16[192,1024]{1,0:T(8,128)(2,1)}, u32[]{:S(2)}, u32[]{:S(2)}) %collective-permute-start.23) | collective-permute-done | bytes 393248 | tf_op jit(solution)/shard_map/ppermute | solution.py:740
  230.0 39.3 %shard_map.292 = (bf16[768,4096]{1,0:T(8,128)(2,1)}, bf16[768,1024]{1,0:T(8,128)(2,1)}, bf16[8,512,512]{2,1,0:T(8,128)(2,1)}, bf16[8,512,512]{2,1,0:T(8,128)(2,1)}) custom-call(s32[2]{0:T(128)} %copy-done.12, bf16[2,3,64,2048]{3,2,1,0:T(8,128)(2,1)} %constant_dynamic-update-slice_fusion.17.refs_0_.refs_8_, ...), custom_call_target="tpu_custom_call" | custom-call | flops 68719476736 | bytes 67108864 | tf_op jit(solution)/shard_map/pallas_call | solution.py:400
  273.3 34.6 %shard_map.293 = (f32[1,4096]{1,0:T(1,128)}, f32[768,1024]{1,0:T(8,128)}, bf16[8,512,512]{2,1,0:T(8,128)(2,1)}, bf16[8,512,512]{2,1,0:T(8,128)(2,1)}) custom-call(s32[2]{0:T(128)} %copy-done.12, bf16[2,3,64,2048]{3,2,1,0:T(8,128)(2,1)} %constant_dynamic-update-slice_fusion.17.refs_0_.refs_8_, ...), custom_call_target="tpu_custom_call" | custom-call | flops 68719476736 | bytes 67108864 | tf_op jit(solution)/shard_map/pallas_call | solution.py:400
  324.4 21.5 %shard_map.294.grad_own.grad_far = bf16[2,768,3072]{2,1,0:T(8,128)(2,1)S(1)} custom-call(s32[6]{0:T(128)S(1)} %get-tuple-element.401.has_far, bf16[768,3072]{1,0:T(8,128)(2,1)S(1)} %bitcast.247, bf16[768,2048]{1,0:T(8,128)(2,1)S(1)} %copy-done.22, bf16[768,1024]{1,0:T(8,128)(2,1)S(1)} %convolution_convert_fusion.grad_ref), custom_call_target="tpu_custom_call" | custom-call | flops 68719476736 | bytes 67108864 | tf_op jit(solution)/shard_map/pallas_call | solution.py:182
  359.2 18.7 %collective-permute-done.36 = bf16[4,256,512]{2,1,0:T(8,128)(2,1)S(1)} collective-permute-done((bf16[4,256,512]{2,1,0:T(8,128)(2,1)S(1)}, bf16[4,256,512]{2,1,0:T(8,128)(2,1)S(1)}, u32[]{:S(2)}, u32[]{:S(2)}) %collective-permute-start.36) | collective-permute-done | bytes 1048608 | tf_op jit(solution)/shard_map/ppermute | solution.py:28
  390.2 10.5 %shard_map.295 = (bf16[12,128,512]{2,1,0:T(8,128)(2,1)S(1)}, bf16[12,128,512]{2,1,0:T(8,128)(2,1)}, bf16[12,128,512]{2,1,0:T(8,128)(2,1)S(1)}, bf16[12,128,512]{2,1,0:T(8,128)(2,1)}) custom-call(s32[12]{0:T(128)S(1)} %get-tuple-element.397.where_a, s32[12]{0:T(128)S(1)} %get-tuple-element.393.where_b, bf16[6,128,1024]{2,1,0:T(8,128)(2,1)} %bitcast.56.mine_ref, ...), custom_call_target="tpu_custom_call" | custom-call | flops 68719476736 | bytes 67108864 | tf_op jit(solution)/shard_map/pallas_call | solution.py:488
  403.2 17.8 %shard_map.296 = (bf16[16,512,256]{2,1,0:T(8,128)(2,1)S(1)}, bf16[16,512,256]{2,1,0:T(8,128)(2,1)}) custom-call(s32[2]{0:T(128)S(1)} %copy-done.13, bf16[1024,768]{1,0:T(8,128)(2,1)S(1)} %bitcast.233, bf16[1024,768]{1,0:T(8,128)(2,1)S(1)} %bitcast.232, bf16[1024,768]{1,0:T(8,128)(2,1)S(1)} %copy-done.6, bf16[2,768,3072]{2,1,0:T(8,128)(2,1)S(1)} %bitcast.231, ...), custom_call_target="tpu_custom_call" | custom-call | flops 68719476736 | bytes 67108864 | tf_op jit(solution)/shard_map/pallas_call | solution.py:658
  449.7 24.4 %collective-permute-done.52 = bf16[2,4,128,512]{3,2,1,0:T(8,128)(2,1)} collective-permute-done((bf16[2,4,128,512]{3,2,1,0:T(8,128)(2,1)}, bf16[2,4,128,512]{3,2,1,0:T(8,128)(2,1)}, u32[]{:S(2)}, u32[]{:S(2)}) %collective-permute-start.52) | collective-permute-done | bytes 1048608 | tf_op jit(solution)/shard_map/ppermute | solution.py:28
  483.5 11.1 %collective-permute-done.44.refs_2_ = bf16[6,128,512]{2,1,0:T(8,128)(2,1)S(1)} collective-permute-done((bf16[6,128,512]{2,1,0:T(8,128)(2,1)S(1)}, bf16[6,128,512]{2,1,0:T(8,128)(2,1)S(1)}, u32[]{:S(2)}, u32[]{:S(2)}) %collective-permute-start.44) | collective-permute-done | bytes 786464 | tf_op jit(solution)/shard_map/ppermute | solution.py:28
  495.9 9.3 %shard_map.297 = (bf16[768,1024]{1,0:T(8,128)(2,1)}, f32[4,1024]{1,0:T(4,128)}, f32[1,1024]{1,0:T(1,128)}, f32[1,1024]{1,0:T(1,128)}) custom-call(f32[768,1024]{1,0:T(8,128)} %fusion.own_ref, f32[768,1024]{1,0:T(8,128)} %copy-done.16, f32[768,1024]{1,0:T(8,128)} %get-tuple-element.392.res_ref, bf16[192,1024]{1,0:T(8,128)(2,1)} %copy-done.23, ...), custom_call_target="tpu_custom_call" | custom-call | flops 68719476736 | bytes 67108864 | tf_op jit(solution)/shard_map/pallas_call | solution.py:543
  505.3 9.0 %collective-permute-done.47 = bf16[8,256,256]{2,1,0:T(8,128)(2,1)} collective-permute-done((bf16[8,256,256]{2,1,0:T(8,128)(2,1)}, bf16[8,256,256]{2,1,0:T(8,128)(2,1)}, u32[]{:S(2)}, u32[]{:S(2)}) %collective-permute-start.47) | collective-permute-done | bytes 1048608 | tf_op jit(solution)/shard_map/ppermute | solution.py:28
  537.3 18.8 %collective-permute-done.54 = bf16[2,4,128,256]{3,2,1,0:T(8,128)(2,1)S(1)} collective-permute-done((bf16[2,4,128,256]{3,2,1,0:T(8,128)(2,1)S(1)}, bf16[2,4,128,256]{3,2,1,0:T(8,128)(2,1)S(1)}, u32[]{:S(2)}, u32[]{:S(2)}) %collective-permute-start.54) | collective-permute-done | bytes 524320 | tf_op jit(solution)/shard_map/ppermute | solution.py:28
  559.0 9.7 %collective-permute-done.48 = bf16[192,1024]{1,0:T(8,128)(2,1)S(1)} collective-permute-done((bf16[192,1024]{1,0:T(8,128)(2,1)S(1)}, bf16[192,1024]{1,0:T(8,128)(2,1)S(1)}, u32[]{:S(2)}, u32[]{:S(2)}) %collective-permute-start.48) | collective-permute-done | bytes 393248 | tf_op jit(solution)/shard_map/ppermute | solution.py:740
  (530 shorter events, 242.6 us)
Async XLA Ops:
  43.8 33.9 %collective-permute-start.3 = (bf16[240,1024]{1,0:T(8,128)(2,1)S(1)}, bf16[240,1024]{1,0:T(8,128)(2,1)S(1)}, u32[]{:S(2)}, u32[]{:S(2)}) collective-permute-start(bf16[240,1024]{1,0:T(8,128)(2,1)S(1)} %copy-done.49), channel_id=1, source_target_pairs={{0,2},{1,3},{2,0},{3,1},{4,6},{5,7},{6,4},{7,5},{8,10},{9,11},{10,... | collective-permute-start | bytes 1474568 | tf_op jit(solution)/shard_map/ppermute | solution.py:740
  82.9 34.6 %collective-permute-start.14 = (bf16[4,3,64,1024]{3,2,1,0:T(8,128)(2,1)S(1)}, bf16[4,3,64,1024]{3,2,1,0:T(8,128)(2,1)S(1)}, u32[]{:S(2)}, u32[]{:S(2)}) collective-permute-start(bf16[4,3,64,1024]{3,2,1,0:T(8,128)(2,1)S(1)} %constant_dynamic-update-slice_fusion.8.refs_1_), channel_id=1, source_target_pairs={{0,4},{4,0},{8,12},{12,8},{16,20},{20,16},{24,28},{28,24},{1,5},{5... | collective-permute-start | bytes 4718600 | tf_op jit(solution)/shard_map/ppermute | solution.py:28
  82.9 34.6 %collective-permute-start.13 = (bf16[4,3,64,1024]{3,2,1,0:T(8,128)(2,1)S(1)}, bf16[4,3,64,1024]{3,2,1,0:T(8,128)(2,1)S(1)}, u32[]{:S(2)}, u32[]{:S(2)}) collective-permute-start(bf16[4,3,64,1024]{3,2,1,0:T(8,128)(2,1)S(1)} %constant_dynamic-update-slice_fusion.6.refs_0_), channel_id=1, source_target_pairs={{0,4},{4,0},{8,12},{12,8},{16,20},{20,16},{24,28},{28,24},{1,5},{5... | collective-permute-start | bytes 4718600 | tf_op jit(solution)/shard_map/ppermute | solution.py:28
  83.4 33.2 %collective-permute-start.11 = (bf16[1,128,2048]{2,1,0:T(8,128)(2,1)S(1)}, bf16[1,128,2048]{2,1,0:T(8,128)(2,1)S(1)}, u32[]{:S(2)}, u32[]{:S(2)}) collective-permute-start(bf16[1,128,2048]{2,1,0:T(8,128)(2,1)S(1)} %bitcast.261), channel_id=1, source_target_pairs={{0,2},{1,3},{2,0},{3,1},{4,6},{5,7},{6,4},{7,5},{8,10},{9,11},{10,... | collective-permute-start | bytes 1572872 | tf_op jit(solution)/shard_map/ppermute | solution.py:28
  101.2 40.2 %collective-permute-start.16 = (bf16[12,128,512]{2,1,0:T(8,128)(2,1)S(1)}, bf16[12,128,512]{2,1,0:T(8,128)(2,1)S(1)}, u32[]{:S(2)}, u32[]{:S(2)}) collective-permute-start(bf16[12,128,512]{2,1,0:T(8,128)(2,1)S(1)} %constant_dynamic-update-slice_fusion.12.refs_2_.refs_6_), channel_id=1, source_target_pairs={{0,8},{4,12},{8,0},{12,4},{16,24},{20,28},{24,16},{28,20},{1,9},{5... | collective-permute-start | bytes 4718600 | tf_op jit(solution)/shard_map/ppermute | solution.py:28
  101.9 39.5 %collective-permute-start.15 = (bf16[12,128,512]{2,1,0:T(8,128)(2,1)S(1)}, bf16[12,128,512]{2,1,0:T(8,128)(2,1)S(1)}, u32[]{:S(2)}, u32[]{:S(2)}) collective-permute-start(bf16[12,128,512]{2,1,0:T(8,128)(2,1)S(1)} %constant_dynamic-update-slice_fusion.10.refs_0_.refs_4_), channel_id=1, source_target_pairs={{0,16},{4,20},{8,24},{12,28},{16,0},{20,4},{24,8},{28,12},{1,17},{... | collective-permute-start | bytes 4718600 | tf_op jit(solution)/shard_map/ppermute | solution.py:28
  169.2 54.7 %collective-permute-start.20 = (bf16[2,3,64,2048]{3,2,1,0:T(8,128)(2,1)}, bf16[2,3,64,2048]{3,2,1,0:T(8,128)(2,1)}, u32[]{:S(2)}, u32[]{:S(2)}) collective-permute-start(bf16[2,3,64,2048]{3,2,1,0:T(8,128)(2,1)} %constant_dynamic-update-slice_fusion.19.refs_2_.refs_10_), channel_id=1, source_target_pairs={{0,8},{4,12},{8,0},{12,4},{16,24},{20,28},{24,16},{28,20},{1,9},{5... | collective-permute-start | bytes 4718600 | tf_op jit(solution)/shard_map/ppermute | solution.py:28
  171.4 52.5 %collective-permute-start.18 = (bf16[2,3,64,2048]{3,2,1,0:T(8,128)(2,1)}, bf16[2,3,64,2048]{3,2,1,0:T(8,128)(2,1)}, u32[]{:S(2)}, u32[]{:S(2)}) collective-permute-start(bf16[2,3,64,2048]{3,2,1,0:T(8,128)(2,1)} %constant_dynamic-update-slice_fusion.17.refs_0_.refs_8_), channel_id=1, source_target_pairs={{0,16},{4,20},{8,24},{12,28},{16,0},{20,4},{24,8},{28,12},{1,17},{... | collective-permute-start | bytes 4718600 | tf_op jit(solution)/shard_map/ppermute | solution.py:28
  172.8 56.5 %collective-permute-start.27 = (bf16[2,3,64,2048]{3,2,1,0:T(8,128)(2,1)}, bf16[2,3,64,2048]{3,2,1,0:T(8,128)(2,1)}, u32[]{:S(2)}, u32[]{:S(2)}) collective-permute-start(bf16[2,3,64,2048]{3,2,1,0:T(8,128)(2,1)} %constant_dynamic-update-slice_fusion.19.refs_2_.refs_10_), channel_id=1, source_target_pairs={{0,4},{4,0},{8,12},{12,8},{16,20},{20,16},{24,28},{28,24},{1,5},{5... | collective-permute-start | bytes 4718600 | tf_op jit(solution)/shard_map/ppermute | solution.py:28
  192.3 37.0 %collective-permute-start.25 = (bf16[2,3,64,2048]{3,2,1,0:T(8,128)(2,1)}, bf16[2,3,64,2048]{3,2,1,0:T(8,128)(2,1)}, u32[]{:S(2)}, u32[]{:S(2)}) collective-permute-start(bf16[2,3,64,2048]{3,2,1,0:T(8,128)(2,1)} %constant_dynamic-update-slice_fusion.17.refs_0_.refs_8_), channel_id=1, source_target_pairs={{0,4},{4,0},{8,12},{12,8},{16,20},{20,16},{24,28},{28,24},{1,5},{5... | collective-permute-start | bytes 4718600 | tf_op jit(solution)/shard_map/ppermute | solution.py:28
  271.9 233.3 %collective-permute-start.29 = (bf16[192,1024]{1,0:T(8,128)(2,1)}, bf16[192,1024]{1,0:T(8,128)(2,1)}, u32[]{:S(2)}, u32[]{:S(2)}) collective-permute-start(bf16[192,1024]{1,0:T(8,128)(2,1)} %get-tuple-element.421), channel_id=1, source_target_pairs={{1,0},{2,1},{3,2},{0,3},{5,4},{6,5},{7,6},{4,7},{9,8},{10,9},{11,1... | collective-permute-start | bytes 1179656 | tf_op jit(solution)/shard_map/ppermute | solution.py:740
  273.3 37.7 %collective-permute-start.32 = (bf16[8,512,512]{2,1,0:T(8,128)(2,1)}, bf16[8,512,512]{2,1,0:T(8,128)(2,1)}, u32[]{:S(2)}, u32[]{:S(2)}) collective-permute-start(bf16[8,512,512]{2,1,0:T(8,128)(2,1)} %get-tuple-element.259), channel_id=1, source_target_pairs={{0,4},{4,0},{8,12},{12,8},{16,20},{20,16},{24,28},{28,24},{1,5},{5... | collective-permute-start | bytes 12582920 | tf_op jit(solution)/shard_map/ppermute | solution.py:28
  307.9 43.5 %collective-permute-start.35 = (bf16[8,512,512]{2,1,0:T(8,128)(2,1)}, bf16[8,512,512]{2,1,0:T(8,128)(2,1)}, u32[]{:S(2)}, u32[]{:S(2)}) collective-permute-start(bf16[8,512,512]{2,1,0:T(8,128)(2,1)} %get-tuple-element.267), channel_id=1, source_target_pairs={{0,4},{4,0},{8,12},{12,8},{16,20},{20,16},{24,28},{28,24},{1,5},{5... | collective-permute-start | bytes 12582920 | tf_op jit(solution)/shard_map/ppermute | solution.py:28
  313.0 33.0 %collective-permute-start.34 = (bf16[4,256,512]{2,1,0:T(8,128)(2,1)S(1)}, bf16[4,256,512]{2,1,0:T(8,128)(2,1)S(1)}, u32[]{:S(2)}, u32[]{:S(2)}) collective-permute-start(bf16[4,256,512]{2,1,0:T(8,128)(2,1)S(1)} %add_convert_fusion.9), channel_id=1, source_target_pairs={{0,8},{4,12},{8,0},{12,4},{16,24},{20,28},{24,16},{28,20},{1,9},{5... | collective-permute-start | bytes 3145736 | tf_op jit(solution)/shard_map/ppermute | solution.py:28
  387.3 33.7 %collective-permute-start.41 = (bf16[8,128,512]{2,1,0:T(8,128)(2,1)}, bf16[8,128,512]{2,1,0:T(8,128)(2,1)S(1)}, u32[]{:S(2)}, u32[]{:S(2)}) collective-permute-start(bf16[8,128,512]{2,1,0:T(8,128)(2,1)} %pad_maximum_fusion.4), channel_id=1, source_target_pairs={{0,16},{4,20},{8,24},{12,28},{16,0},{20,4},{24,8},{28,12},{1,17},{... | collective-permute-start | bytes 3145736 | tf_op jit(solution)/shard_map/ppermute | solution.py:28
  388.7 35.2 %collective-permute-start.42 = (bf16[8,128,512]{2,1,0:T(8,128)(2,1)}, bf16[8,128,512]{2,1,0:T(8,128)(2,1)S(1)}, u32[]{:S(2)}, u32[]{:S(2)}) collective-permute-start(bf16[8,128,512]{2,1,0:T(8,128)(2,1)} %pad_maximum_fusion.5), channel_id=1, source_target_pairs={{0,8},{4,12},{8,0},{12,4},{16,24},{20,28},{24,16},{28,20},{1,9},{5... | collective-permute-start | bytes 3145736 | tf_op jit(solution)/shard_map/ppermute | solution.py:28
  401.9 44.1 %collective-permute-start.43 = (bf16[12,128,512]{2,1,0:T(8,128)(2,1)}, bf16[12,128,512]{2,1,0:T(8,128)(2,1)}, u32[]{:S(2)}, u32[]{:S(2)}) collective-permute-start(bf16[12,128,512]{2,1,0:T(8,128)(2,1)} %get-tuple-element.292), channel_id=1, source_target_pairs={{0,8},{4,12},{8,0},{12,4},{16,24},{20,28},{24,16},{28,20},{1,9},{5... | collective-permute-start | bytes 4718600 | tf_op jit(solution)/shard_map/ppermute | solution.py:28
  402.4 45.2 %collective-permute-start.40 = (bf16[12,128,512]{2,1,0:T(8,128)(2,1)}, bf16[12,128,512]{2,1,0:T(8,128)(2,1)}, u32[]{:S(2)}, u32[]{:S(2)}) collective-permute-start(bf16[12,128,512]{2,1,0:T(8,128)(2,1)} %get-tuple-element.290), channel_id=1, source_target_pairs={{0,16},{4,20},{8,24},{12,28},{16,0},{20,4},{24,8},{28,12},{1,17},{... | collective-permute-start | bytes 4718600 | tf_op jit(solution)/shard_map/ppermute | solution.py:28
  421.0 56.8 %collective-permute-start.39 = (bf16[16,512,256]{2,1,0:T(8,128)(2,1)}, bf16[16,512,256]{2,1,0:T(8,128)(2,1)}, u32[]{:S(2)}, u32[]{:S(2)}) collective-permute-start(bf16[16,512,256]{2,1,0:T(8,128)(2,1)} %get-tuple-element.295), channel_id=1, source_target_pairs={{0,4},{4,0},{8,12},{12,8},{16,20},{20,16},{24,28},{28,24},{1,5},{5... | collective-permute-start | bytes 12582920 | tf_op jit(solution)/shard_map/ppermute | solution.py:28
  446.0 59.3 %collective-permute-start.30 = (bf16[192,1024]{1,0:T(8,128)(2,1)}, bf16[192,1024]{1,0:T(8,128)(2,1)}, u32[]{:S(2)}, u32[]{:S(2)}) collective-permute-start(bf16[192,1024]{1,0:T(8,128)(2,1)} %get-tuple-element.420), channel_id=1, source_target_pairs={{2,0},{3,1},{0,2},{1,3},{6,4},{7,5},{4,6},{5,7},{10,8},{11,9},{8,1... | collective-permute-start | bytes 1179656 | tf_op jit(solution)/shard_map/ppermute | solution.py:740
  447.6 35.2 %collective-permute-start.45 = (bf16[6,128,512]{2,1,0:T(8,128)(2,1)S(1)}, bf16[6,128,512]{2,1,0:T(8,128)(2,1)S(1)}, u32[]{:S(2)}, u32[]{:S(2)}) collective-permute-start(bf16[6,128,512]{2,1,0:T(8,128)(2,1)S(1)} %add_convert_fusion.10), channel_id=1, source_target_pairs={{0,16},{4,20},{8,24},{12,28},{16,0},{20,4},{24,8},{28,12},{1,17},{... | collective-permute-start | bytes 2359304 | tf_op jit(solution)/shard_map/ppermute | solution.py:28
  505.2 82.0 %collective-permute-start.61 = (bf16[1,4,128,512]{3,2,1,0:T(8,128)(2,1)}, bf16[1,4,128,512]{3,2,1,0:T(8,128)(2,1)}, u32[]{:S(2)}, u32[]{:S(2)}) collective-permute-start(bf16[1,4,128,512]{3,2,1,0:T(8,128)(2,1)} %slice.652), channel_id=1, source_target_pairs={{0,2},{1,3},{2,0},{3,1},{4,6},{5,7},{6,4},{7,5},{8,10},{9,11},{10,... | collective-permute-start | bytes 1572872 | tf_op jit(solution)/shard_map/ppermute | solution.py:28
  534.7 33.9 %collective-permute-start.48 = (bf16[192,1024]{1,0:T(8,128)(2,1)S(1)}, bf16[192,1024]{1,0:T(8,128)(2,1)S(1)}, u32[]{:S(2)}, u32[]{:S(2)}) collective-permute-start(bf16[192,1024]{1,0:T(8,128)(2,1)S(1)} %get-tuple-element.413), channel_id=1, source_target_pairs={{1,0},{2,1},{3,2},{0,3},{5,4},{6,5},{7,6},{4,7},{9,8},{10,9},{11,1... | collective-permute-start | bytes 1179656 | tf_op jit(solution)/shard_map/ppermute | solution.py:740
  534.7 33.9 %collective-permute-start.49 = (bf16[192,1024]{1,0:T(8,128)(2,1)S(1)}, bf16[192,1024]{1,0:T(8,128)(2,1)S(1)}, u32[]{:S(2)}, u32[]{:S(2)}) collective-permute-start(bf16[192,1024]{1,0:T(8,128)(2,1)S(1)} %get-tuple-element.412), channel_id=1, source_target_pairs={{2,0},{3,1},{0,2},{1,3},{6,4},{7,5},{4,6},{5,7},{10,8},{11,9},{8,1... | collective-permute-start | bytes 1179656 | tf_op jit(solution)/shard_map/ppermute | solution.py:740
  (146 other events, 1927.1 us)

commit v5 on v4

--- a/solution.py
+++ b/solution.py
@@ -13,7 +13,7 @@
 UP = 4
 HALVES = 2
 VMEM_LIMIT = 58 << 20
-STEPS = ["tokens_out", "feed", "two_first", "norm", "attention", "wait_two", "far_back", "one_first", "pause", "hidden_rest", "branch", "pause", "route", "weights", "hidden_head", "own", "pause", "far_rest", "att_first", "layer", "pause", "leave", "att_rest", "small", "tokens_back", "pause", "pause", "hidden_step", "att_head", "tokens_end", "pause", "att_step", "small_step", "small_end"]
+STEPS = ["tokens_out", "feed", "two_first", "one_first", "norm", "attention", "far_back", "hidden_rest", "branch", "pause", "route", "weights", "hidden_head", "own", "pause", "far_rest", "att_first", "layer", "pause", "leave", "att_rest", "tokens_back", "pause", "pause", "pause", "small", "hidden_step", "att_head", "tokens_end", "pause", "att_step", "small_step", "small_end"]
 PAIR = 2 * HEAD_DIM
 NEGATIVE = -1e30
 epsilon = 1e-05
@@ -89,10 +89,11 @@
 def pair_probs(q_pair, k_cat, allowed):
     low_half = lax.broadcasted_iota(jnp.int32, (BLOCK, PAIR), 1) < HEAD_DIM
     zero = jnp.zeros_like(q_pair)
+    q_pair = q_pair * jnp.asarray(1.0 / math.sqrt(HEAD_DIM), q_pair.dtype)
     q_stack = jnp.concatenate(
         [jnp.where(low_half, q_pair, zero), jnp.where(low_half, zero, q_pair)], axis=0
     )
-    scores = mm_nt(k_cat, q_stack) * (1.0 / math.sqrt(HEAD_DIM))
+    scores = mm_nt(k_cat, q_stack)
     scores = jnp.where(allowed, scores, NEGATIVE)
     top = jnp.max(scores, axis=0, keepdims=True)
     raised = jnp.exp(scores - top)
@@ -166,9 +167,10 @@
         grad_probs = mm_nt(v_cat, grad_stack)
         total = jnp.sum(probs * grad_probs, axis=0, keepdims=True)
         grad_scores = (probs * (grad_probs - total)).astype(bf16)
-        dq = mm_tn(grad_scores, k_cat) * scale
-        out_ref[0, :, columns[0]] = jnp.where(low_half, dq[:BLOCK], dq[BLOCK:]).astype(bf16)
-        dk = (mm(grad_scores, q_stack) * scale).astype(bf16)
+        dq = mm_tn(grad_scores, k_cat)
+        dq = jnp.where(low_half, dq[:BLOCK], dq[BLOCK:]) * scale
+        out_ref[0, :, columns[0]] = dq.astype(bf16)
+        dk = mm(grad_scores, q_stack).astype(bf16)
         dv = mm(probs.astype(bf16), grad_stack).astype(bf16)
         for half in range(2):
             rows = slice(half * BLOCK, (half + 1) * BLOCK)
@@ -260,12 +262,20 @@
         fill_chunk(masks, me, tables, out_ref)
 
 
-def by_parity(step, buffers, body):
+def by_stage(step, n, buffers, begin, body, end):
+    @pl.when(step == 0)
+    def _():
+        begin(buffers[0])
+
     for parity in range(2):
 
-        @pl.when(step % 2 == parity)
+        @pl.when((step % 2 == parity) & (step > 0) & (step < n))
         def _():
             body(buffers[1 - parity], buffers[parity])
+
+    @pl.when(step == n)
+    def _():
+        end(buffers[(n + 1) % 2])
 
 
 def scatter_rows(masks, color, me, value, held_ref):
@@ -299,29 +309,48 @@
     load_chunk(masks, me[0], jnp.minimum(step, n - 1), n_own, own_one, one_tables, w_one)
     load_chunk(masks, me[0], jnp.maximum(step - 1, 0), n_own, own_two, two_tables, w_two)
     ratio = ROOT_2_PI * 0.044715
-    rows = x_ref.shape[0] // 2
+    rows = x_ref.shape[0] // 3
+
+    parts = [slice(r * rows, (r + 1) * rows) for r in range(3)]
+
+    def finish(at, before):
+        h = before[at, :]
+        square = h * h
+        gate = 0.5 + 0.5 * jnp.tanh(h * (ROOT_2_PI + ratio * square))
+        act = (h * gate).astype(bf16)
+        act_ref[at, :] = act
+        slope_ref[at, :] = (
+            gate * (1.0 + 2.0 * h * (1.0 - gate) * (ROOT_2_PI + 3.0 * ratio * square))
+        ).astype(bf16)
+        return act
+
+    def start(at, now):
+        now[at, :] = mm(x_ref[at, :], w_one[...]) + bias_ref[...]
+
+    def gradient():
+        color = jnp.maximum(step - 1, 0) % n_own
+        scatter_rows(masks, color, me[0], mm(left_ref[...], act_ref[...]), held_ref)
+
+    def begin(now):
+        acc_ref[...] = jnp.zeros_like(acc_ref)
+        for at in parts:
+            start(at, now)
 
     def body(before, now):
-        for r in range(2):
-            at = slice(r * rows, (r + 1) * rows)
-            h = before[at, :]
-            square = h * h
-            gate = 0.5 + 0.5 * jnp.tanh(h * (ROOT_2_PI + ratio * square))
-            act = (h * gate).astype(bf16)
-            act_ref[at, :] = act
-            slope_ref[at, :] = (
-                gate * (1.0 + 2.0 * h * (1.0 - gate) * (ROOT_2_PI + 3.0 * ratio * square))
-            ).astype(bf16)
-            now[at, :] = mm(x_ref[at, :], w_one[...]) + bias_ref[...]
+        for at in parts:
+            act = finish(at, before)
+            start(at, now)
             acc_ref[at, :] += mm_nt(act, w_two[...])
-        scatter_rows(masks, jnp.maximum(step - 1, 0) % n_own, me[0], mm(left_ref[...], act_ref[...]), held_ref)
-
-    by_parity(step, (even_ref, odd_ref), body)
+        gradient()
+
+    def end(before):
+        for at in parts:
+            act = finish(at, before)
+            acc_ref[at, :] += mm_nt(act, w_two[...])
+        gradient()
+
+    by_stage(step, n, (even_ref, odd_ref), begin, body, end)
     split_rows(held_ref, keep_ref, send_ref)
-
-    @pl.when(step == 0)
-    def _():
-        acc_ref[...] = jnp.zeros_like(acc_ref)
 
     @pl.when(step == n)
     def _():
@@ -338,24 +367,39 @@
     load_chunk(masks, me[0], jnp.maximum(step - 1, 0), n_own, own_one, one_tables, w_one)
     rows = g_ref.shape[0] // 2
 
+    parts = [slice(r * rows, (r + 1) * rows) for r in range(2)]
+
+    def start(at, now):
+        now[at, :] = mm(g_ref[at, :], w_two[...])
+
+    def finish(at, before):
+        grad = (before[at, :] * slope_ref[at, :].astype(f32)).astype(bf16)
+        grad_ref[at, :] = grad
+        out_ref[at, :] += mm_nt(grad, w_one[...])
+        return jnp.sum(grad.astype(f32), axis=0, keepdims=True)
+
+    def gradient(sums):
+        bias_ref[...] = sums[0] + sums[1]
+        color = jnp.maximum(step - 1, 0) % n_own
+        scatter_rows(masks, color, me[0], mm(left_ref[...], grad_ref[...]), held_ref)
+
+    def begin(now):
+        out_ref[...] = jnp.zeros_like(out_ref)
+        for at in parts:
+            start(at, now)
+
     def body(before, now):
         sums = []
-        for r in range(2):
-            at = slice(r * rows, (r + 1) * rows)
-            grad = (before[at, :] * slope_ref[at, :].astype(f32)).astype(bf16)
-            grad_ref[at, :] = grad
-            sums.append(jnp.sum(grad.astype(f32), axis=0, keepdims=True))
-            now[at, :] = mm(g_ref[at, :], w_two[...])
-            out_ref[at, :] += mm_nt(grad, w_one[...])
-        bias_ref[...] = sums[0] + sums[1]
-        scatter_rows(masks, jnp.maximum(step - 1, 0) % n_own, me[0], mm(left_ref[...], grad_ref[...]), held_ref)
-
-    by_parity(step, (even_ref, odd_ref), body)
+        for at in parts:
+            start(at, now)
+            sums.append(finish(at, before))
+        gradient(sums)
+
+    def end(before):
+        gradient([finish(at, before) for at in parts])
+
+    by_stage(step, n, (even_ref, odd_ref), begin, body, end)
     split_rows(held_ref, keep_ref, send_ref)
-
-    @pl.when(step == 0)
-    def _():
-        out_ref[...] = jnp.zeros_like(out_ref)
 
 
 def feed_call(kernel, masks, me, tables, own_first, own_second, first_part, arrays, outs, scratch):

time: 606 us -> 574 us (0.947)
  waiting for transfers between devices: 204 us -> 177 us
    ppermute x50, waiting for transfers between devices: 167 us -> 134 us  [xor_swap(): return lax.ppermute(value, axis, [(i, i ^ mask) for i in range(size)])]
    unnamed x249 -> x227, local copies, waits for them, and re-layouts: 16.4 us -> 17.3 us
  transfers between devices with their start and end apart: 62 -> 62, of which waited for: 23 -> 24; matrix products, arithmetic and copies ran while one was open for 25% -> 26% of each run, Pallas kernels for 18% -> 18%
where the time goes in v5:
time: 574 us; the launch traced here: 564 us
  waiting for transfers between devices  177 us (31%)
  Pallas kernels  148 us (26%)
  other arithmetic  81.4 us (14%)
  starting transfers between devices  67.3 us (12%)
  local copies, waits for them, and re-layouts  62.3 us (11%)
  matrix products  25.5 us (4%)
    ppermute x50, waiting for transfers between devices, xor_swap(): return lax.ppermute(value, axis, [(i, i ^ mask) for i in range(size)])  134 us
    pallas_call x2, Pallas kernels, feed_call(): pl.pallas_call(functools.partial(kernel, masks, n_own, n), grid_spec=pltp...  68.2 us
    ppermute x50, starting transfers between devices, xor_swap(): return lax.ppermute(value, axis, [(i, i ^ mask) for i in range(size)])  50.4 us
    ppermute x12, waiting for transfers between devices, send(): lax.ppermute(value, 'head', pairs)  42.9 us
    convert_element_type x18, other arithmetic, upto(): total = total.astype(bf16)  33.2 us
    pallas_call x1, Pallas kernels, attention_backward(): pl.pallas_call(functools.partial(attention_backward_kernel, width // PAIR...  21.5 us
    pallas_call x1, Pallas kernels, attention_weights(): pl.pallas_call(functools.partial(attention_weights_kernel, masks, heads),...  17.8 us
    unnamed x227, local copies, waits for them, and re-layouts  17.3 us
  transfers between devices with their start and end apart: 62, of which 24 were waited for; matrix products, arithmetic and copies ran while one was open for 26% of the time, Pallas kernels for 18%

profile of v5, /device:TPU:0, one launch (start us, length us, event | category | flops | bytes accessed | tf_op | source)
XLA Modules:
  0.0 564.4 jit_solution(4676296113514065755)
XLA Ops:
  52.5 15.0 %collective-permute-done.8 = bf16[2,3,64,1024]{3,2,1,0:T(8,128)(2,1)S(1)} collective-permute-done((bf16[2,3,64,1024]{3,2,1,0:T(8,128)(2,1)S(1)}, bf16[2,3,64,1024]{3,2,1,0:T(8,128)(2,1)S(1)}, u32[]{:S(2)}, u32[]{:S(2)}) %collective-permute-start.8) | collective-permute-done | bytes 786464 | tf_op jit(solution)/shard_map/ppermute | solution.py:28
  68.9 8.9 %collective-permute-done.3.refs_2_ = bf16[240,1024]{1,0:T(8,128)(2,1)S(1)} collective-permute-done((bf16[240,1024]{1,0:T(8,128)(2,1)S(1)}, bf16[240,1024]{1,0:T(8,128)(2,1)S(1)}, u32[]{:S(2)}, u32[]{:S(2)}) %collective-permute-start.3) | collective-permute-done | bytes 491552 | tf_op jit(solution)/shard_map/ppermute | solution.py:784
  83.4 9.9 %collective-permute-start.11 = (bf16[1,128,2048]{2,1,0:T(8,128)(2,1)S(1)}, bf16[1,128,2048]{2,1,0:T(8,128)(2,1)S(1)}, u32[]{:S(2)}, u32[]{:S(2)}) collective-permute-start(bf16[1,128,2048]{2,1,0:T(8,128)(2,1)S(1)} %bitcast.261), channel_id=1, source_target_pairs={{0,2},{1,3},{2,0},{3,1},{4,6},{5,7},{6,4},{7,5},{8,10},{9,11},{10,... | collective-permute-start | bytes 1572872 | tf_op jit(solution)/shard_map/ppermute | solution.py:28
  93.5 7.6 %collective-permute-done.10 = bf16[6,128,512]{2,1,0:T(8,128)(2,1)S(1)} collective-permute-done((bf16[6,128,512]{2,1,0:T(8,128)(2,1)S(1)}, bf16[6,128,512]{2,1,0:T(8,128)(2,1)S(1)}, u32[]{:S(2)}, u32[]{:S(2)}) %collective-permute-start.10) | collective-permute-done | bytes 786464 | tf_op jit(solution)/shard_map/ppermute | solution.py:28
  103.1 13.6 %collective-permute-done.11 = bf16[1,128,2048]{2,1,0:T(8,128)(2,1)S(1)} collective-permute-done((bf16[1,128,2048]{2,1,0:T(8,128)(2,1)S(1)}, bf16[1,128,2048]{2,1,0:T(8,128)(2,1)S(1)}, u32[]{:S(2)}, u32[]{:S(2)}) %collective-permute-start.11) | collective-permute-done | bytes 524320 | tf_op jit(solution)/shard_map/ppermute | solution.py:28
  125.8 15.5 %collective-permute-done.12 = bf16[2,128,2048]{2,1,0:T(8,128)(2,1)S(1)} collective-permute-done((bf16[2,128,2048]{2,1,0:T(8,128)(2,1)S(1)}, bf16[2,128,2048]{2,1,0:T(8,128)(2,1)S(1)}, u32[]{:S(2)}, u32[]{:S(2)}) %collective-permute-start.12) | collective-permute-done | bytes 1048608 | tf_op jit(solution)/shard_map/ppermute | solution.py:28
  143.1 6.9 %shard_map.290 = (bf16[6,128,1024]{2,1,0:T(8,128)(2,1)}, bf16[6,128,1024]{2,1,0:T(8,128)(2,1)}) custom-call(s32[12]{0:T(128)} %get-tuple-element.396.where_a, s32[12]{0:T(128)} %get-tuple-element.392.where_b, bf16[12,128,512]{2,1,0:T(8,128)(2,1)} %copy-done.44, bf16[12,128,512]{2,1,0:T(8,128)(2,1)} %copy-done.81, bf16[12,128,512]{2,1,0:T(8,128)(2,1)} %copy-done.45, ...), custom_call_target="tpu_custom_call" | custom-call | flops 68719476736 | bytes 67108864 | tf_op jit(solution)/shard_map/pallas_call | solution.py:492
  155.2 13.0 %collective-permute-done.19 = bf16[1,3,64,2048]{3,2,1,0:T(8,128)(2,1)S(1)} collective-permute-done((bf16[1,3,64,2048]{3,2,1,0:T(8,128)(2,1)S(1)}, bf16[1,3,64,2048]{3,2,1,0:T(8,128)(2,1)S(1)}, u32[]{:S(2)}, u32[]{:S(2)}) %collective-permute-start.19) | collective-permute-done | bytes 786464 | tf_op jit(solution)/shard_map/ppermute | solution.py:28
  182.6 9.5 %shard_map.291.attended = bf16[768,1024]{1,0:T(8,128)(2,1)S(1)} custom-call(s32[6]{0:T(128)S(1)} %get-tuple-element.399.has_far, bf16[768,3072]{1,0:T(8,128)(2,1)S(1)} %bitcast.245, bf16[768,2048]{1,0:T(8,128)(2,1)S(1)} %add_convert_fusion.1.far_ref), custom_call_target="tpu_custom_call" | custom-call | flops 68719476736 | bytes 67108864 | tf_op jit(solution)/shard_map/pallas_call | solution.py:139
  192.4 8.1 %collective-permute-done.24 = bf16[192,1024]{1,0:T(8,128)(2,1)S(1)} collective-permute-done((bf16[192,1024]{1,0:T(8,128)(2,1)S(1)}, bf16[192,1024]{1,0:T(8,128)(2,1)S(1)}, u32[]{:S(2)}, u32[]{:S(2)}) %collective-permute-start.24) | collective-permute-done | bytes 393248 | tf_op jit(solution)/shard_map/ppermute | solution.py:784
  210.6 10.6 %collective-permute-done.23 = bf16[192,1024]{1,0:T(8,128)(2,1)} collective-permute-done((bf16[192,1024]{1,0:T(8,128)(2,1)}, bf16[192,1024]{1,0:T(8,128)(2,1)}, u32[]{:S(2)}, u32[]{:S(2)}) %collective-permute-start.23) | collective-permute-done | bytes 393248 | tf_op jit(solution)/shard_map/ppermute | solution.py:784
  230.0 36.0 %shard_map.292 = (bf16[768,4096]{1,0:T(8,128)(2,1)}, bf16[768,1024]{1,0:T(8,128)(2,1)}, bf16[8,512,512]{2,1,0:T(8,128)(2,1)}, bf16[8,512,512]{2,1,0:T(8,128)(2,1)}) custom-call(s32[2]{0:T(128)} %copy-done.13, bf16[2,3,64,2048]{3,2,1,0:T(8,128)(2,1)} %constant_dynamic-update-slice_fusion.17.refs_0_.refs_8_, ...), custom_call_target="tpu_custom_call" | custom-call | flops 68719476736 | bytes 67108864 | tf_op jit(solution)/shard_map/pallas_call | solution.py:444
  268.7 32.2 %shard_map.293 = (f32[1,4096]{1,0:T(1,128)}, f32[768,1024]{1,0:T(8,128)}, bf16[8,512,512]{2,1,0:T(8,128)(2,1)}, bf16[8,512,512]{2,1,0:T(8,128)(2,1)}) custom-call(s32[2]{0:T(128)} %copy-done.13, bf16[2,3,64,2048]{3,2,1,0:T(8,128)(2,1)} %constant_dynamic-update-slice_fusion.17.refs_0_.refs_8_, ...), custom_call_target="tpu_custom_call" | custom-call | flops 68719476736 | bytes 67108864 | tf_op jit(solution)/shard_map/pallas_call | solution.py:444
  326.0 21.5 %shard_map.294.grad_own.grad_far = bf16[2,768,3072]{2,1,0:T(8,128)(2,1)S(1)} custom-call(s32[6]{0:T(128)S(1)} %get-tuple-element.399.has_far, bf16[768,3072]{1,0:T(8,128)(2,1)S(1)} %bitcast.247, bf16[768,2048]{1,0:T(8,128)(2,1)S(1)} %copy-done.23, bf16[768,1024]{1,0:T(8,128)(2,1)S(1)} %convolution_convert_fusion.grad_ref), custom_call_target="tpu_custom_call" | custom-call | flops 68719476736 | bytes 67108864 | tf_op jit(solution)/shard_map/pallas_call | solution.py:184
  365.3 10.7 %shard_map.295 = (bf16[12,128,512]{2,1,0:T(8,128)(2,1)S(1)}, bf16[12,128,512]{2,1,0:T(8,128)(2,1)}, bf16[12,128,512]{2,1,0:T(8,128)(2,1)S(1)}, bf16[12,128,512]{2,1,0:T(8,128)(2,1)}) custom-call(s32[12]{0:T(128)S(1)} %get-tuple-element.395.where_a, s32[12]{0:T(128)S(1)} %get-tuple-element.391.where_b, bf16[6,128,1024]{2,1,0:T(8,128)(2,1)} %bitcast.56.mine_ref, ...), custom_call_target="tpu_custom_call" | custom-call | flops 68719476736 | bytes 67108864 | tf_op jit(solution)/shard_map/pallas_call | solution.py:532
  380.1 17.8 %shard_map.296 = (bf16[16,512,256]{2,1,0:T(8,128)(2,1)S(1)}, bf16[16,512,256]{2,1,0:T(8,128)(2,1)}) custom-call(s32[2]{0:T(128)S(1)} %copy-done.14, bf16[1024,768]{1,0:T(8,128)(2,1)S(1)} %bitcast.233, bf16[1024,768]{1,0:T(8,128)(2,1)S(1)} %bitcast.232, bf16[1024,768]{1,0:T(8,128)(2,1)S(1)} %copy-done.6, bf16[2,768,3072]{2,1,0:T(8,128)(2,1)S(1)} %bitcast.231, ...), custom_call_target="tpu_custom_call" | custom-call | flops 68719476736 | bytes 67108864 | tf_op jit(solution)/shard_map/pallas_call | solution.py:702
  410.1 6.8 %fusion.own_ref = f32[768,1024]{1,0:T(8,128)} fusion(bf16[1024,3072]{1,0:T(8,128)(2,1)S(1)} %bitcast.243, bf16[2,768,3072]{2,1,0:T(8,128)(2,1)S(1)} %bitcast.231), kind=kOutput, calls=%fused_computation.3 | convolution fusion | flops 4831838208 | bytes 14155776 | tf_op jit(solution)/shard_map/dot_general | solution.py:82
  434.4 18.1 %collective-permute-done.52 = bf16[2,4,128,512]{3,2,1,0:T(8,128)(2,1)} collective-permute-done((bf16[2,4,128,512]{3,2,1,0:T(8,128)(2,1)}, bf16[2,4,128,512]{3,2,1,0:T(8,128)(2,1)}, u32[]{:S(2)}, u32[]{:S(2)}) %collective-permute-start.52) | collective-permute-done | bytes 1048608 | tf_op jit(solution)/shard_map/ppermute | solution.py:28
  454.0 9.6 %shard_map.297 = (bf16[768,1024]{1,0:T(8,128)(2,1)}, f32[4,1024]{1,0:T(4,128)}, f32[1,1024]{1,0:T(1,128)}, f32[1,1024]{1,0:T(1,128)}) custom-call(f32[768,1024]{1,0:T(8,128)} %fusion.own_ref, f32[768,1024]{1,0:T(8,128)} %copy-done.17, f32[768,1024]{1,0:T(8,128)} %get-tuple-element.390.res_ref, bf16[192,1024]{1,0:T(8,128)(2,1)} %copy-done.24, ...), custom_call_target="tpu_custom_call" | custom-call | flops 68719476736 | bytes 67108864 | tf_op jit(solution)/shard_map/pallas_call | solution.py:587
  468.9 7.5 %collective-permute-done.47 = bf16[8,256,256]{2,1,0:T(8,128)(2,1)} collective-permute-done((bf16[8,256,256]{2,1,0:T(8,128)(2,1)}, bf16[8,256,256]{2,1,0:T(8,128)(2,1)}, u32[]{:S(2)}, u32[]{:S(2)}) %collective-permute-start.47) | collective-permute-done | bytes 1048608 | tf_op jit(solution)/shard_map/ppermute | solution.py:28
  481.9 7.3 %collective-permute-done.51 = bf16[8,128,256]{2,1,0:T(8,128)(2,1)S(1)} collective-permute-done((bf16[8,128,256]{2,1,0:T(8,128)(2,1)S(1)}, bf16[8,128,256]{2,1,0:T(8,128)(2,1)S(1)}, u32[]{:S(2)}, u32[]{:S(2)}) %collective-permute-start.51) | collective-permute-done | bytes 524320 | tf_op jit(solution)/shard_map/ppermute | solution.py:28
  497.6 18.6 %collective-permute-done.54 = bf16[2,4,128,256]{3,2,1,0:T(8,128)(2,1)S(1)} collective-permute-done((bf16[2,4,128,256]{3,2,1,0:T(8,128)(2,1)S(1)}, bf16[2,4,128,256]{3,2,1,0:T(8,128)(2,1)S(1)}, u32[]{:S(2)}, u32[]{:S(2)}) %collective-permute-start.54) | collective-permute-done | bytes 524320 | tf_op jit(solution)/shard_map/ppermute | solution.py:28
  522.9 9.9 %collective-permute-done.50 = bf16[192,1024]{1,0:T(8,128)(2,1)S(1)} collective-permute-done((bf16[192,1024]{1,0:T(8,128)(2,1)S(1)}, bf16[192,1024]{1,0:T(8,128)(2,1)S(1)}, u32[]{:S(2)}, u32[]{:S(2)}) %collective-permute-start.50) | collective-permute-done | bytes 393248 | tf_op jit(solution)/shard_map/ppermute | solution.py:784
  548.5 7.2 %collective-permute-done.59 = f32[16,1024]{1,0:T(8,128)S(1)} collective-permute-done((f32[16,1024]{1,0:T(8,128)S(1)}, f32[16,1024]{1,0:T(8,128)S(1)}, u32[]{:S(2)}, u32[]{:S(2)}) %collective-permute-start.59) | collective-permute-done | bytes 65568 | tf_op jit(solution)/shard_map/ppermute | solution.py:28
  (508 shorter events, 239.7 us)
Async XLA Ops:
  43.8 33.9 %collective-permute-start.3 = (bf16[240,1024]{1,0:T(8,128)(2,1)S(1)}, bf16[240,1024]{1,0:T(8,128)(2,1)S(1)}, u32[]{:S(2)}, u32[]{:S(2)}) collective-permute-start(bf16[240,1024]{1,0:T(8,128)(2,1)S(1)} %copy-done.42), channel_id=1, source_target_pairs={{0,2},{1,3},{2,0},{3,1},{4,6},{5,7},{6,4},{7,5},{8,10},{9,11},{10,... | collective-permute-start | bytes 1474568 | tf_op jit(solution)/shard_map/ppermute | solution.py:784
  82.9 34.6 %collective-permute-start.14 = (bf16[4,3,64,1024]{3,2,1,0:T(8,128)(2,1)S(1)}, bf16[4,3,64,1024]{3,2,1,0:T(8,128)(2,1)S(1)}, u32[]{:S(2)}, u32[]{:S(2)}) collective-permute-start(bf16[4,3,64,1024]{3,2,1,0:T(8,128)(2,1)S(1)} %constant_dynamic-update-slice_fusion.8.refs_1_), channel_id=1, source_target_pairs={{0,4},{4,0},{8,12},{12,8},{16,20},{20,16},{24,28},{28,24},{1,5},{5... | collective-permute-start | bytes 4718600 | tf_op jit(solution)/shard_map/ppermute | solution.py:28
  82.9 34.6 %collective-permute-start.13 = (bf16[4,3,64,1024]{3,2,1,0:T(8,128)(2,1)S(1)}, bf16[4,3,64,1024]{3,2,1,0:T(8,128)(2,1)S(1)}, u32[]{:S(2)}, u32[]{:S(2)}) collective-permute-start(bf16[4,3,64,1024]{3,2,1,0:T(8,128)(2,1)S(1)} %constant_dynamic-update-slice_fusion.6.refs_0_), channel_id=1, source_target_pairs={{0,4},{4,0},{8,12},{12,8},{16,20},{20,16},{24,28},{28,24},{1,5},{5... | collective-permute-start | bytes 4718600 | tf_op jit(solution)/shard_map/ppermute | solution.py:28
  83.4 33.2 %collective-permute-start.11 = (bf16[1,128,2048]{2,1,0:T(8,128)(2,1)S(1)}, bf16[1,128,2048]{2,1,0:T(8,128)(2,1)S(1)}, u32[]{:S(2)}, u32[]{:S(2)}) collective-permute-start(bf16[1,128,2048]{2,1,0:T(8,128)(2,1)S(1)} %bitcast.261), channel_id=1, source_target_pairs={{0,2},{1,3},{2,0},{3,1},{4,6},{5,7},{6,4},{7,5},{8,10},{9,11},{10,... | collective-permute-start | bytes 1572872 | tf_op jit(solution)/shard_map/ppermute | solution.py:28
  101.2 40.2 %collective-permute-start.16 = (bf16[12,128,512]{2,1,0:T(8,128)(2,1)S(1)}, bf16[12,128,512]{2,1,0:T(8,128)(2,1)S(1)}, u32[]{:S(2)}, u32[]{:S(2)}) collective-permute-start(bf16[12,128,512]{2,1,0:T(8,128)(2,1)S(1)} %constant_dynamic-update-slice_fusion.12.refs_2_.refs_6_), channel_id=1, source_target_pairs={{0,8},{4,12},{8,0},{12,4},{16,24},{20,28},{24,16},{28,20},{1,9},{5... | collective-permute-start | bytes 4718600 | tf_op jit(solution)/shard_map/ppermute | solution.py:28
  101.9 39.5 %collective-permute-start.15 = (bf16[12,128,512]{2,1,0:T(8,128)(2,1)S(1)}, bf16[12,128,512]{2,1,0:T(8,128)(2,1)S(1)}, u32[]{:S(2)}, u32[]{:S(2)}) collective-permute-start(bf16[12,128,512]{2,1,0:T(8,128)(2,1)S(1)} %constant_dynamic-update-slice_fusion.10.refs_0_.refs_4_), channel_id=1, source_target_pairs={{0,16},{4,20},{8,24},{12,28},{16,0},{20,4},{24,8},{28,12},{1,17},{... | collective-permute-start | bytes 4718600 | tf_op jit(solution)/shard_map/ppermute | solution.py:28
  169.1 54.8 %collective-permute-start.20 = (bf16[2,3,64,2048]{3,2,1,0:T(8,128)(2,1)}, bf16[2,3,64,2048]{3,2,1,0:T(8,128)(2,1)}, u32[]{:S(2)}, u32[]{:S(2)}) collective-permute-start(bf16[2,3,64,2048]{3,2,1,0:T(8,128)(2,1)} %constant_dynamic-update-slice_fusion.19.refs_2_.refs_10_), channel_id=1, source_target_pairs={{0,8},{4,12},{8,0},{12,4},{16,24},{20,28},{24,16},{28,20},{1,9},{5... | collective-permute-start | bytes 4718600 | tf_op jit(solution)/shard_map/ppermute | solution.py:28
  171.3 52.6 %collective-permute-start.18 = (bf16[2,3,64,2048]{3,2,1,0:T(8,128)(2,1)}, bf16[2,3,64,2048]{3,2,1,0:T(8,128)(2,1)}, u32[]{:S(2)}, u32[]{:S(2)}) collective-permute-start(bf16[2,3,64,2048]{3,2,1,0:T(8,128)(2,1)} %constant_dynamic-update-slice_fusion.17.refs_0_.refs_8_), channel_id=1, source_target_pairs={{0,16},{4,20},{8,24},{12,28},{16,0},{20,4},{24,8},{28,12},{1,17},{... | collective-permute-start | bytes 4718600 | tf_op jit(solution)/shard_map/ppermute | solution.py:28
  173.0 56.3 %collective-permute-start.27 = (bf16[2,3,64,2048]{3,2,1,0:T(8,128)(2,1)}, bf16[2,3,64,2048]{3,2,1,0:T(8,128)(2,1)}, u32[]{:S(2)}, u32[]{:S(2)}) collective-permute-start(bf16[2,3,64,2048]{3,2,1,0:T(8,128)(2,1)} %constant_dynamic-update-slice_fusion.19.refs_2_.refs_10_), channel_id=1, source_target_pairs={{0,4},{4,0},{8,12},{12,8},{16,20},{20,16},{24,28},{28,24},{1,5},{5... | collective-permute-start | bytes 4718600 | tf_op jit(solution)/shard_map/ppermute | solution.py:28
  192.3 37.1 %collective-permute-start.25 = (bf16[2,3,64,2048]{3,2,1,0:T(8,128)(2,1)}, bf16[2,3,64,2048]{3,2,1,0:T(8,128)(2,1)}, u32[]{:S(2)}, u32[]{:S(2)}) collective-permute-start(bf16[2,3,64,2048]{3,2,1,0:T(8,128)(2,1)} %constant_dynamic-update-slice_fusion.17.refs_0_.refs_8_), channel_id=1, source_target_pairs={{0,4},{4,0},{8,12},{12,8},{16,20},{20,16},{24,28},{28,24},{1,5},{5... | collective-permute-start | bytes 4718600 | tf_op jit(solution)/shard_map/ppermute | solution.py:28
  268.5 36.8 %collective-permute-start.33 = (bf16[8,512,512]{2,1,0:T(8,128)(2,1)}, bf16[8,512,512]{2,1,0:T(8,128)(2,1)}, u32[]{:S(2)}, u32[]{:S(2)}) collective-permute-start(bf16[8,512,512]{2,1,0:T(8,128)(2,1)} %get-tuple-element.260), channel_id=1, source_target_pairs={{0,4},{4,0},{8,12},{12,8},{16,20},{20,16},{24,28},{28,24},{1,5},{5... | collective-permute-start | bytes 12582920 | tf_op jit(solution)/shard_map/ppermute | solution.py:28
  301.3 166.8 %collective-permute-start.29 = (bf16[192,1024]{1,0:T(8,128)(2,1)}, bf16[192,1024]{1,0:T(8,128)(2,1)}, u32[]{:S(2)}, u32[]{:S(2)}) collective-permute-start(bf16[192,1024]{1,0:T(8,128)(2,1)} %get-tuple-element.419), channel_id=1, source_target_pairs={{1,0},{2,1},{3,2},{0,3},{5,4},{6,5},{7,6},{4,7},{9,8},{10,9},{11,1... | collective-permute-start | bytes 1179656 | tf_op jit(solution)/shard_map/ppermute | solution.py:784
  307.4 44.8 %collective-permute-start.35 = (bf16[4,256,512]{2,1,0:T(8,128)(2,1)S(1)}, bf16[4,256,512]{2,1,0:T(8,128)(2,1)}, u32[]{:S(2)}, u32[]{:S(2)}) collective-permute-start(bf16[4,256,512]{2,1,0:T(8,128)(2,1)S(1)} %add_convert_fusion.9), channel_id=1, source_target_pairs={{0,8},{4,12},{8,0},{12,4},{16,24},{20,28},{24,16},{28,20},{1,9},{5... | collective-permute-start | bytes 3145736 | tf_op jit(solution)/shard_map/ppermute | solution.py:28
  309.7 47.8 %collective-permute-start.34 = (bf16[4,256,512]{2,1,0:T(8,128)(2,1)S(1)}, bf16[4,256,512]{2,1,0:T(8,128)(2,1)}, u32[]{:S(2)}, u32[]{:S(2)}) collective-permute-start(bf16[4,256,512]{2,1,0:T(8,128)(2,1)S(1)} %add_convert_fusion.8), channel_id=1, source_target_pairs={{0,16},{4,20},{8,24},{12,28},{16,0},{20,4},{24,8},{28,12},{1,17},{... | collective-permute-start | bytes 3145736 | tf_op jit(solution)/shard_map/ppermute | solution.py:28
  312.9 42.1 %collective-permute-start.36 = (bf16[4,256,512]{2,1,0:T(8,128)(2,1)}, bf16[4,256,512]{2,1,0:T(8,128)(2,1)}, u32[]{:S(2)}, u32[]{:S(2)}) collective-permute-start(bf16[4,256,512]{2,1,0:T(8,128)(2,1)} %add_convert_fusion.7), channel_id=1, source_target_pairs={{0,8},{4,12},{8,0},{12,4},{16,24},{20,28},{24,16},{28,20},{1,9},{5... | collective-permute-start | bytes 3145736 | tf_op jit(solution)/shard_map/ppermute | solution.py:28
  316.2 42.9 %collective-permute-start.37 = (bf16[4,256,512]{2,1,0:T(8,128)(2,1)S(1)}, bf16[4,256,512]{2,1,0:T(8,128)(2,1)}, u32[]{:S(2)}, u32[]{:S(2)}) collective-permute-start(bf16[4,256,512]{2,1,0:T(8,128)(2,1)S(1)} %add_convert_fusion.6), channel_id=1, source_target_pairs={{0,16},{4,20},{8,24},{12,28},{16,0},{20,4},{24,8},{28,12},{1,17},{... | collective-permute-start | bytes 3145736 | tf_op jit(solution)/shard_map/ppermute | solution.py:28
  364.3 33.7 %collective-permute-start.41 = (bf16[8,128,512]{2,1,0:T(8,128)(2,1)}, bf16[8,128,512]{2,1,0:T(8,128)(2,1)S(1)}, u32[]{:S(2)}, u32[]{:S(2)}) collective-permute-start(bf16[8,128,512]{2,1,0:T(8,128)(2,1)} %pad_maximum_fusion.4), channel_id=1, source_target_pairs={{0,16},{4,20},{8,24},{12,28},{16,0},{20,4},{24,8},{28,12},{1,17},{... | collective-permute-start | bytes 3145736 | tf_op jit(solution)/shard_map/ppermute | solution.py:28
  364.9 35.9 %collective-permute-start.42 = (bf16[8,128,512]{2,1,0:T(8,128)(2,1)}, bf16[8,128,512]{2,1,0:T(8,128)(2,1)S(1)}, u32[]{:S(2)}, u32[]{:S(2)}) collective-permute-start(bf16[8,128,512]{2,1,0:T(8,128)(2,1)} %pad_maximum_fusion.5), channel_id=1, source_target_pairs={{0,8},{4,12},{8,0},{12,4},{16,24},{20,28},{24,16},{28,20},{1,9},{5... | collective-permute-start | bytes 3145736 | tf_op jit(solution)/shard_map/ppermute | solution.py:28
  377.1 45.9 %collective-permute-start.43 = (bf16[12,128,512]{2,1,0:T(8,128)(2,1)}, bf16[12,128,512]{2,1,0:T(8,128)(2,1)}, u32[]{:S(2)}, u32[]{:S(2)}) collective-permute-start(bf16[12,128,512]{2,1,0:T(8,128)(2,1)} %get-tuple-element.290), channel_id=1, source_target_pairs={{0,8},{4,12},{8,0},{12,4},{16,24},{20,28},{24,16},{28,20},{1,9},{5... | collective-permute-start | bytes 4718600 | tf_op jit(solution)/shard_map/ppermute | solution.py:28
  378.7 47.9 %collective-permute-start.40 = (bf16[12,128,512]{2,1,0:T(8,128)(2,1)}, bf16[12,128,512]{2,1,0:T(8,128)(2,1)}, u32[]{:S(2)}, u32[]{:S(2)}) collective-permute-start(bf16[12,128,512]{2,1,0:T(8,128)(2,1)} %get-tuple-element.288), channel_id=1, source_target_pairs={{0,16},{4,20},{8,24},{12,28},{16,0},{20,4},{24,8},{28,12},{1,17},{... | collective-permute-start | bytes 4718600 | tf_op jit(solution)/shard_map/ppermute | solution.py:28
  419.4 33.1 %collective-permute-start.52 = (bf16[2,4,128,512]{3,2,1,0:T(8,128)(2,1)}, bf16[2,4,128,512]{3,2,1,0:T(8,128)(2,1)}, u32[]{:S(2)}, u32[]{:S(2)}) collective-permute-start(bf16[2,4,128,512]{3,2,1,0:T(8,128)(2,1)} %pad_maximum_fusion.6), channel_id=1, source_target_pairs={{0,1},{1,0},{2,3},{3,2},{4,5},{5,4},{6,7},{7,6},{8,9},{9,8},{10,11... | collective-permute-start | bytes 3145736 | tf_op jit(solution)/shard_map/ppermute | solution.py:28
  428.7 39.4 %collective-permute-start.30 = (bf16[192,1024]{1,0:T(8,128)(2,1)}, bf16[192,1024]{1,0:T(8,128)(2,1)}, u32[]{:S(2)}, u32[]{:S(2)}) collective-permute-start(bf16[192,1024]{1,0:T(8,128)(2,1)} %get-tuple-element.418), channel_id=1, source_target_pairs={{2,0},{3,1},{0,2},{1,3},{6,4},{7,5},{4,6},{5,7},{10,8},{11,9},{8,1... | collective-permute-start | bytes 1179656 | tf_op jit(solution)/shard_map/ppermute | solution.py:784
  468.1 48.2 %collective-permute-start.55 = (f32[16,1024]{1,0:T(8,128)}, f32[16,1024]{1,0:T(8,128)S(1)}, u32[]{:S(2)}, u32[]{:S(2)}) collective-permute-start(f32[16,1024]{1,0:T(8,128)} %concatenate.126), channel_id=1, source_target_pairs={{0,4},{4,0},{8,12},{12,8},{16,20},{20,16},{24,28},{28,24},{1,5},{5... | collective-permute-start | bytes 196616 | tf_op jit(solution)/shard_map/ppermute | solution.py:28
  468.1 88.2 %collective-permute-start.61 = (bf16[1,4,128,512]{3,2,1,0:T(8,128)(2,1)}, bf16[1,4,128,512]{3,2,1,0:T(8,128)(2,1)}, u32[]{:S(2)}, u32[]{:S(2)}) collective-permute-start(bf16[1,4,128,512]{3,2,1,0:T(8,128)(2,1)} %slice.651), channel_id=1, source_target_pairs={{0,2},{1,3},{2,0},{3,1},{4,6},{5,7},{6,4},{7,5},{8,10},{9,11},{10,... | collective-permute-start | bytes 1572872 | tf_op jit(solution)/shard_map/ppermute | solution.py:28
  (135 other events, 1698.4 us)

commit v6 on v5

--- a/solution.py
+++ b/solution.py
@@ -979,7 +979,7 @@
     tie.pause()
     held_f = colors_of(gather_f.slots())
     got_f = swap_stage(held_f, 0)
-    got_cot = sent(cot_out, passed_got)
+    got_cot = sent(cot_out, *held_f)
     passed = passed_got
     for step in range(1, len(masks)):
         tie.pause()

time: 574 us -> 561 us (0.977)
  waiting for transfers between devices: 177 us -> 156 us
  starting transfers between devices: 67.3 us -> 76.8 us
    ppermute x12, waiting for transfers between devices: 42.9 us -> 24.8 us  [send(): lax.ppermute(value, 'head', pairs)]
    ppermute x12, starting transfers between devices: 16.8 us -> 23.5 us  [send(): lax.ppermute(value, 'head', pairs)]
  transfers between devices with their start and end apart: 62 -> 62, of which waited for: 24 -> 24; matrix products, arithmetic and copies ran while one was open for 26% -> 27% of each run, Pallas kernels for 18% -> 19%
where the time goes in v6:
time: 561 us; the launch traced here: 553 us
  waiting for transfers between devices  156 us (28%)
  Pallas kernels  148 us (26%)
  other arithmetic  81.4 us (15%)
  starting transfers between devices  76.8 us (14%)
  local copies, waits for them, and re-layouts  62.4 us (11%)
  matrix products  25.5 us (5%)
    ppermute x50, waiting for transfers between devices, xor_swap(): return lax.ppermute(value, axis, [(i, i ^ mask) for i in range(size)])  131 us
    pallas_call x2, Pallas kernels, feed_call(): pl.pallas_call(functools.partial(kernel, masks, n_own, n), grid_spec=pltp...  68.2 us
    ppermute x50, starting transfers between devices, xor_swap(): return lax.ppermute(value, axis, [(i, i ^ mask) for i in range(size)])  53.3 us
    convert_element_type x18, other arithmetic, upto(): total = total.astype(bf16)  33.2 us
    ppermute x12, waiting for transfers between devices, send(): lax.ppermute(value, 'head', pairs)  24.8 us
    ppermute x12, starting transfers between devices, send(): lax.ppermute(value, 'head', pairs)  23.5 us
    pallas_call x1, Pallas kernels, attention_backward(): pl.pallas_call(functools.partial(attention_backward_kernel, width // PAIR...  21.5 us
    pallas_call x1, Pallas kernels, attention_weights(): pl.pallas_call(functools.partial(attention_weights_kernel, masks, heads),...  17.8 us
  transfers between devices with their start and end apart: 62, of which 24 were waited for; matrix products, arithmetic and copies ran while one was open for 27% of the time, Pallas kernels for 19%

profile of v6, /device:TPU:0, one launch (start us, length us, event | category | flops | bytes accessed | tf_op | source)
XLA Modules:
  0.0 552.6 jit_solution(4772923210471102946)
XLA Ops:
  52.5 15.0 %collective-permute-done.8 = bf16[2,3,64,1024]{3,2,1,0:T(8,128)(2,1)S(1)} collective-permute-done((bf16[2,3,64,1024]{3,2,1,0:T(8,128)(2,1)S(1)}, bf16[2,3,64,1024]{3,2,1,0:T(8,128)(2,1)S(1)}, u32[]{:S(2)}, u32[]{:S(2)}) %collective-permute-start.8) | collective-permute-done | bytes 786464 | tf_op jit(solution)/shard_map/ppermute | solution.py:28
  68.9 8.9 %collective-permute-done.3.refs_2_ = bf16[240,1024]{1,0:T(8,128)(2,1)S(1)} collective-permute-done((bf16[240,1024]{1,0:T(8,128)(2,1)S(1)}, bf16[240,1024]{1,0:T(8,128)(2,1)S(1)}, u32[]{:S(2)}, u32[]{:S(2)}) %collective-permute-start.3) | collective-permute-done | bytes 491552 | tf_op jit(solution)/shard_map/ppermute | solution.py:784
  83.4 9.9 %collective-permute-start.11 = (bf16[1,128,2048]{2,1,0:T(8,128)(2,1)S(1)}, bf16[1,128,2048]{2,1,0:T(8,128)(2,1)S(1)}, u32[]{:S(2)}, u32[]{:S(2)}) collective-permute-start(bf16[1,128,2048]{2,1,0:T(8,128)(2,1)S(1)} %bitcast.261), channel_id=1, source_target_pairs={{0,2},{1,3},{2,0},{3,1},{4,6},{5,7},{6,4},{7,5},{8,10},{9,11},{10,... | collective-permute-start | bytes 1572872 | tf_op jit(solution)/shard_map/ppermute | solution.py:28
  93.5 7.6 %collective-permute-done.10 = bf16[6,128,512]{2,1,0:T(8,128)(2,1)S(1)} collective-permute-done((bf16[6,128,512]{2,1,0:T(8,128)(2,1)S(1)}, bf16[6,128,512]{2,1,0:T(8,128)(2,1)S(1)}, u32[]{:S(2)}, u32[]{:S(2)}) %collective-permute-start.10) | collective-permute-done | bytes 786464 | tf_op jit(solution)/shard_map/ppermute | solution.py:28
  103.1 13.6 %collective-permute-done.11 = bf16[1,128,2048]{2,1,0:T(8,128)(2,1)S(1)} collective-permute-done((bf16[1,128,2048]{2,1,0:T(8,128)(2,1)S(1)}, bf16[1,128,2048]{2,1,0:T(8,128)(2,1)S(1)}, u32[]{:S(2)}, u32[]{:S(2)}) %collective-permute-start.11) | collective-permute-done | bytes 524320 | tf_op jit(solution)/shard_map/ppermute | solution.py:28
  119.1 6.7 %add_convert_fusion.own_ref = bf16[768,3072]{1,0:T(8,128)(2,1)} fusion(bf16[768,1024]{1,0:T(8,128)(2,1)S(1)} %get-tuple-element.246, bf16[1024,3072]{1,0:T(8,128)(2,1)S(1)} %get-tuple-element.222, f32[3072]{0:T(1024)S(1)} %get-tuple-element.496), kind=kOutput, calls=%fused_computation | convolution fusion | flops 4836556800 | bytes 12595200 | tf_op jit(solution)/shard_map/dot_general | solution.py:78
  125.8 15.5 %collective-permute-done.12 = bf16[2,128,2048]{2,1,0:T(8,128)(2,1)S(1)} collective-permute-done((bf16[2,128,2048]{2,1,0:T(8,128)(2,1)S(1)}, bf16[2,128,2048]{2,1,0:T(8,128)(2,1)S(1)}, u32[]{:S(2)}, u32[]{:S(2)}) %collective-permute-start.12) | collective-permute-done | bytes 1048608 | tf_op jit(solution)/shard_map/ppermute | solution.py:28
  143.1 7.0 %shard_map.290 = (bf16[6,128,1024]{2,1,0:T(8,128)(2,1)}, bf16[6,128,1024]{2,1,0:T(8,128)(2,1)}) custom-call(s32[12]{0:T(128)} %get-tuple-element.396.where_a, s32[12]{0:T(128)} %get-tuple-element.392.where_b, bf16[12,128,512]{2,1,0:T(8,128)(2,1)} %copy-done.44, bf16[12,128,512]{2,1,0:T(8,128)(2,1)} %copy-done.81, bf16[12,128,512]{2,1,0:T(8,128)(2,1)} %copy-done.45, ...), custom_call_target="tpu_custom_call" | custom-call | flops 68719476736 | bytes 67108864 | tf_op jit(solution)/shard_map/pallas_call | solution.py:492
  153.1 5.4 collective-permute-start.21
  160.7 7.6 %collective-permute-done.19 = bf16[1,3,64,2048]{3,2,1,0:T(8,128)(2,1)S(1)} collective-permute-done((bf16[1,3,64,2048]{3,2,1,0:T(8,128)(2,1)S(1)}, bf16[1,3,64,2048]{3,2,1,0:T(8,128)(2,1)S(1)}, u32[]{:S(2)}, u32[]{:S(2)}) %collective-permute-start.19) | collective-permute-done | bytes 786464 | tf_op jit(solution)/shard_map/ppermute | solution.py:28
  181.4 9.5 %shard_map.291.attended = bf16[768,1024]{1,0:T(8,128)(2,1)S(1)} custom-call(s32[6]{0:T(128)S(1)} %get-tuple-element.399.has_far, bf16[768,3072]{1,0:T(8,128)(2,1)S(1)} %bitcast.245, bf16[768,2048]{1,0:T(8,128)(2,1)S(1)} %add_convert_fusion.1.far_ref), custom_call_target="tpu_custom_call" | custom-call | flops 68719476736 | bytes 67108864 | tf_op jit(solution)/shard_map/pallas_call | solution.py:139
  214.9 36.0 %shard_map.292 = (bf16[768,4096]{1,0:T(8,128)(2,1)}, bf16[768,1024]{1,0:T(8,128)(2,1)}, bf16[8,512,512]{2,1,0:T(8,128)(2,1)}, bf16[8,512,512]{2,1,0:T(8,128)(2,1)}) custom-call(s32[2]{0:T(128)} %copy-done.13, bf16[2,3,64,2048]{3,2,1,0:T(8,128)(2,1)} %constant_dynamic-update-slice_fusion.17.refs_0_.refs_8_, ...), custom_call_target="tpu_custom_call" | custom-call | flops 68719476736 | bytes 67108864 | tf_op jit(solution)/shard_map/pallas_call | solution.py:444
  253.6 32.2 %shard_map.293 = (f32[1,4096]{1,0:T(1,128)}, f32[768,1024]{1,0:T(8,128)}, bf16[8,512,512]{2,1,0:T(8,128)(2,1)}, bf16[8,512,512]{2,1,0:T(8,128)(2,1)}) custom-call(s32[2]{0:T(128)} %copy-done.13, bf16[2,3,64,2048]{3,2,1,0:T(8,128)(2,1)} %constant_dynamic-update-slice_fusion.17.refs_0_.refs_8_, ...), custom_call_target="tpu_custom_call" | custom-call | flops 68719476736 | bytes 67108864 | tf_op jit(solution)/shard_map/pallas_call | solution.py:444
  313.2 21.5 %shard_map.294.grad_own.grad_far = bf16[2,768,3072]{2,1,0:T(8,128)(2,1)S(1)} custom-call(s32[6]{0:T(128)S(1)} %get-tuple-element.399.has_far, bf16[768,3072]{1,0:T(8,128)(2,1)S(1)} %bitcast.247, bf16[768,2048]{1,0:T(8,128)(2,1)S(1)} %copy-done.23, bf16[768,1024]{1,0:T(8,128)(2,1)S(1)} %convolution_convert_fusion.grad_ref), custom_call_target="tpu_custom_call" | custom-call | flops 68719476736 | bytes 67108864 | tf_op jit(solution)/shard_map/pallas_call | solution.py:184
  352.8 10.6 %shard_map.295 = (bf16[12,128,512]{2,1,0:T(8,128)(2,1)S(1)}, bf16[12,128,512]{2,1,0:T(8,128)(2,1)}, bf16[12,128,512]{2,1,0:T(8,128)(2,1)S(1)}, bf16[12,128,512]{2,1,0:T(8,128)(2,1)}) custom-call(s32[12]{0:T(128)S(1)} %get-tuple-element.395.where_a, s32[12]{0:T(128)S(1)} %get-tuple-element.391.where_b, bf16[6,128,1024]{2,1,0:T(8,128)(2,1)} %bitcast.56.mine_ref, ...), custom_call_target="tpu_custom_call" | custom-call | flops 68719476736 | bytes 67108864 | tf_op jit(solution)/shard_map/pallas_call | solution.py:532
  367.0 17.8 %shard_map.296 = (bf16[16,512,256]{2,1,0:T(8,128)(2,1)S(1)}, bf16[16,512,256]{2,1,0:T(8,128)(2,1)}) custom-call(s32[2]{0:T(128)S(1)} %copy-done.14, bf16[1024,768]{1,0:T(8,128)(2,1)S(1)} %bitcast.233, bf16[1024,768]{1,0:T(8,128)(2,1)S(1)} %bitcast.232, bf16[1024,768]{1,0:T(8,128)(2,1)S(1)} %copy-done.6, bf16[2,768,3072]{2,1,0:T(8,128)(2,1)S(1)} %bitcast.231, ...), custom_call_target="tpu_custom_call" | custom-call | flops 68719476736 | bytes 67108864 | tf_op jit(solution)/shard_map/pallas_call | solution.py:702
  397.0 6.8 %fusion.own_ref = f32[768,1024]{1,0:T(8,128)} fusion(bf16[1024,3072]{1,0:T(8,128)(2,1)S(1)} %bitcast.243, bf16[2,768,3072]{2,1,0:T(8,128)(2,1)S(1)} %bitcast.231), kind=kOutput, calls=%fused_computation.3 | convolution fusion | flops 4831838208 | bytes 14155776 | tf_op jit(solution)/shard_map/dot_general | solution.py:82
  422.0 17.4 %collective-permute-done.52 = bf16[2,4,128,512]{3,2,1,0:T(8,128)(2,1)} collective-permute-done((bf16[2,4,128,512]{3,2,1,0:T(8,128)(2,1)}, bf16[2,4,128,512]{3,2,1,0:T(8,128)(2,1)}, u32[]{:S(2)}, u32[]{:S(2)}) %collective-permute-start.52) | collective-permute-done | bytes 1048608 | tf_op jit(solution)/shard_map/ppermute | solution.py:28
  441.7 9.6 %shard_map.297 = (bf16[768,1024]{1,0:T(8,128)(2,1)}, f32[4,1024]{1,0:T(4,128)}, f32[1,1024]{1,0:T(1,128)}, f32[1,1024]{1,0:T(1,128)}) custom-call(f32[768,1024]{1,0:T(8,128)} %fusion.own_ref, f32[768,1024]{1,0:T(8,128)} %copy-done.17, f32[768,1024]{1,0:T(8,128)} %get-tuple-element.390.res_ref, bf16[192,1024]{1,0:T(8,128)(2,1)} %copy-done.24, ...), custom_call_target="tpu_custom_call" | custom-call | flops 68719476736 | bytes 67108864 | tf_op jit(solution)/shard_map/pallas_call | solution.py:587
  456.7 6.5 %collective-permute-done.47 = bf16[8,256,256]{2,1,0:T(8,128)(2,1)} collective-permute-done((bf16[8,256,256]{2,1,0:T(8,128)(2,1)}, bf16[8,256,256]{2,1,0:T(8,128)(2,1)}, u32[]{:S(2)}, u32[]{:S(2)}) %collective-permute-start.47) | collective-permute-done | bytes 1048608 | tf_op jit(solution)/shard_map/ppermute | solution.py:28
  469.4 6.7 %collective-permute-done.51 = bf16[8,128,256]{2,1,0:T(8,128)(2,1)S(1)} collective-permute-done((bf16[8,128,256]{2,1,0:T(8,128)(2,1)S(1)}, bf16[8,128,256]{2,1,0:T(8,128)(2,1)S(1)}, u32[]{:S(2)}, u32[]{:S(2)}) %collective-permute-start.51) | collective-permute-done | bytes 524320 | tf_op jit(solution)/shard_map/ppermute | solution.py:28
  484.6 17.7 %collective-permute-done.54 = bf16[2,4,128,256]{3,2,1,0:T(8,128)(2,1)S(1)} collective-permute-done((bf16[2,4,128,256]{3,2,1,0:T(8,128)(2,1)S(1)}, bf16[2,4,128,256]{3,2,1,0:T(8,128)(2,1)S(1)}, u32[]{:S(2)}, u32[]{:S(2)}) %collective-permute-start.54) | collective-permute-done | bytes 524320 | tf_op jit(solution)/shard_map/ppermute | solution.py:28
  510.7 10.9 %collective-permute-done.50 = bf16[192,1024]{1,0:T(8,128)(2,1)S(1)} collective-permute-done((bf16[192,1024]{1,0:T(8,128)(2,1)S(1)}, bf16[192,1024]{1,0:T(8,128)(2,1)S(1)}, u32[]{:S(2)}, u32[]{:S(2)}) %collective-permute-start.50) | collective-permute-done | bytes 393248 | tf_op jit(solution)/shard_map/ppermute | solution.py:784
  543.1 6.5 %collective-permute-done.60 = bf16[1,4,128,256]{3,2,1,0:T(8,128)(2,1)} collective-permute-done((bf16[1,4,128,256]{3,2,1,0:T(8,128)(2,1)S(1)}, bf16[1,4,128,256]{3,2,1,0:T(8,128)(2,1)}, u32[]{:S(2)}, u32[]{:S(2)}) %collective-permute-start.60) | collective-permute-done | bytes 262176 | tf_op jit(solution)/shard_map/ppermute | solution.py:28
  (508 shorter events, 242.8 us)
Async XLA Ops:
  43.8 33.9 %collective-permute-start.3 = (bf16[240,1024]{1,0:T(8,128)(2,1)S(1)}, bf16[240,1024]{1,0:T(8,128)(2,1)S(1)}, u32[]{:S(2)}, u32[]{:S(2)}) collective-permute-start(bf16[240,1024]{1,0:T(8,128)(2,1)S(1)} %copy-done.42), channel_id=1, source_target_pairs={{0,2},{1,3},{2,0},{3,1},{4,6},{5,7},{6,4},{7,5},{8,10},{9,11},{10,... | collective-permute-start | bytes 1474568 | tf_op jit(solution)/shard_map/ppermute | solution.py:784
  82.9 34.6 %collective-permute-start.14 = (bf16[4,3,64,1024]{3,2,1,0:T(8,128)(2,1)S(1)}, bf16[4,3,64,1024]{3,2,1,0:T(8,128)(2,1)S(1)}, u32[]{:S(2)}, u32[]{:S(2)}) collective-permute-start(bf16[4,3,64,1024]{3,2,1,0:T(8,128)(2,1)S(1)} %constant_dynamic-update-slice_fusion.8.refs_1_), channel_id=1, source_target_pairs={{0,4},{4,0},{8,12},{12,8},{16,20},{20,16},{24,28},{28,24},{1,5},{5... | collective-permute-start | bytes 4718600 | tf_op jit(solution)/shard_map/ppermute | solution.py:28
  82.9 34.6 %collective-permute-start.13 = (bf16[4,3,64,1024]{3,2,1,0:T(8,128)(2,1)S(1)}, bf16[4,3,64,1024]{3,2,1,0:T(8,128)(2,1)S(1)}, u32[]{:S(2)}, u32[]{:S(2)}) collective-permute-start(bf16[4,3,64,1024]{3,2,1,0:T(8,128)(2,1)S(1)} %constant_dynamic-update-slice_fusion.6.refs_0_), channel_id=1, source_target_pairs={{0,4},{4,0},{8,12},{12,8},{16,20},{20,16},{24,28},{28,24},{1,5},{5... | collective-permute-start | bytes 4718600 | tf_op jit(solution)/shard_map/ppermute | solution.py:28
  83.4 33.2 %collective-permute-start.11 = (bf16[1,128,2048]{2,1,0:T(8,128)(2,1)S(1)}, bf16[1,128,2048]{2,1,0:T(8,128)(2,1)S(1)}, u32[]{:S(2)}, u32[]{:S(2)}) collective-permute-start(bf16[1,128,2048]{2,1,0:T(8,128)(2,1)S(1)} %bitcast.261), channel_id=1, source_target_pairs={{0,2},{1,3},{2,0},{3,1},{4,6},{5,7},{6,4},{7,5},{8,10},{9,11},{10,... | collective-permute-start | bytes 1572872 | tf_op jit(solution)/shard_map/ppermute | solution.py:28
  101.2 40.2 %collective-permute-start.16 = (bf16[12,128,512]{2,1,0:T(8,128)(2,1)S(1)}, bf16[12,128,512]{2,1,0:T(8,128)(2,1)S(1)}, u32[]{:S(2)}, u32[]{:S(2)}) collective-permute-start(bf16[12,128,512]{2,1,0:T(8,128)(2,1)S(1)} %constant_dynamic-update-slice_fusion.12.refs_2_.refs_6_), channel_id=1, source_target_pairs={{0,8},{4,12},{8,0},{12,4},{16,24},{20,28},{24,16},{28,20},{1,9},{5... | collective-permute-start | bytes 4718600 | tf_op jit(solution)/shard_map/ppermute | solution.py:28
  101.9 39.5 %collective-permute-start.15 = (bf16[12,128,512]{2,1,0:T(8,128)(2,1)S(1)}, bf16[12,128,512]{2,1,0:T(8,128)(2,1)S(1)}, u32[]{:S(2)}, u32[]{:S(2)}) collective-permute-start(bf16[12,128,512]{2,1,0:T(8,128)(2,1)S(1)} %constant_dynamic-update-slice_fusion.10.refs_0_.refs_4_), channel_id=1, source_target_pairs={{0,16},{4,20},{8,24},{12,28},{16,0},{20,4},{24,8},{28,12},{1,17},{... | collective-permute-start | bytes 4718600 | tf_op jit(solution)/shard_map/ppermute | solution.py:28
  153.1 37.7 %collective-permute-start.21 = (bf16[192,1024]{1,0:T(8,128)(2,1)S(1)}, bf16[192,1024]{1,0:T(8,128)(2,1)S(1)}, u32[]{:S(2)}, u32[]{:S(2)}) collective-permute-start(bf16[192,1024]{1,0:T(8,128)(2,1)S(1)} %copy-done.48), channel_id=1, source_target_pairs={{0,1},{1,2},{2,3},{3,0},{4,5},{5,6},{6,7},{7,4},{8,9},{9,10},{10,1... | collective-permute-start | bytes 1179656 | tf_op jit(solution)/shard_map/ppermute | solution.py:784
  168.3 32.6 %collective-permute-start.22 = (bf16[192,1024]{1,0:T(8,128)(2,1)}, bf16[192,1024]{1,0:T(8,128)(2,1)}, u32[]{:S(2)}, u32[]{:S(2)}) collective-permute-start(bf16[192,1024]{1,0:T(8,128)(2,1)} %get-tuple-element.235), channel_id=1, source_target_pairs={{0,2},{1,3},{2,0},{3,1},{4,6},{5,7},{6,4},{7,5},{8,10},{9,11},{10,... | collective-permute-start | bytes 1179656 | tf_op jit(solution)/shard_map/ppermute | solution.py:784
  174.0 33.6 %collective-permute-start.20 = (bf16[2,3,64,2048]{3,2,1,0:T(8,128)(2,1)}, bf16[2,3,64,2048]{3,2,1,0:T(8,128)(2,1)}, u32[]{:S(2)}, u32[]{:S(2)}) collective-permute-start(bf16[2,3,64,2048]{3,2,1,0:T(8,128)(2,1)} %constant_dynamic-update-slice_fusion.19.refs_2_.refs_10_), channel_id=1, source_target_pairs={{0,8},{4,12},{8,0},{12,4},{16,24},{20,28},{24,16},{28,20},{1,9},{5... | collective-permute-start | bytes 4718600 | tf_op jit(solution)/shard_map/ppermute | solution.py:28
  175.8 33.1 %collective-permute-start.18 = (bf16[2,3,64,2048]{3,2,1,0:T(8,128)(2,1)}, bf16[2,3,64,2048]{3,2,1,0:T(8,128)(2,1)}, u32[]{:S(2)}, u32[]{:S(2)}) collective-permute-start(bf16[2,3,64,2048]{3,2,1,0:T(8,128)(2,1)} %constant_dynamic-update-slice_fusion.17.refs_0_.refs_8_), channel_id=1, source_target_pairs={{0,16},{4,20},{8,24},{12,28},{16,0},{20,4},{24,8},{28,12},{1,17},{... | collective-permute-start | bytes 4718600 | tf_op jit(solution)/shard_map/ppermute | solution.py:28
  253.5 38.7 %collective-permute-start.33 = (bf16[8,512,512]{2,1,0:T(8,128)(2,1)}, bf16[8,512,512]{2,1,0:T(8,128)(2,1)}, u32[]{:S(2)}, u32[]{:S(2)}) collective-permute-start(bf16[8,512,512]{2,1,0:T(8,128)(2,1)} %get-tuple-element.260), channel_id=1, source_target_pairs={{0,4},{4,0},{8,12},{12,8},{16,20},{20,16},{24,28},{28,24},{1,5},{5... | collective-permute-start | bytes 12582920 | tf_op jit(solution)/shard_map/ppermute | solution.py:28
  286.3 169.7 %collective-permute-start.29 = (bf16[192,1024]{1,0:T(8,128)(2,1)}, bf16[192,1024]{1,0:T(8,128)(2,1)}, u32[]{:S(2)}, u32[]{:S(2)}) collective-permute-start(bf16[192,1024]{1,0:T(8,128)(2,1)} %get-tuple-element.419), channel_id=1, source_target_pairs={{1,0},{2,1},{3,2},{0,3},{5,4},{6,5},{7,6},{4,7},{9,8},{10,9},{11,1... | collective-permute-start | bytes 1179656 | tf_op jit(solution)/shard_map/ppermute | solution.py:784
  294.2 45.1 %collective-permute-start.35 = (bf16[4,256,512]{2,1,0:T(8,128)(2,1)S(1)}, bf16[4,256,512]{2,1,0:T(8,128)(2,1)}, u32[]{:S(2)}, u32[]{:S(2)}) collective-permute-start(bf16[4,256,512]{2,1,0:T(8,128)(2,1)S(1)} %add_convert_fusion.9), channel_id=1, source_target_pairs={{0,8},{4,12},{8,0},{12,4},{16,24},{20,28},{24,16},{28,20},{1,9},{5... | collective-permute-start | bytes 3145736 | tf_op jit(solution)/shard_map/ppermute | solution.py:28
  297.5 46.9 %collective-permute-start.34 = (bf16[4,256,512]{2,1,0:T(8,128)(2,1)S(1)}, bf16[4,256,512]{2,1,0:T(8,128)(2,1)}, u32[]{:S(2)}, u32[]{:S(2)}) collective-permute-start(bf16[4,256,512]{2,1,0:T(8,128)(2,1)S(1)} %add_convert_fusion.8), channel_id=1, source_target_pairs={{0,16},{4,20},{8,24},{12,28},{16,0},{20,4},{24,8},{28,12},{1,17},{... | collective-permute-start | bytes 3145736 | tf_op jit(solution)/shard_map/ppermute | solution.py:28
  300.5 41.4 %collective-permute-start.36 = (bf16[4,256,512]{2,1,0:T(8,128)(2,1)}, bf16[4,256,512]{2,1,0:T(8,128)(2,1)}, u32[]{:S(2)}, u32[]{:S(2)}) collective-permute-start(bf16[4,256,512]{2,1,0:T(8,128)(2,1)} %add_convert_fusion.7), channel_id=1, source_target_pairs={{0,8},{4,12},{8,0},{12,4},{16,24},{20,28},{24,16},{28,20},{1,9},{5... | collective-permute-start | bytes 3145736 | tf_op jit(solution)/shard_map/ppermute | solution.py:28
  303.2 42.8 %collective-permute-start.37 = (bf16[4,256,512]{2,1,0:T(8,128)(2,1)S(1)}, bf16[4,256,512]{2,1,0:T(8,128)(2,1)}, u32[]{:S(2)}, u32[]{:S(2)}) collective-permute-start(bf16[4,256,512]{2,1,0:T(8,128)(2,1)S(1)} %add_convert_fusion.6), channel_id=1, source_target_pairs={{0,16},{4,20},{8,24},{12,28},{16,0},{20,4},{24,8},{28,12},{1,17},{... | collective-permute-start | bytes 3145736 | tf_op jit(solution)/shard_map/ppermute | solution.py:28
  351.1 33.7 %collective-permute-start.41 = (bf16[8,128,512]{2,1,0:T(8,128)(2,1)}, bf16[8,128,512]{2,1,0:T(8,128)(2,1)S(1)}, u32[]{:S(2)}, u32[]{:S(2)}) collective-permute-start(bf16[8,128,512]{2,1,0:T(8,128)(2,1)} %pad_maximum_fusion.4), channel_id=1, source_target_pairs={{0,16},{4,20},{8,24},{12,28},{16,0},{20,4},{24,8},{28,12},{1,17},{... | collective-permute-start | bytes 3145736 | tf_op jit(solution)/shard_map/ppermute | solution.py:28
  351.9 35.8 %collective-permute-start.42 = (bf16[8,128,512]{2,1,0:T(8,128)(2,1)}, bf16[8,128,512]{2,1,0:T(8,128)(2,1)S(1)}, u32[]{:S(2)}, u32[]{:S(2)}) collective-permute-start(bf16[8,128,512]{2,1,0:T(8,128)(2,1)} %pad_maximum_fusion.5), channel_id=1, source_target_pairs={{0,8},{4,12},{8,0},{12,4},{16,24},{20,28},{24,16},{28,20},{1,9},{5... | collective-permute-start | bytes 3145736 | tf_op jit(solution)/shard_map/ppermute | solution.py:28
  364.5 45.4 %collective-permute-start.43 = (bf16[12,128,512]{2,1,0:T(8,128)(2,1)}, bf16[12,128,512]{2,1,0:T(8,128)(2,1)}, u32[]{:S(2)}, u32[]{:S(2)}) collective-permute-start(bf16[12,128,512]{2,1,0:T(8,128)(2,1)} %get-tuple-element.290), channel_id=1, source_target_pairs={{0,8},{4,12},{8,0},{12,4},{16,24},{20,28},{24,16},{28,20},{1,9},{5... | collective-permute-start | bytes 4718600 | tf_op jit(solution)/shard_map/ppermute | solution.py:28
  365.7 48.0 %collective-permute-start.40 = (bf16[12,128,512]{2,1,0:T(8,128)(2,1)}, bf16[12,128,512]{2,1,0:T(8,128)(2,1)}, u32[]{:S(2)}, u32[]{:S(2)}) collective-permute-start(bf16[12,128,512]{2,1,0:T(8,128)(2,1)} %get-tuple-element.288), channel_id=1, source_target_pairs={{0,16},{4,20},{8,24},{12,28},{16,0},{20,4},{24,8},{28,12},{1,17},{... | collective-permute-start | bytes 4718600 | tf_op jit(solution)/shard_map/ppermute | solution.py:28
  406.3 33.1 %collective-permute-start.52 = (bf16[2,4,128,512]{3,2,1,0:T(8,128)(2,1)}, bf16[2,4,128,512]{3,2,1,0:T(8,128)(2,1)}, u32[]{:S(2)}, u32[]{:S(2)}) collective-permute-start(bf16[2,4,128,512]{3,2,1,0:T(8,128)(2,1)} %pad_maximum_fusion.6), channel_id=1, source_target_pairs={{0,1},{1,0},{2,3},{3,2},{4,5},{5,4},{6,7},{7,6},{8,9},{9,8},{10,11... | collective-permute-start | bytes 3145736 | tf_op jit(solution)/shard_map/ppermute | solution.py:28
  416.3 39.7 %collective-permute-start.30 = (bf16[192,1024]{1,0:T(8,128)(2,1)}, bf16[192,1024]{1,0:T(8,128)(2,1)}, u32[]{:S(2)}, u32[]{:S(2)}) collective-permute-start(bf16[192,1024]{1,0:T(8,128)(2,1)} %get-tuple-element.418), channel_id=1, source_target_pairs={{2,0},{3,1},{0,2},{1,3},{6,4},{7,5},{4,6},{5,7},{10,8},{11,9},{8,1... | collective-permute-start | bytes 1179656 | tf_op jit(solution)/shard_map/ppermute | solution.py:784
  455.9 46.5 %collective-permute-start.55 = (f32[16,1024]{1,0:T(8,128)}, f32[16,1024]{1,0:T(8,128)S(1)}, u32[]{:S(2)}, u32[]{:S(2)}) collective-permute-start(f32[16,1024]{1,0:T(8,128)} %concatenate.126), channel_id=1, source_target_pairs={{0,4},{4,0},{8,12},{12,8},{16,20},{20,16},{24,28},{28,24},{1,5},{5... | collective-permute-start | bytes 196616 | tf_op jit(solution)/shard_map/ppermute | solution.py:28
  455.9 82.2 %collective-permute-start.61 = (bf16[1,4,128,512]{3,2,1,0:T(8,128)(2,1)}, bf16[1,4,128,512]{3,2,1,0:T(8,128)(2,1)}, u32[]{:S(2)}, u32[]{:S(2)}) collective-permute-start(bf16[1,4,128,512]{3,2,1,0:T(8,128)(2,1)} %slice.651), channel_id=1, source_target_pairs={{0,2},{1,3},{2,0},{3,1},{4,6},{5,7},{6,4},{7,5},{8,10},{9,11},{10,... | collective-permute-start | bytes 1572872 | tf_op jit(solution)/shard_map/ppermute | solution.py:28
  (135 other events, 1697.0 us)
